TPU v7x, 512 devices: a whole 4x8x8 slice. The times are simulated.
512 devices in a mesh: event: 64 (over z, x, core), wrow: 8 (over y).
Axes of the slice: x: 4, y: 8, z: 8, core: 2. Of those that a mesh axis runs over, the one named last changes fastest.
Arguments:
- mc_mass: float32 [196608], P('event'), may hold values from 0.5 to 4
- mc_basis: bfloat16 [64, 196608], P(None, 'event'), may hold values from -4 to 4
- data_mass: float32 [262144], P('event'), may hold values from 0.5 to 4
- data_basis: bfloat16 [64, 262144], P(None, 'event'), may hold values from -4 to 4
- data_weight: float32 [262144], P('event'), may hold values from 0.2 to 7.2, as said below
- res_mass: float32 [1024], P('wrow'), may hold values from 0.8 to 1.9
- res_width: float32 [1024], P('wrow'), may hold values from 0.05 to 0.5
- res_wave: int32 [1024], P('wrow'), may hold values from 0 to 511, as said below
- wave_q: int32 [512], P('wrow'), may hold values from 0 to 63
- couplings: float32 [2, 512], P(None, 'wrow'), may hold values from -0.25 to 0.25
Outputs:
- coupling_out: float32 [2, 512], P(None, 'wrow')
- intensity: float32 [262144], P('event')
Inputs may be any that keep to these rules, and one draw needn't show every extreme that they name: Resonance r belongs to a wave of block r // 128: res_wave[r] // 64 == r // 128; every wave has exactly 2 resonances. `data_weight`: positive event weights.
All inputs are finite; a program needn't handle non-finite values.
Results may differ from a plain program's by a relative error of at most 0.0024.
Values may be sent and summed in bfloat16 or wider, within the bound.
No kernel may reach another device: no remote copies, remote signals or barrier semaphores. Data moves between devices by JAX's collectives and lax.ppermute only.
A program may use at most 64 MiB of HBM per device.

v0:
```python
import jax
import jax.numpy as jnp
from jax import lax
from jax.sharding import PartitionSpec as P

ITERS = 3


BACKGROUND = 0.5


def wave_amplitudes(mass_sq, angular_basis, res_mass, res_width, local_wave, wave_q):
    wave_count = wave_q.shape[0]
    res_count = res_mass.shape[0]
    events = mass_sq.shape[0]
    per_wave = res_count // wave_count
    ordering = jnp.argsort(local_wave, stable=True)
    sorted_mass = res_mass[ordering]
    sorted_width = res_width[ordering]
    product = sorted_mass * sorted_width
    spacing = (sorted_mass * sorted_mass)[:, None] - mass_sq[None, :]
    denominator = spacing * spacing + (product * product)[:, None]
    real_part = product[:, None] * spacing / denominator
    imag_part = (product * product)[:, None] / denominator
    summed_real = real_part.reshape(wave_count, per_wave, events).sum(axis=1)
    summed_imag = imag_part.reshape(wave_count, per_wave, events).sum(axis=1)
    levels = jnp.arange(angular_basis.shape[0], dtype=jnp.int32)
    chooser = (wave_q[:, None] == levels[None, :]).astype(jnp.bfloat16)
    angular = jnp.dot(chooser, angular_basis, preferred_element_type=jnp.float32)
    return jnp.stack([angular * summed_real, angular * summed_imag]).astype(jnp.bfloat16)


def shards(
    mc_mass,
    mc_basis,
    data_mass,
    data_basis,
    data_weight,
    res_mass,
    res_width,
    res_wave,
    wave_q,
    couplings,
):
    highest = lax.Precision.HIGHEST
    wave_count = wave_q.shape[0]
    event_devices = lax.axis_size("event")
    local_wave = res_wave - lax.axis_index("wrow") * wave_count
    mc_amp = wave_amplitudes(mc_mass, mc_basis, res_mass, res_width, local_wave, wave_q)
    normalize = 1.0 / (mc_mass.shape[0] * event_devices)
    left_rows = mc_amp.reshape(2 * wave_count, mc_mass.shape[0])
    portion = lax.all_gather(mc_amp, "wrow", axis=1, tiled=True)
    width_here = portion.shape[1]
    right_rows = portion.reshape(2 * width_here, portion.shape[2])
    products = lax.dot_general(
        left_rows, right_rows, (((1,), (1,)), ((), ())), preferred_element_type=jnp.float32
    )
    tile_real = (
        products[:wave_count, :width_here] + products[wave_count:, width_here:]
    ) * normalize
    tile_imag = (
        products[:wave_count, width_here:] - products[wave_count:, :width_here]
    ) * normalize
    gram_part = jnp.stack([tile_real, tile_imag])
    gram = lax.psum(gram_part, "event")
    row_weight = jnp.sum(jnp.abs(gram[0]) + jnp.abs(gram[1]), axis=1)
    data_amp = wave_amplitudes(data_mass, data_basis, res_mass, res_width, local_wave, wave_q)
    stacked = data_amp.reshape(2 * wave_count, data_mass.shape[0])
    real_amp = data_amp[0].astype(jnp.float32)
    imag_amp = data_amp[1].astype(jnp.float32)
    squares = real_amp * real_amp + imag_amp * imag_amp
    inverse_count = 1.0 / (data_mass.shape[0] * event_devices)

    def field_total(coupling):
        kernel = jnp.stack(
            [
                jnp.concatenate([coupling[0], -coupling[1]]),
                jnp.concatenate([coupling[1], coupling[0]]),
            ]
        )
        partial_field = jnp.dot(
            kernel, stacked, preferred_element_type=jnp.float32, precision=highest
        )
        return lax.psum(partial_field, "wrow")

    coupling = couplings
    for iteration in range(ITERS):
        field_sum = field_total(coupling)
        whole_coupling = lax.all_gather(coupling, "wrow", axis=1, tiled=True)
        mixed_real = jnp.dot(gram[0], whole_coupling[0], precision=highest) - jnp.dot(
            gram[1], whole_coupling[1], precision=highest
        )
        mixed_imag = jnp.dot(gram[0], whole_coupling[1], precision=highest) + jnp.dot(
            gram[1], whole_coupling[0], precision=highest
        )
        power = field_sum[0] * field_sum[0] + field_sum[1] * field_sum[1]
        intensity = power + BACKGROUND
        weighting = data_weight / intensity
        carried = jnp.stack([field_sum[0] * weighting, field_sum[1] * weighting], axis=1)
        projected = jnp.dot(stacked, carried, preferred_element_type=jnp.float32, precision=highest)
        curvature = jnp.dot(
            squares, data_weight * power / (intensity * intensity), precision=highest
        )
        grad_real = -(projected[:wave_count, 0] + projected[wave_count:, 1]) * inverse_count
        grad_imag = -(projected[:wave_count, 1] - projected[wave_count:, 0]) * inverse_count
        total_grad, total_curve = lax.psum(
            (jnp.stack([grad_real, grad_imag]), curvature * inverse_count), "event"
        )
        total_grad = total_grad + jnp.stack([mixed_real, mixed_imag])
        total_curve = total_curve + row_weight
        coupling = coupling - total_grad / total_curve[None, :]
    field_sum = field_total(coupling)
    intensity = field_sum[0] * field_sum[0] + field_sum[1] * field_sum[1] + BACKGROUND
    return (coupling, intensity)


def solution(mesh):
    placed = (
        P("event"),
        P(None, "event"),
        P("event"),
        P(None, "event"),
        P("event"),
        P("wrow"),
        P("wrow"),
        P("wrow"),
        P("wrow"),
        P(None, "wrow"),
    )
    return jax.shard_map(
        shards, mesh=mesh, in_specs=placed, out_specs=(P(None, "wrow"), P("event")), check_vma=False
    )
```

profile of v0, /device:TPU:1, one launch (start us, length us, event | category | flops | bytes accessed | tf_op | source)
XLA Modules:
  0.0 665.5 jit_solution(12966085749098315449)
XLA Ops:
  7.3 0.7 broadcast_subtract_fusion
  8.0 2.5 sort.19
  10.5 1.6 gather_fusion
  12.1 1.6 gather_fusion.1
  14.2 1.5 fusion.6
  16.0 1.0 pad_maximum_fusion
  17.1 0.8 fusion.1
  18.9 25.0 %psum.77 = f32[2,4096]{1,0:T(2,128)S(1)} all-reduce(f32[2,4096]{1,0:T(2,128)S(1)} %fusion.64), channel_id=1, replica_groups=mesh['event'=64,'wrow'=8] {'wrow'}, use_global_device_ids=true, to_apply=%region_3.4 | all-reduce | flops 8192 | bytes 65536 | tf_op jit(solution)/shard_map/psum | solution.py:84
  44.0 1.0 fusion.14
  45.0 0.9 fusion.40
  45.9 53.5 %all-gather.5.cloned.1.call-done = bf16[2,512,3072]{2,1,0:T(8,128)(2,1)} async-done(((bf16[2,64,3072]{2,1,0:T(8,128)(2,1)}), bf16[2,512,3072]{2,1,0:T(8,128)(2,1)}) %all-gather.5.cloned.1.call-update) | async-done | bytes 6291472 | tf_op jit(solution)/shard_map/all_gather | solution.py:52
  99.4 5.0 fusion.95
  104.5 0.7 pad_maximum_fusion.1
  105.3 11.3 %all-gather = f32[8,64,2]{1,2,0:T(2,128)S(1)} all-gather(f32[1,64,2]{1,2,0:T(2,128)S(1)} %bitcast.289), channel_id=1, replica_groups=mesh['event'=64,'wrow'=8] {'wrow'}, dimensions={0}, use_global_device_ids=true | all-gather | bytes 4608 | tf_op jit(solution)/shard_map/all_gather | solution.py:89
  116.7 129.0 %all-reduce.2 = (f32[2,64]{1,0:T(2,128)S(1)}, f32[64]{0:T(128)S(1)}) all-reduce(f32[2,64]{1,0:T(2,128)S(1)} %pad_maximum_fusion.2, f32[64]{0:T(128)S(1)} %fusion.14), channel_id=1, replica_groups=mesh['event'=64,'wrow'=8] {'event'}, use_global_device_ids=true, to_apply=%region_4.5 | all-reduce | flops 192 | bytes 1536 | tf_op jit(solution)/shard_map/psum | solution.py:106
  245.6 48.2 %all-reduce.5.cloned.1.call-done = f32[2,64,512]{2,1,0:T(8,128)} async-done(((f32[2,64,512]{2,1,0:T(8,128)}), f32[2,64,512]{2,1,0:T(8,128)}) %all-reduce.5.cloned.1.call-update) | async-done | bytes 262160 | tf_op jit(solution)/shard_map/psum | solution.py:65
  293.9 1.1 add_reduce_fusion
  295.0 1.1 convolution_bitcast_fusion.13
  296.0 1.1 convolution_bitcast_fusion.11
  297.2 1.1 fusion.11
  298.3 1.2 fusion.13
  300.2 22.5 %psum.81 = f32[2,4096]{1,0:T(2,128)S(1)} all-reduce(f32[2,4096]{1,0:T(2,128)S(1)} %fusion.68), channel_id=1, replica_groups=mesh['event'=64,'wrow'=8] {'wrow'}, use_global_device_ids=true, to_apply=%region_10.11 | all-reduce | flops 8192 | bytes 65536 | tf_op jit(solution)/shard_map/psum | solution.py:84
  322.7 1.0 fusion.19
  323.8 0.9 fusion.44
  324.8 129.8 %all-reduce.1 = (f32[2,64]{1,0:T(2,128)S(1)}, f32[64]{0:T(128)S(1)}) all-reduce(f32[2,64]{1,0:T(2,128)S(1)} %pad_maximum_fusion.3, f32[64]{0:T(128)S(1)} %fusion.19), channel_id=1, replica_groups=mesh['event'=64,'wrow'=8] {'event'}, use_global_device_ids=true, to_apply=%region_11.12 | all-reduce | flops 192 | bytes 1536 | tf_op jit(solution)/shard_map/psum | solution.py:106
  454.6 9.8 %all-gather.1 = f32[8,64,2]{1,2,0:T(2,128)S(1)} all-gather(f32[1,64,2]{1,2,0:T(2,128)S(1)} %bitcast.285), channel_id=1, replica_groups=mesh['event'=64,'wrow'=8] {'wrow'}, dimensions={0}, use_global_device_ids=true | all-gather | bytes 4608 | tf_op jit(solution)/shard_map/all_gather | solution.py:89
  466.0 21.9 %psum.84 = f32[2,4096]{1,0:T(2,128)S(1)} all-reduce(f32[2,4096]{1,0:T(2,128)S(1)} %fusion.72), channel_id=1, replica_groups=mesh['event'=64,'wrow'=8] {'wrow'}, use_global_device_ids=true, to_apply=%region_13.14 | all-reduce | flops 8192 | bytes 65536 | tf_op jit(solution)/shard_map/psum | solution.py:84
  488.0 1.0 fusion.24
  489.0 0.9 fusion.48
  490.1 134.6 %all-reduce = (f32[2,64]{1,0:T(2,128)S(1)}, f32[64]{0:T(128)S(1)}) all-reduce(f32[2,64]{1,0:T(2,128)S(1)} %pad_maximum_fusion.4, f32[64]{0:T(128)S(1)} %fusion.24), channel_id=1, replica_groups=mesh['event'=64,'wrow'=8] {'event'}, use_global_device_ids=true, to_apply=%region_14.15 | all-reduce | flops 192 | bytes 1536 | tf_op jit(solution)/shard_map/psum | solution.py:106
  624.6 9.8 %all-gather.2 = f32[8,64,2]{1,2,0:T(2,128)S(1)} all-gather(f32[1,64,2]{1,2,0:T(2,128)S(1)} %bitcast.284), channel_id=1, replica_groups=mesh['event'=64,'wrow'=8] {'wrow'}, dimensions={0}, use_global_device_ids=true | all-gather | bytes 4608 | tf_op jit(solution)/shard_map/all_gather | solution.py:89
  636.1 21.9 %psum.87 = f32[2,4096]{1,0:T(2,128)S(1)} all-reduce(f32[2,4096]{1,0:T(2,128)S(1)} %fusion.76), channel_id=1, replica_groups=mesh['event'=64,'wrow'=8] {'wrow'}, use_global_device_ids=true, to_apply=%region_16.17 | all-reduce | flops 8192 | bytes 65536 | tf_op jit(solution)/shard_map/psum | solution.py:84
  (84 shorter events, 7.0 us)
Async XLA Ops:
  7.2 10.8 %copy-start = (bf16[64,4096]{1,0:T(8,128)(2,1)S(1)}, bf16[64,4096]{1,0:T(8,128)(2,1)}, u32[]{:S(2)}) copy-start(bf16[64,4096]{1,0:T(8,128)(2,1)} %param.13) | copy-start | bytes 1572868
  7.2 8.5 %copy-start.3 = (bf16[64,3072]{1,0:T(8,128)(2,1)S(1)}, bf16[64,3072]{1,0:T(8,128)(2,1)}, u32[]{:S(2)}) copy-start(bf16[64,3072]{1,0:T(8,128)(2,1)} %param.11) | copy-start | bytes 1179652
  7.2 8.5 %copy-start.8 = (s32[64]{0:T(128)S(1)}, s32[64]{0:T(128)}, u32[]{:S(2)}) copy-start(s32[64]{0:T(128)} %param.18) | copy-start | bytes 772
  7.2 92.2 %all-gather.5.cloned.1.call-start = ((), (), s32[]{:S(2)}) async-start(), calls=%async_computation | async-start | bytes 7077888 | tf_op jit(solution)/shard_map/all_gather | solution.py:52
  15.7 1.4 copy-start.6
  15.7 1.5 copy-start.5
  17.0 276.9 %all-reduce.5.cloned.1.call-start = ((), (), s32[]{:S(2)}) async-start(), calls=%async_computation.1 | async-start | bytes 524288 | tf_op jit(solution)/shard_map/psum | solution.py:65
  18.3 25.6 %copy-start.4 = (f32[4096]{0:T(1024)S(1)}, f32[4096]{0:T(1024)}, u32[]{:S(2)}) copy-start(f32[4096]{0:T(1024)} %param.14) | copy-start | bytes 49156
  18.4 81.0 %copy-start.2 = (bf16[2,64,3072]{2,1,0:T(8,128)(2,1)S(1)}, bf16[2,64,3072]{2,1,0:T(8,128)(2,1)}, u32[]{:S(2)}) copy-start(bf16[2,64,3072]{2,1,0:T(8,128)(2,1)} %pad_maximum_fusion) | copy-start | bytes 2359300
  298.3 166.2 %copy-start.1 = (f32[2,64,512]{2,1,0:T(8,128)S(1)}, f32[2,64,512]{2,1,0:T(8,128)}, u32[]{:S(2)}) copy-start(f32[2,64,512]{2,1,0:T(8,128)} %all-reduce.5.cloned.1.call-done) | copy-start | bytes 786436
  635.5 23.2 %copy-start.7 = (f32[2,64]{1,0:T(2,128)}, f32[2,64]{1,0:T(2,128)S(1)}, u32[]{:S(2)}) copy-start(f32[2,64]{1,0:T(2,128)S(1)} %divide_subtract_fusion) | copy-start | bytes 1540
Sparse Core Ops, SparseCore 0:
  17.1 82.2 all-gather.4
  105.3 188.4 all-reduce.4
where the time goes:
time: 673 us; the launch traced here: 665 us
  blocking collectives  516 us (77%)
  waiting for transfers between devices  102 us (15%)
  matrix products  19.8 us (3%)
  between operations  14.4 us (2%)
  other arithmetic  9.9 us (1%)
    psum x3, blocking collectives, shards(): lax.psum((jnp.stack([grad_real, grad_imag]), curvature * inverse_count),...  393 us
    psum x4, blocking collectives, field_total(): return lax.psum(partial_field, 'wrow')  91.3 us
    all_gather x1, waiting for transfers between devices, shards(): portion = lax.all_gather(mc_amp, 'wrow', axis=1, tiled=True)  53.5 us
    psum x1, waiting for transfers between devices, shards(): gram = lax.psum(gram_part, 'event')  48.2 us
    all_gather x3, blocking collectives, shards(): whole_coupling = lax.all_gather(coupling, 'wrow', axis=1, tiled=True)  31 us
  transfers between devices with their start and end apart: 2, of which 2 were waited for; matrix products, arithmetic and copies ran while one was open for 1% of the time, Pallas kernels for 0%

commit v1 on v0

v1 whole, which is shorter than its diff:
```python
import jax
import jax.numpy as jnp
from jax import lax
from jax.sharding import Mesh, PartitionSpec as P

ITERS = 3
BACKGROUND = 0.5
ZX = ("z", "x")
EVENT = ("z", "x", "core")
PEERS = ("core", "wrow")


def share(values, axes, count):
    spread = jnp.broadcast_to(values[None], (count,) + values.shape)
    return lax.all_to_all(spread, axes, 0, 0)


def split3(values):
    high = lax.reduce_precision(values, 8, 7)
    rest = values - high
    middle = lax.reduce_precision(rest, 8, 7)
    low = rest - middle
    return [part.astype(jnp.bfloat16) for part in (high, middle, low)]


def pair_parameters(res_mass, res_width, local_wave, wave_count):
    owner = local_wave[None, :] == jnp.arange(wave_count, dtype=jnp.int32)[:, None]
    index = jnp.arange(res_mass.shape[0], dtype=jnp.int32)[None, :]
    first_at = jnp.min(jnp.where(owner, index, res_mass.shape[0]), axis=1, keepdims=True)
    first = owner & (index == first_at)
    second = owner & (index != first_at)
    square = (res_mass * res_mass)[None, :]
    product = (res_mass * res_width)[None, :]
    zero = jnp.float32(0.0)
    return [
        jnp.sum(jnp.where(mask, value, zero), axis=1)
        for mask in (first, second)
        for value in (square, product)
    ]


def amplitudes(mass_sq, angular_basis, table):
    square_a, product_a, square_b, product_b, angular_index = (row[:, None] for row in table)
    levels = jnp.arange(angular_basis.shape[0], dtype=jnp.float32)[None, :]
    chooser = (angular_index == levels).astype(jnp.bfloat16)
    angular = jnp.dot(chooser, angular_basis, preferred_element_type=jnp.float32)
    gap_a = square_a - mass_sq[None, :]
    gap_b = square_b - mass_sq[None, :]
    power_a = product_a * product_a
    power_b = product_b * product_b
    den_a = gap_a * gap_a + power_a
    den_b = gap_b * gap_b + power_b
    scale = angular / (den_a * den_b)
    real = (product_a * gap_a * den_b + product_b * gap_b * den_a) * scale
    imag = (power_a * den_b + power_b * den_a) * scale
    return jnp.stack([real, imag]).astype(jnp.bfloat16)


def shards(
    mc_mass, mc_basis, data_mass, data_basis, data_weight, res_mass, res_width, res_wave, wave_q, couplings
):
    own = wave_q.shape[0]
    rows = lax.axis_size("wrow")
    waves = own * rows
    zx = lax.axis_size("z") * lax.axis_size("x")
    events = zx * lax.axis_size("core")
    row = lax.axis_index("wrow")
    place = lax.axis_index(EVENT)
    own_table = pair_parameters(res_mass, res_width, res_wave - row * own, own)
    own_table = own_table + [wave_q.astype(jnp.float32), couplings[0], couplings[1], jnp.zeros((own,), jnp.float32)]
    gathered = share(jnp.stack(own_table).reshape(-1, 128), ("wrow",), rows)
    table = gathered.reshape(rows, 8, own).transpose(1, 0, 2).reshape(8, waves)
    mc_amp = amplitudes(mc_mass, mc_basis, table[:5])
    mc_rows = lax.dynamic_slice_in_dim(mc_amp, row * own, own, 1).reshape(2 * own, -1)
    products = lax.dot_general(
        mc_rows, mc_amp.reshape(2 * waves, -1), (((1,), (1,)), ((), ())), preferred_element_type=jnp.float32
    )
    normalize = 1.0 / (mc_mass.shape[0] * events)
    tile_real = products[:own, :waves] + products[own:, waves:]
    tile_imag = products[:own, waves:] - products[own:, :waves]
    tile = jnp.concatenate([tile_real, tile_imag], axis=1) * normalize
    pieces = lax.all_to_all(tile.astype(jnp.bfloat16).reshape(own, 8, -1), EVENT, 0, 0)
    gram_row = jnp.sum(pieces.astype(jnp.float32), axis=0).reshape(2, waves)
    data_amp = amplitudes(data_mass, data_basis, table[:5])
    stacked = data_amp.reshape(2 * waves, -1)
    block = lax.dynamic_slice_in_dim(data_amp, row * own, own, 1).astype(jnp.float32)
    squares = block[0] * block[0] + block[1] * block[1]
    inverse_count = 1.0 / (data_mass.shape[0] * events)
    mine = (jnp.arange(own, dtype=jnp.int32) == place).astype(jnp.float32)

    def field_of(coupling):
        kernel = jnp.stack(
            [
                jnp.concatenate([coupling[0], -coupling[1]]),
                jnp.concatenate([coupling[1], coupling[0]]),
            ]
        )
        parts = jnp.dot(jnp.concatenate(split3(kernel)), stacked, preferred_element_type=jnp.float32)
        return (parts[4:6] + parts[2:4]) + parts[0:2]

    coupling = table[5:7]
    row_weight = None
    for iteration in range(ITERS):
        field = field_of(coupling)
        power = field[0] * field[0] + field[1] * field[1]
        intensity = power + BACKGROUND
        weighting = data_weight / intensity
        carried = field * weighting
        curving = weighting * power / intensity
        grad_real = -jnp.sum(block[0] * carried[0] + block[1] * carried[1], axis=1) * inverse_count
        grad_imag = -jnp.sum(block[0] * carried[1] - block[1] * carried[0], axis=1) * inverse_count
        curve = jnp.sum(squares * curving, axis=1) * inverse_count
        mixed_real = jnp.sum(gram_row[0] * coupling[0] - gram_row[1] * coupling[1])
        mixed_imag = jnp.sum(gram_row[0] * coupling[1] + gram_row[1] * coupling[0])
        terms = [grad_real + mine * mixed_real, grad_imag + mine * mixed_imag, curve]
        terms.append(mine * jnp.sum(jnp.abs(gram_row)) if row_weight is None else jnp.zeros_like(curve))
        nearby = jnp.sum(share(jnp.stack(terms).reshape(-1, 128), ZX, zx), axis=0)
        everyone = share(nearby, PEERS, 2 * rows)
        total = jnp.sum(everyone.reshape(2, rows, 4, own), axis=0).transpose(1, 0, 2).reshape(4, waves)
        if row_weight is None:
            row_weight = total[3]
        coupling = coupling - total[:2] / (total[2] + row_weight)[None, :]
    field = field_of(coupling)
    intensity = field[0] * field[0] + field[1] * field[1] + BACKGROUND
    return (lax.dynamic_slice_in_dim(coupling, row * own, own, 1), intensity)


def solution(mesh):
    chips = Mesh(mesh.devices.reshape(4, 8, 2, 8), ("z", "x", "core", "wrow"))
    placed = (
        P(EVENT),
        P(None, EVENT),
        P(EVENT),
        P(None, EVENT),
        P(EVENT),
        P("wrow"),
        P("wrow"),
        P("wrow"),
        P("wrow"),
        P(None, "wrow"),
    )
    return jax.shard_map(
        shards, mesh=chips, in_specs=placed, out_specs=(P(None, "wrow"), P(EVENT)), check_vma=False
    )
```

time: 673 us -> 168 us (0.25)
  blocking collectives: 516 us -> 63.7 us
  waiting for transfers between devices: 102 us -> 13.5 us
  starting transfers between devices: 0.08 us -> 28.2 us
  matrix products: 19.8 us -> 34 us
  between operations: 14.4 us -> 1.15 us
  other arithmetic: 9.9 us -> 21.7 us
    psum x7 -> x0, blocking collectives: 485 us -> none  [the longest x3 393 us: shards(): lax.psum((jnp.stack([grad_real, grad_imag]), curvature * inverse_count),...]
    all_to_all x0 -> x5, blocking collectives: none -> 63.7 us  [share(): return lax.all_to_all(spread, axes, 0, 0)]
    all_gather x1 -> x0, waiting for transfers between devices: 53.5 us -> none  [shards(): portion = lax.all_gather(mc_amp, 'wrow', axis=1, tiled=True)]
    psum x1 -> x0, waiting for transfers between devices: 48.2 us -> none  [shards(): gram = lax.psum(gram_part, 'event')]
    all_gather x3 -> x0, blocking collectives: 31 us -> none  [shards(): whole_coupling = lax.all_gather(coupling, 'wrow', axis=1, tiled=True)]
    all_to_all x0 -> x3, starting transfers between devices: none -> 28.2 us  [the longest x1 15.5 us: shards(): lax.all_to_all(tile.astype(jnp.bfloat16).reshape(own, 8, -1), EVENT, 0, 0)]
    dot_general x25 -> x7, matrix products: 19.8 us -> 34 us  [the longest x4 18.3 us: field_of(): jnp.dot(jnp.concatenate(split3(kernel)), stacked, preferred_element_type=...]
    all_to_all x0 -> x3, waiting for transfers between devices: none -> 13.5 us  [the longest x2 13.5 us: share(): return lax.all_to_all(spread, axes, 0, 0)]
  transfers between devices with their start and end apart: 2 -> 3, of which waited for: 2 -> 2; matrix products, arithmetic and copies ran while one was open for 1% -> 12% of each run, Pallas kernels for 0% -> 0%
where the time goes in v1:
time: 168 us; the launch traced here: 167 us
  blocking collectives  63.7 us (38%)
  matrix products  34 us (20%)
  starting transfers between devices  28.2 us (17%)
  other arithmetic  21.7 us (13%)
  waiting for transfers between devices  13.5 us (8%)
  local copies, waits for them, and re-layouts  4.84 us (3%)
    all_to_all x5, blocking collectives, share(): return lax.all_to_all(spread, axes, 0, 0)  63.7 us
    dot_general x4, matrix products, field_of(): jnp.dot(jnp.concatenate(split3(kernel)), stacked, preferred_element_type=...  18.3 us
    all_to_all x1, starting transfers between devices, shards(): lax.all_to_all(tile.astype(jnp.bfloat16).reshape(own, 8, -1), EVENT, 0, 0)  15.5 us
    all_to_all x2, waiting for transfers between devices, share(): return lax.all_to_all(spread, axes, 0, 0)  13.5 us
    dot_general x2, matrix products, amplitudes(): jnp.dot(chooser, angular_basis, preferred_element_type=jnp.float32)  13.4 us
    all_to_all x2, starting transfers between devices, share(): return lax.all_to_all(spread, axes, 0, 0)  12.7 us
    convert_element_type x1, other arithmetic, amplitudes(): return jnp.stack([real, imag]).astype(jnp.bfloat16)  6.17 us
  transfers between devices with their start and end apart: 3, of which 2 were waited for; matrix products, arithmetic and copies ran while one was open for 12% of the time, Pallas kernels for 0%

profile of v1, /device:TPU:1, one launch (start us, length us, event | category | flops | bytes accessed | tf_op | source)
XLA Modules:
  0.0 167.1 jit_solution(14658214878688864489)
XLA Ops:
  0.7 0.7 broadcast_subtract_fusion
  1.5 0.7 convert_bitcast_fusion
  2.1 0.7 fusion.80
  3.0 0.7 stack.100
  4.4 7.6 %all-to-all-start = ((f32[8,4,128]{2,1,0:T(4,128)}), f32[8,4,128]{2,1,0:T(4,128)S(1)}, u32[]{:S(2)}, u32[]{:S(2)}) async-start(f32[8,4,128]{2,1,0:T(4,128)} %broadcast_in_dim.108), calls=%async_computation | async-start | bytes 32768 | tf_op jit(solution)/shard_map/all_to_all | solution.py:15
  12.1 6.6 %all-to-all-done = f32[8,4,128]{2,1,0:T(4,128)S(1)} async-done(((f32[8,4,128]{2,1,0:T(4,128)}), f32[8,4,128]{2,1,0:T(4,128)S(1)}, u32[]{:S(2)}, u32[]{:S(2)}) %all-to-all-start) | async-done | bytes 16416 | tf_op jit(solution)/shard_map/all_to_all | solution.py:15
  19.4 6.0 %fusion.28 = (bf16[1,512,3072]{2,1,0:T(8,128)(2,1)S(1)}, bf16[1,512,3072]{2,1,0:T(8,128)(2,1)S(1)}) fusion(f32[512]{0:T(512)S(1)} %sub.117, f32[512]{0:T(512)S(1)} %mul.548, f32[3072]{0:T(1024)} %param.10, f32[512]{0:T(512)S(1)} %sub.121, f32[512]{0:T(512)S(1)} %mul.553, f32[512]{0:T(512)S(1)} %broadcast_in_dim_unstack.2, f32[512]{0:T(512)S(1)} %mul.544, ...), kind=kOutput, calls=%fused_computation.40 | convolution fusion | flops 232816640 | bytes 6711296 | tf_op jit(solution)/shard_map/dot_general | solution.py:46
  26.0 2.3 %fusion.81 = f32[128,1024]{1,0:T(8,128)S(1)} fusion(bf16[128,3072]{1,0:T(8,128)(2,1)S(1)} %bitcast.132, bf16[1024,3072]{1,0:T(8,128)(2,1)S(1)} %bitcast.131), kind=kOutput, calls=%fused_computation.211 | convolution fusion | flops 805306368 | bytes 7602176 | tf_op jit(solution)/shard_map/dot_general | solution.py:75
  28.5 0.7 fusion.31
  29.2 15.5 %all-to-all-start.1 = ((bf16[64,8,128]{2,1,0:T(8,128)(2,1)}), bf16[64,8,128]{2,1,0:T(8,128)(2,1)S(1)}, u32[]{:S(2)}, u32[]{:S(2)}) async-start(bf16[64,8,128]{2,1,0:T(8,128)(2,1)} %fusion.31), calls=%async_computation.1 | async-start | bytes 262144 | tf_op jit(solution)/shard_map/all_to_all | solution.py:82
  44.7 7.5 %fusion.3 = (bf16[1,512,4096]{2,1,0:T(8,128)(2,1)S(1)}, bf16[1,512,4096]{2,1,0:T(8,128)(2,1)}) fusion(f32[512]{0:T(512)S(1)} %mul.553, f32[512]{0:T(512)S(1)} %broadcast_in_dim_unstack.2, f32[512]{0:T(512)S(1)} %mul.548, f32[512]{0:T(512)S(1)} %sub.121, f32[4096]{0:T(1024)S(1)} %copy-done.2, f32[512]{0:T(512)S(1)} %sub.117, f32[512]{0:T(512)S(1)} %mul.544, ...), kind=kOutput, calls=%fused_computation.12 | convolution fusion | flops 310411264 | bytes 8943616 | tf_op jit(solution)/shard_map/dot_general | solution.py:46
  52.2 6.2 %maximum_convert_fusion = bf16[2,512,4096]{2,1,0:T(8,128)(2,1)} fusion(bf16[1,512,4096]{2,1,0:T(8,128)(2,1)} %get-tuple-element.31, bf16[1,512,4096]{2,1,0:T(8,128)(2,1)S(1)} %get-tuple-element.30), kind=kLoop, calls=%fused_computation | loop fusion | flops 4194304 | bytes 16777216 | tf_op jit(solution)/shard_map/convert_element_type | solution.py:56
  58.3 1.4 dynamic-slice_convert_fusion
  59.8 4.6 %fusion.40 = f32[6,4096]{1,0:T(8,128)S(1)} fusion(bf16[1024,4096]{1,0:T(8,128)(2,1)} %bitcast.127, bf16[2,1024]{1,0:T(2,128)(2,1)S(1)} %get-tuple-element.61, bf16[2,1024]{1,0:T(2,128)(2,1)S(1)} %get-tuple-element.60, bf16[2,1024]{1,0:T(2,128)(2,1)S(1)} %get-tuple-element.59), kind=kOutput, calls=%fused_computation.94 | convolution fusion | flops 50368512 | bytes 8499200 | tf_op jit(solution)/shard_map/dot_general | solution.py:98
  64.6 0.7 add_reduce_fusion.2
  66.7 0.6 fusion.69
  67.3 0.7 bitcast_add_fusion.5
  68.7 18.0 %all_to_all.40 = f32[32,2,128]{2,1,0:T(2,128)S(1)} all-to-all(f32[32,2,128]{2,1,0:T(2,128)S(1)} %broadcast_in_dim.110), channel_id=1, replica_groups=mesh['z'=4,'x'=8,'core'=2,'wrow'=8] {'z','x'}, dimensions={0} | all-to-all | bytes 65536 | tf_op jit(solution)/shard_map/all_to_all | solution.py:15
  87.3 5.1 %all-to-all-start.3 = ((f32[16,2,128]{2,1,0:T(2,128)}), f32[16,2,128]{2,1,0:T(2,128)S(1)}, u32[]{:S(2)}, u32[]{:S(2)}) async-start(f32[16,2,128]{2,1,0:T(2,128)} %broadcast_in_dim.111), calls=%async_computation.3 | async-start | bytes 32768 | tf_op jit(solution)/shard_map/all_to_all | solution.py:15
  92.5 6.9 %all-to-all-done.3 = f32[16,2,128]{2,1,0:T(2,128)S(1)} async-done(((f32[16,2,128]{2,1,0:T(2,128)}), f32[16,2,128]{2,1,0:T(2,128)S(1)}, u32[]{:S(2)}, u32[]{:S(2)}) %all-to-all-start.3) | async-done | bytes 16416 | tf_op jit(solution)/shard_map/all_to_all | solution.py:15
  99.8 4.6 %fusion.46 = f32[6,4096]{1,0:T(8,128)S(1)} fusion(bf16[1024,4096]{1,0:T(8,128)(2,1)} %bitcast.128, bf16[2,1024]{1,0:T(2,128)(2,1)S(1)} %get-tuple-element.58, bf16[2,1024]{1,0:T(2,128)(2,1)S(1)} %get-tuple-element.57, bf16[2,1024]{1,0:T(2,128)(2,1)S(1)} %get-tuple-element.56), kind=kOutput, calls=%fused_computation.100 | convolution fusion | flops 50368512 | bytes 8499200 | tf_op jit(solution)/shard_map/dot_general | solution.py:98
  105.8 0.6 bitcast_add_fusion.3
  106.4 0.7 bitcast_add_fusion.2
  107.2 11.6 %all_to_all.41 = f32[32,2,128]{2,1,0:T(2,128)S(1)} all-to-all(f32[32,2,128]{2,1,0:T(2,128)S(1)} %broadcast_in_dim.113), channel_id=1, replica_groups=mesh['z'=4,'x'=8,'core'=2,'wrow'=8] {'z','x'}, dimensions={0} | all-to-all | bytes 65536 | tf_op jit(solution)/shard_map/all_to_all | solution.py:15
  118.8 11.3 %all_to_all.42 = f32[16,2,128]{2,1,0:T(2,128)S(1)} all-to-all(f32[16,2,128]{2,1,0:T(2,128)S(1)} %broadcast_in_dim.114), channel_id=1, replica_groups=mesh['z'=4,'x'=8,'core'=2,'wrow'=8] {'core','wrow'}, dimensions={0} | all-to-all | bytes 32768 | tf_op jit(solution)/shard_map/all_to_all | solution.py:15
  130.5 4.6 %fusion.52 = f32[6,4096]{1,0:T(8,128)S(1)} fusion(bf16[1024,4096]{1,0:T(8,128)(2,1)} %bitcast.129, bf16[2,1024]{1,0:T(2,128)(2,1)S(1)} %get-tuple-element.55, bf16[2,1024]{1,0:T(2,128)(2,1)S(1)} %get-tuple-element.54, bf16[2,1024]{1,0:T(2,128)(2,1)S(1)} %get-tuple-element.53), kind=kOutput, calls=%fused_computation.106 | convolution fusion | flops 50368512 | bytes 8499200 | tf_op jit(solution)/shard_map/dot_general | solution.py:98
  136.5 1.3 bitcast_add_fusion
  137.9 11.6 %all_to_all.43 = f32[32,2,128]{2,1,0:T(2,128)S(1)} all-to-all(f32[32,2,128]{2,1,0:T(2,128)S(1)} %broadcast_in_dim.116), channel_id=1, replica_groups=mesh['z'=4,'x'=8,'core'=2,'wrow'=8] {'z','x'}, dimensions={0} | all-to-all | bytes 65536 | tf_op jit(solution)/shard_map/all_to_all | solution.py:15
  149.5 11.3 %all_to_all.44 = f32[16,2,128]{2,1,0:T(2,128)S(1)} all-to-all(f32[16,2,128]{2,1,0:T(2,128)S(1)} %broadcast_in_dim.117), channel_id=1, replica_groups=mesh['z'=4,'x'=8,'core'=2,'wrow'=8] {'core','wrow'}, dimensions={0} | all-to-all | bytes 32768 | tf_op jit(solution)/shard_map/all_to_all | solution.py:15
  161.1 0.6 constant_dynamic-slice_fusion
  161.8 4.6 %fusion.58 = f32[6,4096]{1,0:T(8,128)S(1)} fusion(bf16[1024,4096]{1,0:T(8,128)(2,1)} %bitcast.130, bf16[2,1024]{1,0:T(2,128)(2,1)S(1)} %get-tuple-element.52, bf16[2,1024]{1,0:T(2,128)(2,1)S(1)} %get-tuple-element.51, bf16[2,1024]{1,0:T(2,128)(2,1)S(1)} %get-tuple-element.50), kind=kOutput, calls=%fused_computation.112 | convolution fusion | flops 50368512 | bytes 8499200 | tf_op jit(solution)/shard_map/dot_general | solution.py:98
  166.4 0.6 fusion.64
  (114 shorter events, 9.6 us)
Async XLA Ops:
  0.6 44.0 %copy-start = (bf16[64,4096]{1,0:T(8,128)(2,1)S(1)}, bf16[64,4096]{1,0:T(8,128)(2,1)}, u32[]{:S(2)}) copy-start(bf16[64,4096]{1,0:T(8,128)(2,1)} %param.13) | copy-start | bytes 1572868
  4.4 14.3 %all-to-all-start = ((f32[8,4,128]{2,1,0:T(4,128)}), f32[8,4,128]{2,1,0:T(4,128)S(1)}, u32[]{:S(2)}, u32[]{:S(2)}) async-start(f32[8,4,128]{2,1,0:T(4,128)} %broadcast_in_dim.108), calls=%async_computation | async-start | bytes 32768 | tf_op jit(solution)/shard_map/all_to_all | solution.py:15
  26.0 18.6 %copy-start.2 = (f32[4096]{0:T(1024)S(1)}, f32[4096]{0:T(1024)}, u32[]{:S(2)}) copy-start(f32[4096]{0:T(1024)} %param.12) | copy-start | bytes 49156
  29.2 36.2 %all-to-all-start.1 = ((bf16[64,8,128]{2,1,0:T(8,128)(2,1)}), bf16[64,8,128]{2,1,0:T(8,128)(2,1)S(1)}, u32[]{:S(2)}, u32[]{:S(2)}) async-start(bf16[64,8,128]{2,1,0:T(8,128)(2,1)} %fusion.31), calls=%async_computation.1 | async-start | bytes 262144 | tf_op jit(solution)/shard_map/all_to_all | solution.py:82
  59.8 4.7 %copy-start.1 = (f32[4096]{0:T(1024)S(1)}, f32[4096]{0:T(1024)}, u32[]{:S(2)}) copy-start(f32[4096]{0:T(1024)} %param.14) | copy-start | bytes 49156
  87.3 12.1 %all-to-all-start.3 = ((f32[16,2,128]{2,1,0:T(2,128)}), f32[16,2,128]{2,1,0:T(2,128)S(1)}, u32[]{:S(2)}, u32[]{:S(2)}) async-start(f32[16,2,128]{2,1,0:T(2,128)} %broadcast_in_dim.111), calls=%async_computation.3 | async-start | bytes 32768 | tf_op jit(solution)/shard_map/all_to_all | solution.py:15

commit v2 on v1

v2 whole, which is shorter than its diff:
```python
import functools

import jax
import jax.numpy as jnp
from jax import lax
from jax.experimental import pallas as pl
from jax.experimental.pallas import tpu as pltpu
from jax.sharding import Mesh, PartitionSpec as P

ITERS = 3
BACKGROUND = 0.5
ZX = ("z", "x")
EVENT = ("z", "x", "core")
PEERS = ("core", "wrow")
OWN = 64
LANES = 128
TILE = 256
CHUNK = 16
PARAMS = 6
VMEM_LIMIT = 24 << 20


def prepare_kernel(mass_ref, width_ref, wave_ref, level_ref, coupling_ref, place_ref, out_ref):
    count = mass_ref.shape[1]
    local = wave_ref[...] - place_ref[0] * OWN
    index = lax.broadcasted_iota(jnp.int32, (OWN, count), 1)
    owner = lax.broadcasted_iota(jnp.int32, (OWN, count), 0) == local
    first_at = jnp.min(jnp.where(owner, index, count), axis=1, keepdims=True)
    first = owner & (index == first_at)
    second = owner & (index != first_at)
    mass = mass_ref[...]
    square = mass * mass
    product = mass * width_ref[...]
    columns = [
        jnp.sum(jnp.where(mask, value, 0.0), axis=1, keepdims=True)
        for mask in (first, second)
        for value in (square, product)
    ]
    lane = lax.broadcasted_iota(jnp.int32, (OWN, LANES), 1)
    table = jnp.zeros((OWN, LANES), jnp.float32)
    for place, column in enumerate(columns):
        table = jnp.where(lane == place, column, table)
    turned = jnp.concatenate([table, jnp.zeros((LANES - OWN, LANES), jnp.float32)], axis=0).T
    rest = jnp.concatenate(
        [level_ref[...].astype(jnp.float32), coupling_ref[...], jnp.zeros((1, OWN), jnp.float32)], axis=0
    )
    rows = jnp.concatenate([turned[0:4, 0:OWN], rest], axis=1)
    send_terms(rows, out_ref)


def load_table(table_ref, wide_ref, chooser_ref):
    blocks = table_ref.shape[0]
    levels = chooser_ref.shape[1]
    for block in range(blocks):
        turned = jnp.concatenate([table_ref[block], jnp.zeros((LANES - 4, LANES), jnp.float32)], axis=0).T
        square_a, product_a, square_b, product_b = (turned[0:OWN, k : k + 1] for k in range(4))
        level = turned[OWN : 2 * OWN, 0:1]
        values = (
            square_a,
            square_b,
            product_a * square_b + product_b * square_a,
            product_a + product_b,
            product_a * product_b,
            2.0 * product_a * product_b,
        )
        rows = slice(block * OWN, (block + 1) * OWN)
        for place, value in enumerate(values):
            wide_ref[place, rows, :] = jnp.broadcast_to(value, (OWN, LANES))
        column = lax.broadcasted_iota(jnp.int32, (OWN, levels), 1).astype(jnp.float32)
        chooser_ref[rows, :] = (level == column).astype(jnp.bfloat16)


def fill_tile(mass_row, basis_tile, wide_ref, chooser_ref, store):
    waves = chooser_ref.shape[0]
    for start in range(0, waves, OWN):
        angular = jnp.dot(chooser_ref[start : start + OWN, :], basis_tile, preferred_element_type=jnp.float32)
        for inner in range(0, OWN, CHUNK):
            rows = slice(start + inner, start + inner + CHUNK)
            for half in range(0, TILE, LANES):
                mass = mass_row[:, half : half + LANES]
                gap = wide_ref[0, rows, :] - mass
                other = wide_ref[1, rows, :] - mass
                mixed = wide_ref[2, rows, :] - wide_ref[3, rows, :] * mass
                cross = gap * other
                pair = wide_ref[4, rows, :]
                lower = cross - pair
                mixed_square = mixed * mixed
                scale = angular[inner : inner + CHUNK, half : half + LANES] / (mixed_square + lower * lower)
                real = mixed * (cross + pair) * scale
                imag = (mixed_square - wide_ref[5, rows, :] * lower) * scale
                store(2 * start + inner, half, real.astype(jnp.bfloat16), imag.astype(jnp.bfloat16))


def gram_kernel(scale, table_ref, mass_ref, basis_ref, place_ref, out_ref, wide_ref, chooser_ref, amp_ref, sum_ref, turn_ref):
    load_table(table_ref, wide_ref, chooser_ref)
    sum_ref[...] = jnp.zeros_like(sum_ref)
    blocks = table_ref.shape[0]

    def store(row, half, real, imag):
        amp_ref[row : row + CHUNK, half : half + LANES] = real
        amp_ref[row + OWN : row + OWN + CHUNK, half : half + LANES] = imag

    @pl.loop(0, mass_ref.shape[1] // TILE)
    def _(step):
        columns = pl.ds(pl.multiple_of(step * TILE, TILE), TILE)
        fill_tile(mass_ref[:, columns], basis_ref[:, columns], wide_ref, chooser_ref, store)
        own = amp_ref[pl.ds(pl.multiple_of(place_ref[0] * 2 * OWN, 2 * OWN), 2 * OWN), :]
        sum_ref[...] += lax.dot_general(
            amp_ref[...], own, (((1,), (1,)), ((), ())), preferred_element_type=jnp.float32
        )

    for block in range(blocks):
        real_rows = sum_ref[2 * block * OWN : (2 * block + 1) * OWN, :]
        imag_rows = sum_ref[(2 * block + 1) * OWN : (2 * block + 2) * OWN, :]
        gram_real = real_rows + pltpu.roll(imag_rows, OWN, 1)
        gram_imag = imag_rows - pltpu.roll(real_rows, OWN, 1)
        turned = (jnp.concatenate([gram_real, gram_imag], axis=0) * scale).T
        turn_ref[:, block, :] = turned[0:OWN, :]
    out_ref[...] = turn_ref[...].astype(jnp.bfloat16)


def load_coupling(coupling, parts_ref):
    blocks = coupling.shape[0]
    signed, swapped = signs(coupling)
    parts_ref[...] = jnp.zeros_like(parts_ref)
    for row, value in enumerate((signed, swapped)):
        high = value.astype(jnp.bfloat16)
        rest = value - high.astype(jnp.float32)
        middle = rest.astype(jnp.bfloat16)
        low = (rest - middle.astype(jnp.float32)).astype(jnp.bfloat16)
        for place, part in enumerate((high, middle, low)):
            wide = part.astype(jnp.float32)
            for block in range(blocks):
                parts_ref[2 * place + row : 2 * place + row + 1, block * LANES : (block + 1) * LANES] = wide[block : block + 1]
    return signed, swapped


def field_of(parts, amp_tile):
    sums = jnp.dot(parts, amp_tile, preferred_element_type=jnp.float32)
    real = (sums[4:5] + sums[2:3]) + sums[0:1]
    imag = (sums[5:6] + sums[3:4]) + sums[1:2]
    return real, imag


def project_tile(real, imag, weight, own_tile, by_real_ref, by_imag_ref, curve_ref):
    power = real * real + imag * imag
    inverse = 1.0 / (power + BACKGROUND)
    weighting = weight * inverse
    real = real * weighting
    imag = imag * weighting
    curving = weighting * power * inverse
    for start in range(0, own_tile.shape[0], CHUNK):
        rows = slice(start, start + CHUNK)
        by_real = by_real_ref[rows, :]
        by_imag = by_imag_ref[rows, :]
        curve = curve_ref[rows, :]
        for half in range(0, own_tile.shape[1], LANES):
            lanes = slice(half, half + LANES)
            value = own_tile[rows, lanes].astype(jnp.float32)
            by_real = by_real + value * real[:, lanes]
            by_imag = by_imag + value * imag[:, lanes]
            curve = curve + value * value * curving[:, lanes]
        by_real_ref[rows, :] = by_real
        by_imag_ref[rows, :] = by_imag
        curve_ref[rows, :] = curve


def gradient_rows(scale, by_real_ref, by_imag_ref, curve_ref):
    low, high = slice(0, OWN), slice(OWN, 2 * OWN)
    grad = jnp.concatenate(
        [-(by_real_ref[low, :] + by_imag_ref[high, :]), by_real_ref[high, :] - by_imag_ref[low, :]], axis=0
    )
    curve = jnp.concatenate([curve_ref[low, :] + curve_ref[high, :], jnp.zeros((OWN, LANES), jnp.float32)], axis=0)
    grad_row = jnp.sum(grad.T, axis=0, keepdims=True) * scale
    curve_row = jnp.sum(curve.T, axis=0, keepdims=True) * scale
    return jnp.concatenate([grad_row, curve_row], axis=0)


def gram_rows(gram, signed, swapped, place_ref):
    mixed_real = jnp.sum(gram * signed, keepdims=True)
    mixed_imag = jnp.sum(gram * swapped, keepdims=True)
    row_weight = jnp.sum(jnp.abs(gram), keepdims=True)
    lane = lax.broadcasted_iota(jnp.int32, (1, LANES), 1)
    here = place_ref[1]
    grad_row = jnp.where(lane == here, mixed_real, 0.0) + jnp.where(lane == here + OWN, mixed_imag, 0.0)
    curve_row = jnp.where(lane == here + OWN, row_weight, 0.0)
    return jnp.concatenate([grad_row, curve_row], axis=0)


def signs(coupling):
    lane = lax.broadcasted_iota(jnp.int32, coupling.shape, 1)
    return jnp.where(lane < OWN, coupling, -coupling), pltpu.roll(coupling, OWN, 1)


def send_terms(terms, out_ref):
    for peer in range(out_ref.shape[0]):
        out_ref[peer] = terms


def merge_kernel(received_ref, out_ref):
    send_terms(jnp.sum(received_ref[...], axis=0), out_ref)


def clear(*refs):
    for ref in refs:
        ref[...] = jnp.zeros_like(ref)


def own_rows(place_ref):
    return pl.ds(pl.multiple_of(place_ref[0] * 2 * OWN, 2 * OWN), 2 * OWN)


def first_kernel(
    scale, table_ref, mass_ref, basis_ref, weight_ref, place_ref, pieces_ref, out_ref, coupling_ref, amp_ref, gram_ref,
    wide_ref, chooser_ref, parts_ref, by_real_ref, by_imag_ref, curve_ref
):
    load_table(table_ref, wide_ref, chooser_ref)
    for block in range(table_ref.shape[0]):
        half = table_ref[block]
        coupling_ref[block : block + 1, :] = jnp.concatenate([half[1:2, OWN:LANES], half[2:3, OWN:LANES]], axis=1)
    signed, swapped = load_coupling(coupling_ref[...], parts_ref)
    parts = parts_ref[...].astype(jnp.bfloat16)
    clear(by_real_ref, by_imag_ref, curve_ref)

    @pl.loop(0, mass_ref.shape[1] // TILE)
    def _(step):
        origin = pl.multiple_of(step * TILE, TILE)
        columns = pl.ds(origin, TILE)

        def store(row, half, real, imag):
            lanes = pl.ds(pl.multiple_of(origin + half, LANES), LANES)
            amp_ref[row : row + CHUNK, lanes] = real
            amp_ref[row + OWN : row + OWN + CHUNK, lanes] = imag

        fill_tile(mass_ref[:, columns], basis_ref[:, columns], wide_ref, chooser_ref, store)
        real, imag = field_of(parts, amp_ref[:, columns])
        own = amp_ref[own_rows(place_ref), columns]
        project_tile(real, imag, weight_ref[:, columns], own, by_real_ref, by_imag_ref, curve_ref)

    gram = jnp.sum(pieces_ref[...].astype(jnp.float32), axis=0)
    gram_ref[...] = gram
    terms = gradient_rows(scale, by_real_ref, by_imag_ref, curve_ref)
    send_terms(terms + gram_rows(gram, signed, swapped, place_ref), out_ref)


def new_coupling(received_ref, coupling_ref):
    blocks = coupling_ref.shape[0]
    total = received_ref[0:blocks] + received_ref[blocks : 2 * blocks]
    grad = total[:, 0, :]
    curve = total[:, 1, :]
    return coupling_ref[...] - grad / (curve + pltpu.roll(curve, OWN, 1))


def next_kernel(
    scale, received_ref, old_ref, amp_ref, weight_ref, place_ref, gram_ref, out_ref, coupling_ref,
    parts_ref, by_real_ref, by_imag_ref, curve_ref
):
    coupling = new_coupling(received_ref, old_ref)
    coupling_ref[...] = coupling
    signed, swapped = load_coupling(coupling, parts_ref)
    parts = parts_ref[...].astype(jnp.bfloat16)
    clear(by_real_ref, by_imag_ref, curve_ref)

    @pl.loop(0, amp_ref.shape[1] // (2 * TILE))
    def _(step):
        columns = pl.ds(pl.multiple_of(step * 2 * TILE, 2 * TILE), 2 * TILE)
        real, imag = field_of(parts, amp_ref[:, columns])
        own = amp_ref[own_rows(place_ref), columns]
        project_tile(real, imag, weight_ref[:, columns], own, by_real_ref, by_imag_ref, curve_ref)

    terms = gradient_rows(scale, by_real_ref, by_imag_ref, curve_ref)
    send_terms(terms + gram_rows(gram_ref[...], signed, swapped, place_ref), out_ref)


def last_kernel(received_ref, old_ref, amp_ref, place_ref, coupling_out_ref, intensity_ref, parts_ref, coupling_ref):
    coupling = new_coupling(received_ref, old_ref)
    coupling_ref[...] = coupling
    load_coupling(coupling, parts_ref)
    parts = parts_ref[...].astype(jnp.bfloat16)
    mine = coupling_ref[pl.ds(place_ref[0], 1), :]
    coupling_out_ref[0:1, :] = mine[:, 0:OWN]
    coupling_out_ref[1:2, :] = pltpu.roll(mine, OWN, 1)[:, 0:OWN]

    @pl.loop(0, amp_ref.shape[1] // (2 * TILE))
    def _(step):
        columns = pl.ds(pl.multiple_of(step * 2 * TILE, 2 * TILE), 2 * TILE)
        real, imag = field_of(parts, amp_ref[:, columns])
        intensity_ref[:, columns] = real * real + imag * imag + BACKGROUND


def call(kernel, outs, scratch, *args, smem):
    specs = [pl.BlockSpec(memory_space=pltpu.SMEM if place in smem else pltpu.VMEM) for place in range(len(args))]
    single = not isinstance(outs, tuple)
    return pl.pallas_call(
        kernel,
        out_shape=outs,
        in_specs=specs,
        out_specs=pl.BlockSpec(memory_space=pltpu.VMEM) if single else tuple(pl.BlockSpec(memory_space=pltpu.VMEM) for _ in outs),
        scratch_shapes=scratch,
        compiler_params=pltpu.CompilerParams(vmem_limit_bytes=VMEM_LIMIT),
    )(*args)


def shape(*dims, dtype=jnp.float32):
    return jax.ShapeDtypeStruct(dims, dtype)


def table_scratch(waves, levels):
    return [pltpu.VMEM((PARAMS, waves, LANES), jnp.float32), pltpu.VMEM((waves, levels), jnp.bfloat16)]


def pass_scratch(waves):
    return [pltpu.VMEM((8, 2 * waves), jnp.float32)] + [pltpu.VMEM((2 * OWN, LANES), jnp.float32) for _ in range(3)]


def shards(
    mc_mass, mc_basis, data_mass, data_basis, data_weight, res_mass, res_width, res_wave, wave_q, couplings
):
    rows = lax.axis_size("wrow")
    waves = OWN * rows
    zx = lax.axis_size("z") * lax.axis_size("x")
    events = zx * lax.axis_size("core")
    levels = mc_basis.shape[0]
    mc_count, data_count = mc_mass.shape[0], data_mass.shape[0]
    places = jnp.stack([lax.axis_index("wrow"), lax.axis_index(EVENT)]).astype(jnp.int32)
    own_table = call(
        prepare_kernel,
        shape(rows, 4, LANES),
        [],
        res_mass[None], res_width[None], res_wave[None], wave_q[None], couplings, places,
        smem=(5,),
    )
    table = lax.all_to_all(own_table, "wrow", 0, 0)
    tile = call(
        functools.partial(gram_kernel, 1.0 / (mc_count * events)),
        shape(OWN, rows, LANES, dtype=jnp.bfloat16),
        table_scratch(waves, levels)
        + [
            pltpu.VMEM((2 * waves, TILE), jnp.bfloat16),
            pltpu.VMEM((2 * waves, LANES), jnp.float32),
            pltpu.VMEM((OWN, rows, LANES), jnp.float32),
        ],
        table, mc_mass[None], mc_basis, places,
        smem=(3,),
    )
    pieces = lax.all_to_all(tile, EVENT, 0, 0)
    weight = data_weight[None]
    inverse_count = 1.0 / (data_count * events)
    amp_shape = pltpu.VMEM((2 * waves, data_count), jnp.bfloat16)
    terms, coupling, amp, gram_row = call(
        functools.partial(first_kernel, inverse_count),
        (shape(zx, 2, LANES), shape(rows, LANES), amp_shape, shape(rows, LANES)),
        table_scratch(waves, levels) + pass_scratch(waves),
        table, data_mass[None], data_basis, weight, places, pieces,
        smem=(4,),
    )

    def exchange(values):
        merged = call(merge_kernel, shape(2 * rows, 2, LANES), [], lax.all_to_all(values, ZX, 0, 0), smem=())
        return lax.all_to_all(merged, PEERS, 0, 0)

    for _ in range(1, ITERS):
        received = exchange(terms)
        terms, coupling = call(
            functools.partial(next_kernel, inverse_count),
            (shape(zx, 2, LANES), shape(rows, LANES)),
            pass_scratch(waves),
            received, coupling, amp, weight, places, gram_row,
            smem=(4,),
        )
    received = exchange(terms)
    coupling_out, intensity = call(
        last_kernel,
        (shape(2, OWN), shape(1, data_count)),
        [pltpu.VMEM((8, 2 * waves), jnp.float32), pltpu.VMEM((rows, LANES), jnp.float32)],
        received, coupling, amp, places,
        smem=(3,),
    )
    return coupling_out, intensity.reshape(data_count)


def solution(mesh):
    chips = Mesh(mesh.devices.reshape(4, 8, 2, 8), ("z", "x", "core", "wrow"))
    placed = (
        P(EVENT),
        P(None, EVENT),
        P(EVENT),
        P(None, EVENT),
        P(EVENT),
        P("wrow"),
        P("wrow"),
        P("wrow"),
        P("wrow"),
        P(None, "wrow"),
    )
    return jax.shard_map(
        shards, mesh=chips, in_specs=placed, out_specs=(P(None, "wrow"), P(EVENT)), check_vma=False
    )
```

time: 168 us -> 155 us (0.923)
  blocking collectives: 63.7 us -> 109 us
  Pallas kernels: 0 us -> 36.6 us
  matrix products: 34 us -> 0 us
  starting transfers between devices: 28.2 us -> 0 us
  other arithmetic: 21.7 us -> 0.08 us
  waiting for transfers between devices: 13.5 us -> 0 us
  local copies, waits for them, and re-layouts: 4.84 us -> 7.48 us
    all_to_all x5 -> x8, blocking collectives: 63.7 us -> 109 us  [the longest x3 34.8 us: exchange(): lax.all_to_all(values, ZX, 0, 0)]
    pallas_call x0 -> x9, Pallas kernels: none -> 36.6 us  [call(): pl.pallas_call(kernel, out_shape=outs, in_specs=specs, out_specs=pl.Block...]
    dot_general x7 -> x0, matrix products: 34 us -> none  [the longest x4 18.3 us: field_of(): jnp.dot(jnp.concatenate(split3(kernel)), stacked, preferred_element_type=...]
    all_to_all x3 -> x0, starting transfers between devices: 28.2 us -> none  [the longest x1 15.5 us: shards(): lax.all_to_all(tile.astype(jnp.bfloat16).reshape(own, 8, -1), EVENT, 0, 0)]
    all_to_all x3 -> x0, waiting for transfers between devices: 13.5 us -> none  [the longest x2 13.5 us: share(): return lax.all_to_all(spread, axes, 0, 0)]
    convert_element_type x7 -> x0, other arithmetic: 8.41 us -> none  [the longest x1 6.17 us: amplitudes(): return jnp.stack([real, imag]).astype(jnp.bfloat16)]
    unnamed x9 -> x20, local copies, waits for them, and re-layouts: 0.03 us -> 7.48 us
    reduce_sum x15 -> x0, other arithmetic: 4.81 us -> none  [the longest x3 1.92 us: shards(): jnp.sum(block[0] * carried[0] + block[1] * carried[1], axis=1)]
  transfers between devices with their start and end apart: 3 -> 0, of which waited for: 2 -> 0; matrix products, arithmetic and copies ran while one was open for 12% -> 0% of each run, Pallas kernels for 0% -> 0%
where the time goes in v2:
time: 155 us; the launch traced here: 154 us
  blocking collectives  109 us (70%)
  Pallas kernels  36.6 us (24%)
  local copies, waits for them, and re-layouts  7.48 us (5%)
    pallas_call x9, Pallas kernels, call(): pl.pallas_call(kernel, out_shape=outs, in_specs=specs, out_specs=pl.Block...  36.6 us
    all_to_all x3, blocking collectives, exchange(): lax.all_to_all(values, ZX, 0, 0)  34.8 us
    all_to_all x3, blocking collectives, exchange(): return lax.all_to_all(merged, PEERS, 0, 0)  33.8 us
    all_to_all x1, blocking collectives, shards(): pieces = lax.all_to_all(tile, EVENT, 0, 0)  26.3 us
    all_to_all x1, blocking collectives, shards(): table = lax.all_to_all(own_table, 'wrow', 0, 0)  14.1 us
    unnamed x20, local copies, waits for them, and re-layouts  7.48 us

profile of v2, /device:TPU:1, one launch (start us, length us, event | category | flops | bytes accessed | tf_op | source)
XLA Modules:
  0.0 153.8 jit_solution(11126469381280665300)
XLA Ops:
  0.6 0.1 pad_add_fusion.place_ref
  0.7 0.0 copy-start.5
  0.7 0.7 copy-done.5
  1.4 0.0 copy-start.6
  1.4 0.7 copy-done.6
  2.0 0.0 copy-start.7
  2.1 0.7 copy-done.7
  2.7 0.0 copy-start.8
  2.7 0.7 copy-done.8
  3.4 0.0 copy-start.9
  3.4 0.7 copy-done.9
  4.0 0.9 shard_map.113
  4.9 14.1 %all_to_all.40.table_ref = f32[8,4,128]{2,1,0:T(4,128)S(1)} all-to-all(f32[8,4,128]{2,1,0:T(4,128)S(1)} %shard_map.113), channel_id=1, replica_groups=mesh['z'=4,'x'=8,'core'=2,'wrow'=8] {'wrow'}, dimensions={0} | all-to-all | bytes 32768 | tf_op jit(solution)/shard_map/all_to_all | solution.py:333
  18.9 0.0 copy-start.1
  18.9 1.0 copy-done.1
  19.9 0.0 copy-start.4
  19.9 0.7 copy-done.4
  20.6 11.6 %shard_map.114 = bf16[64,8,128]{2,1,0:T(8,128)(2,1)S(1)} custom-call(f32[8,4,128]{2,1,0:T(4,128)S(1)} %all_to_all.40.table_ref, f32[1,3072]{1,0:T(1,128)S(1)} %bitcast.14, bf16[64,3072]{1,0:T(8,128)(2,1)S(1)} %copy-done.1, s32[2]{0:T(128)S(1)} %pad_add_fusion.place_ref), custom_call_target="tpu_custom_call" | custom-call | tf_op jit(solution)/shard_map/pallas_call | solution.py:294
  32.3 26.3 %all_to_all.41.pieces_ref = bf16[64,8,128]{2,1,0:T(8,128)(2,1)S(1)} all-to-all(bf16[64,8,128]{2,1,0:T(8,128)(2,1)S(1)} %shard_map.114), channel_id=1, replica_groups=mesh['z'=4,'x'=8,'core'=2,'wrow'=8] {'z','x','core'}, dimensions={0} | all-to-all | bytes 262144 | tf_op jit(solution)/shard_map/all_to_all | solution.py:346
  58.6 1.0 copy-done
  59.6 0.7 copy-done.2
  60.3 0.7 copy-done.3
  61.1 13.5 %shard_map.115 = (f32[32,2,128]{2,1,0:T(2,128)S(1)}, f32[8,128]{1,0:T(8,128)S(1)}, bf16[1024,4096]{1,0:T(8,128)(2,1)S(1)}, f32[8,128]{1,0:T(8,128)S(1)}) custom-call(f32[8,4,128]{2,1,0:T(4,128)S(1)} %all_to_all.40.table_ref, f32[1,4096]{1,0:T(1,128)S(1)} %bitcast.13, bf16[64,4096]{1,0:T(8,128)(2,1)S(1)} %copy-done, f32[1,4096]{1,0:T(1,128)S(1)} %bitcast.10, ...), custom_call_target="tpu_custom_call" | custom-call | tf_op jit(solution)/shard_map/pallas_call | solution.py:294
  74.6 11.6 %all_to_all.42.received_ref = f32[32,2,128]{2,1,0:T(2,128)S(1)} all-to-all(f32[32,2,128]{2,1,0:T(2,128)S(1)} %get-tuple-element.12), channel_id=1, replica_groups=mesh['z'=4,'x'=8,'core'=2,'wrow'=8] {'z','x'}, dimensions={0} | all-to-all | bytes 65536 | tf_op jit(solution)/shard_map/all_to_all | solution.py:359
  86.2 11.3 %all_to_all.43.received_ref = f32[16,2,128]{2,1,0:T(2,128)S(1)} all-to-all(f32[16,2,128]{2,1,0:T(2,128)S(1)} %shard_map.116), channel_id=1, replica_groups=mesh['z'=4,'x'=8,'core'=2,'wrow'=8] {'core','wrow'}, dimensions={0} | all-to-all | bytes 32768 | tf_op jit(solution)/shard_map/all_to_all | solution.py:360
  97.5 3.6 %shard_map.117 = (f32[32,2,128]{2,1,0:T(2,128)S(1)}, f32[8,128]{1,0:T(8,128)S(1)}) custom-call(f32[16,2,128]{2,1,0:T(2,128)S(1)} %all_to_all.43.received_ref, f32[8,128]{1,0:T(8,128)S(1)} %get-tuple-element.13.old_ref, bf16[1024,4096]{1,0:T(8,128)(2,1)S(1)} %get-tuple-element.14.amp_ref, f32[1,4096]{1,0:T(1,128)S(1)} %bitcast.11, ...), custom_call_target="tpu_custom_call" | custom-call | tf_op jit(solution)/shard_map/pallas_call | solution.py:294
  101.0 11.6 %all_to_all.44.received_ref = f32[32,2,128]{2,1,0:T(2,128)S(1)} all-to-all(f32[32,2,128]{2,1,0:T(2,128)S(1)} %get-tuple-element.16), channel_id=1, replica_groups=mesh['z'=4,'x'=8,'core'=2,'wrow'=8] {'z','x'}, dimensions={0} | all-to-all | bytes 65536 | tf_op jit(solution)/shard_map/all_to_all | solution.py:359
  112.7 11.3 %all_to_all.45.received_ref = f32[16,2,128]{2,1,0:T(2,128)S(1)} all-to-all(f32[16,2,128]{2,1,0:T(2,128)S(1)} %shard_map.118), channel_id=1, replica_groups=mesh['z'=4,'x'=8,'core'=2,'wrow'=8] {'core','wrow'}, dimensions={0} | all-to-all | bytes 32768 | tf_op jit(solution)/shard_map/all_to_all | solution.py:360
  123.9 3.6 %shard_map.119 = (f32[32,2,128]{2,1,0:T(2,128)S(1)}, f32[8,128]{1,0:T(8,128)S(1)}) custom-call(f32[16,2,128]{2,1,0:T(2,128)S(1)} %all_to_all.45.received_ref, f32[8,128]{1,0:T(8,128)S(1)} %get-tuple-element.17.old_ref, bf16[1024,4096]{1,0:T(8,128)(2,1)S(1)} %get-tuple-element.14.amp_ref, f32[1,4096]{1,0:T(1,128)S(1)} %bitcast.12, ...), custom_call_target="tpu_custom_call" | custom-call | tf_op jit(solution)/shard_map/pallas_call | solution.py:294
  127.5 11.6 %all_to_all.46.received_ref = f32[32,2,128]{2,1,0:T(2,128)S(1)} all-to-all(f32[32,2,128]{2,1,0:T(2,128)S(1)} %get-tuple-element.18), channel_id=1, replica_groups=mesh['z'=4,'x'=8,'core'=2,'wrow'=8] {'z','x'}, dimensions={0} | all-to-all | bytes 65536 | tf_op jit(solution)/shard_map/all_to_all | solution.py:359
  139.1 11.3 %all_to_all.47.received_ref = f32[16,2,128]{2,1,0:T(2,128)S(1)} all-to-all(f32[16,2,128]{2,1,0:T(2,128)S(1)} %shard_map.120), channel_id=1, replica_groups=mesh['z'=4,'x'=8,'core'=2,'wrow'=8] {'core','wrow'}, dimensions={0} | all-to-all | bytes 32768 | tf_op jit(solution)/shard_map/all_to_all | solution.py:360
  150.4 3.4 %shard_map.121 = (f32[2,64]{1,0:T(2,128)}, f32[1,4096]{1,0:T(1,128)}) custom-call(f32[16,2,128]{2,1,0:T(2,128)S(1)} %all_to_all.47.received_ref, f32[8,128]{1,0:T(8,128)S(1)} %get-tuple-element.19.old_ref, bf16[1024,4096]{1,0:T(8,128)(2,1)S(1)} %get-tuple-element.14.amp_ref, s32[2]{0:T(128)S(1)} %pad_add_fusion.place_ref), custom_call_target="tpu_custom_call" | custom-call | tf_op jit(solution)/shard_map/pallas_call | solution.py:294
  (6 shorter events, 0.1 us)
Async XLA Ops:
  0.7 0.7 copy-start.5
  1.4 0.7 copy-start.6
  2.0 0.7 copy-start.7
  2.7 0.7 copy-start.8
  3.4 0.7 copy-start.9
  18.9 1.0 copy-start.1
  19.9 0.7 copy-start.4
  58.6 1.0 copy-start
  59.6 0.7 copy-start.2
  60.3 0.7 copy-start.3

commit v3 on v2

--- a/solution.py
+++ b/solution.py
@@ -14,13 +14,46 @@
 PEERS = ("core", "wrow")
 OWN = 64
 LANES = 128
-TILE = 256
+TILE = 512
 CHUNK = 16
+ROWS = 8
 PARAMS = 6
 VMEM_LIMIT = 24 << 20
 
 
-def prepare_kernel(mass_ref, width_ref, wave_ref, level_ref, coupling_ref, place_ref, out_ref):
+def prepare_kernel(
+    mass_in, width_in, wave_in, level_in, coupling_in, mc_mass_in, mc_basis_in, data_mass_in, data_basis_in,
+    weight_in, place_ref, out_ref, mc_mass_out, mc_basis_out, data_mass_out, data_basis_out, weight_out,
+    mass_ref, width_ref, wave_ref, level_ref, coupling_ref, small_sems, large_sems
+):
+    small = [
+        pltpu.make_async_copy(source, target, small_sems.at[place])
+        for place, (source, target) in enumerate(
+            (
+                (mass_in, mass_ref),
+                (width_in, width_ref),
+                (wave_in, wave_ref),
+                (level_in, level_ref),
+                (coupling_in, coupling_ref),
+            )
+        )
+    ]
+    large = [
+        pltpu.make_async_copy(source, target, large_sems.at[place])
+        for place, (source, target) in enumerate(
+            (
+                (mc_mass_in, mc_mass_out),
+                (mc_basis_in, mc_basis_out),
+                (data_mass_in, data_mass_out),
+                (data_basis_in, data_basis_out),
+                (weight_in, weight_out),
+            )
+        )
+    ]
+    for copy in small + large:
+        copy.start()
+    for copy in small:
+        copy.wait()
     count = mass_ref.shape[1]
     local = wave_ref[...] - place_ref[0] * OWN
     index = lax.broadcasted_iota(jnp.int32, (OWN, count), 1)
@@ -46,49 +79,59 @@
     )
     rows = jnp.concatenate([turned[0:4, 0:OWN], rest], axis=1)
     send_terms(rows, out_ref)
+    for copy in large:
+        copy.wait()
 
 
 def load_table(table_ref, wide_ref, chooser_ref):
     blocks = table_ref.shape[0]
     levels = chooser_ref.shape[1]
+    stacked = [table_ref[block] for block in range(blocks)]
+    stacked.append(jnp.zeros((LANES - 4 * blocks, LANES), jnp.float32))
+    turned = jnp.concatenate(stacked, axis=0).T
+    column = lax.broadcasted_iota(jnp.int32, (OWN, levels), 1).astype(jnp.float32)
     for block in range(blocks):
-        turned = jnp.concatenate([table_ref[block], jnp.zeros((LANES - 4, LANES), jnp.float32)], axis=0).T
-        square_a, product_a, square_b, product_b = (turned[0:OWN, k : k + 1] for k in range(4))
-        level = turned[OWN : 2 * OWN, 0:1]
-        values = (
-            square_a,
-            square_b,
-            product_a * square_b + product_b * square_a,
-            product_a + product_b,
-            product_a * product_b,
-            2.0 * product_a * product_b,
-        )
         rows = slice(block * OWN, (block + 1) * OWN)
-        for place, value in enumerate(values):
-            wide_ref[place, rows, :] = jnp.broadcast_to(value, (OWN, LANES))
-        column = lax.broadcasted_iota(jnp.int32, (OWN, levels), 1).astype(jnp.float32)
+        for pair in range(2):
+            first = 4 * block + 2 * pair
+            square = jnp.broadcast_to(turned[0:OWN, first : first + 1], (OWN, LANES))
+            product = jnp.broadcast_to(turned[0:OWN, first + 1 : first + 2], (OWN, LANES))
+            wide_ref[3 * pair, rows, :] = square
+            wide_ref[3 * pair + 1, rows, :] = product * product
+            wide_ref[3 * pair + 2, rows, :] = product
+        level = turned[OWN : 2 * OWN, 4 * block : 4 * block + 1]
         chooser_ref[rows, :] = (level == column).astype(jnp.bfloat16)
+
+
+def lineshapes(mass, wide_ref, rows):
+    real = imag = None
+    for pair in range(2):
+        product = wide_ref[3 * pair + 2, rows, :]
+        gap = wide_ref[3 * pair, rows, :] - mass
+        quotient = product / (gap * gap + wide_ref[3 * pair + 1, rows, :])
+        real = quotient * gap if real is None else real + quotient * gap
+        imag = quotient * product if imag is None else imag + quotient * product
+    return real, imag
 
 
 def fill_tile(mass_row, basis_tile, wide_ref, chooser_ref, store):
     waves = chooser_ref.shape[0]
+    masses = [
+        jnp.broadcast_to(mass_row[:, half : half + LANES], (ROWS, LANES)) for half in range(0, TILE, LANES)
+    ]
     for start in range(0, waves, OWN):
         angular = jnp.dot(chooser_ref[start : start + OWN, :], basis_tile, preferred_element_type=jnp.float32)
-        for inner in range(0, OWN, CHUNK):
-            rows = slice(start + inner, start + inner + CHUNK)
-            for half in range(0, TILE, LANES):
-                mass = mass_row[:, half : half + LANES]
-                gap = wide_ref[0, rows, :] - mass
-                other = wide_ref[1, rows, :] - mass
-                mixed = wide_ref[2, rows, :] - wide_ref[3, rows, :] * mass
-                cross = gap * other
-                pair = wide_ref[4, rows, :]
-                lower = cross - pair
-                mixed_square = mixed * mixed
-                scale = angular[inner : inner + CHUNK, half : half + LANES] / (mixed_square + lower * lower)
-                real = mixed * (cross + pair) * scale
-                imag = (mixed_square - wide_ref[5, rows, :] * lower) * scale
-                store(2 * start + inner, half, real.astype(jnp.bfloat16), imag.astype(jnp.bfloat16))
+        for inner in range(0, OWN, ROWS):
+            rows = slice(start + inner, start + inner + ROWS)
+            reals, imags = [], []
+            for half, mass in enumerate(masses):
+                real, imag = lineshapes(mass, wide_ref, rows)
+                scale = angular[inner : inner + ROWS, half * LANES : (half + 1) * LANES]
+                reals.append(real * scale)
+                imags.append(imag * scale)
+            real = jnp.concatenate(reals, axis=1).astype(jnp.bfloat16)
+            imag = jnp.concatenate(imags, axis=1).astype(jnp.bfloat16)
+            store(2 * start + inner, real, imag)
 
 
 def gram_kernel(scale, table_ref, mass_ref, basis_ref, place_ref, out_ref, wide_ref, chooser_ref, amp_ref, sum_ref, turn_ref):
@@ -96,9 +139,9 @@
     sum_ref[...] = jnp.zeros_like(sum_ref)
     blocks = table_ref.shape[0]
 
-    def store(row, half, real, imag):
-        amp_ref[row : row + CHUNK, half : half + LANES] = real
-        amp_ref[row + OWN : row + OWN + CHUNK, half : half + LANES] = imag
+    def store(row, real, imag):
+        amp_ref[row : row + ROWS, :] = real
+        amp_ref[row + OWN : row + OWN + ROWS, :] = imag
 
     @pl.loop(0, mass_ref.shape[1] // TILE)
     def _(step):
@@ -211,10 +254,9 @@
 
 
 def first_kernel(
-    scale, table_ref, mass_ref, basis_ref, weight_ref, place_ref, pieces_ref, out_ref, coupling_ref, amp_ref, gram_ref,
-    wide_ref, chooser_ref, parts_ref, by_real_ref, by_imag_ref, curve_ref
+    scale, table_ref, wide_ref, chooser_ref, mass_ref, basis_ref, weight_ref, place_ref, pieces_ref,
+    out_ref, coupling_ref, amp_ref, gram_ref, parts_ref, by_real_ref, by_imag_ref, curve_ref
 ):
-    load_table(table_ref, wide_ref, chooser_ref)
     for block in range(table_ref.shape[0]):
         half = table_ref[block]
         coupling_ref[block : block + 1, :] = jnp.concatenate([half[1:2, OWN:LANES], half[2:3, OWN:LANES]], axis=1)
@@ -224,13 +266,11 @@
 
     @pl.loop(0, mass_ref.shape[1] // TILE)
     def _(step):
-        origin = pl.multiple_of(step * TILE, TILE)
-        columns = pl.ds(origin, TILE)
-
-        def store(row, half, real, imag):
-            lanes = pl.ds(pl.multiple_of(origin + half, LANES), LANES)
-            amp_ref[row : row + CHUNK, lanes] = real
-            amp_ref[row + OWN : row + OWN + CHUNK, lanes] = imag
+        columns = pl.ds(pl.multiple_of(step * TILE, TILE), TILE)
+
+        def store(row, real, imag):
+            amp_ref[row : row + ROWS, columns] = real
+            amp_ref[row + OWN : row + OWN + ROWS, columns] = imag
 
         fill_tile(mass_ref[:, columns], basis_ref[:, columns], wide_ref, chooser_ref, store)
         real, imag = field_of(parts, amp_ref[:, columns])
@@ -261,9 +301,9 @@
     parts = parts_ref[...].astype(jnp.bfloat16)
     clear(by_real_ref, by_imag_ref, curve_ref)
 
-    @pl.loop(0, amp_ref.shape[1] // (2 * TILE))
+    @pl.loop(0, amp_ref.shape[1] // (TILE))
     def _(step):
-        columns = pl.ds(pl.multiple_of(step * 2 * TILE, 2 * TILE), 2 * TILE)
+        columns = pl.ds(pl.multiple_of(step * TILE, TILE), TILE)
         real, imag = field_of(parts, amp_ref[:, columns])
         own = amp_ref[own_rows(place_ref), columns]
         project_tile(real, imag, weight_ref[:, columns], own, by_real_ref, by_imag_ref, curve_ref)
@@ -281,32 +321,31 @@
     coupling_out_ref[0:1, :] = mine[:, 0:OWN]
     coupling_out_ref[1:2, :] = pltpu.roll(mine, OWN, 1)[:, 0:OWN]
 
-    @pl.loop(0, amp_ref.shape[1] // (2 * TILE))
+    @pl.loop(0, amp_ref.shape[1] // (TILE))
     def _(step):
-        columns = pl.ds(pl.multiple_of(step * 2 * TILE, 2 * TILE), 2 * TILE)
+        columns = pl.ds(pl.multiple_of(step * TILE, TILE), TILE)
         real, imag = field_of(parts, amp_ref[:, columns])
         intensity_ref[:, columns] = real * real + imag * imag + BACKGROUND
 
 
-def call(kernel, outs, scratch, *args, smem):
-    specs = [pl.BlockSpec(memory_space=pltpu.SMEM if place in smem else pltpu.VMEM) for place in range(len(args))]
+def call(kernel, outs, scratch, *args, smem, hbm=()):
+    def space(place):
+        return pltpu.SMEM if place in smem else pltpu.HBM if place in hbm else pltpu.VMEM
+
     single = not isinstance(outs, tuple)
+    whole = pl.BlockSpec(memory_space=pltpu.VMEM)
     return pl.pallas_call(
         kernel,
         out_shape=outs,
-        in_specs=specs,
-        out_specs=pl.BlockSpec(memory_space=pltpu.VMEM) if single else tuple(pl.BlockSpec(memory_space=pltpu.VMEM) for _ in outs),
+        in_specs=[pl.BlockSpec(memory_space=space(place)) for place in range(len(args))],
+        out_specs=whole if single else tuple(whole for _ in outs),
         scratch_shapes=scratch,
         compiler_params=pltpu.CompilerParams(vmem_limit_bytes=VMEM_LIMIT),
-    )(*args)
+    )(*(pltpu.with_memory_space_constraint(arg, pltpu.HBM) if place in hbm else arg for place, arg in enumerate(args)))
 
 
 def shape(*dims, dtype=jnp.float32):
     return jax.ShapeDtypeStruct(dims, dtype)
-
-
-def table_scratch(waves, levels):
-    return [pltpu.VMEM((PARAMS, waves, LANES), jnp.float32), pltpu.VMEM((waves, levels), jnp.bfloat16)]
 
 
 def pass_scratch(waves):
@@ -323,36 +362,55 @@
     levels = mc_basis.shape[0]
     mc_count, data_count = mc_mass.shape[0], data_mass.shape[0]
     places = jnp.stack([lax.axis_index("wrow"), lax.axis_index(EVENT)]).astype(jnp.int32)
-    own_table = call(
+    own_table, mc_mass, mc_basis, data_mass, data_basis, weight = call(
         prepare_kernel,
-        shape(rows, 4, LANES),
-        [],
-        res_mass[None], res_width[None], res_wave[None], wave_q[None], couplings, places,
-        smem=(5,),
+        (
+            shape(rows, 4, LANES),
+            shape(1, mc_count),
+            shape(levels, mc_count, dtype=jnp.bfloat16),
+            shape(1, data_count),
+            shape(levels, data_count, dtype=jnp.bfloat16),
+            shape(1, data_count),
+        ),
+        [
+            pltpu.VMEM((1, res_mass.shape[0]), jnp.float32),
+            pltpu.VMEM((1, res_width.shape[0]), jnp.float32),
+            pltpu.VMEM((1, res_wave.shape[0]), jnp.int32),
+            pltpu.VMEM((1, OWN), jnp.int32),
+            pltpu.VMEM((2, OWN), jnp.float32),
+            pltpu.SemaphoreType.DMA((5,)),
+            pltpu.SemaphoreType.DMA((5,)),
+        ],
+        res_mass[None], res_width[None], res_wave[None], wave_q[None], couplings,
+        mc_mass[None], mc_basis, data_mass[None], data_basis, data_weight[None], places,
+        smem=(10,),
+        hbm=range(10),
     )
     table = lax.all_to_all(own_table, "wrow", 0, 0)
-    tile = call(
+    tile, wide, chooser = call(
         functools.partial(gram_kernel, 1.0 / (mc_count * events)),
-        shape(OWN, rows, LANES, dtype=jnp.bfloat16),
-        table_scratch(waves, levels)
-        + [
+        (
+            shape(OWN, rows, LANES, dtype=jnp.bfloat16),
+            shape(PARAMS, waves, LANES),
+            shape(waves, levels, dtype=jnp.bfloat16),
+        ),
+        [
             pltpu.VMEM((2 * waves, TILE), jnp.bfloat16),
             pltpu.VMEM((2 * waves, LANES), jnp.float32),
             pltpu.VMEM((OWN, rows, LANES), jnp.float32),
         ],
-        table, mc_mass[None], mc_basis, places,
+        table, mc_mass, mc_basis, places,
         smem=(3,),
     )
     pieces = lax.all_to_all(tile, EVENT, 0, 0)
-    weight = data_weight[None]
     inverse_count = 1.0 / (data_count * events)
     amp_shape = pltpu.VMEM((2 * waves, data_count), jnp.bfloat16)
     terms, coupling, amp, gram_row = call(
         functools.partial(first_kernel, inverse_count),
         (shape(zx, 2, LANES), shape(rows, LANES), amp_shape, shape(rows, LANES)),
-        table_scratch(waves, levels) + pass_scratch(waves),
-        table, data_mass[None], data_basis, weight, places, pieces,
-        smem=(4,),
+        pass_scratch(waves),
+        table, wide, chooser, data_mass, data_basis, weight, places, pieces,
+        smem=(6,),
     )
 
     def exchange(values):

time: 155 us -> 140 us (0.903)
  local copies, waits for them, and re-layouts: 7.48 us -> 0 us
  Pallas kernels: 36.6 us -> 30.2 us
    unnamed x20 -> x0, local copies, waits for them, and re-layouts: 7.48 us -> none
    pallas_call x9, Pallas kernels: 36.6 us -> 30.2 us  [call(): pl.pallas_call(kernel, out_shape=outs, in_specs=[pl.BlockSpec(memory_spac...]
where the time goes in v3:
time: 140 us
  blocking collectives  109 us (78%)
  Pallas kernels  30.2 us (22%)
    all_to_all x3, blocking collectives, exchange(): lax.all_to_all(values, ZX, 0, 0)  34.9 us
    all_to_all x3, blocking collectives, exchange(): return lax.all_to_all(merged, PEERS, 0, 0)  33.7 us
    pallas_call x9, Pallas kernels, call(): pl.pallas_call(kernel, out_shape=outs, in_specs=[pl.BlockSpec(memory_spac...  30.2 us
    all_to_all x1, blocking collectives, shards(): pieces = lax.all_to_all(tile, EVENT, 0, 0)  26.3 us
    all_to_all x1, blocking collectives, shards(): table = lax.all_to_all(own_table, 'wrow', 0, 0)  14.1 us

profile of v3, /device:TPU:1, one launch (start us, length us, event | category | flops | bytes accessed | tf_op | source)
XLA Modules:
  0.0 139.9 jit_solution(1772955012319216967)
XLA Ops:
  0.6 0.1 pad_add_fusion.place_ref
  0.7 2.0 %shard_map.113 = (f32[8,4,128]{2,1,0:T(4,128)S(1)}, f32[1,3072]{1,0:T(1,128)S(1)}, bf16[64,3072]{1,0:T(8,128)(2,1)S(1)}, f32[1,4096]{1,0:T(1,128)S(1)}, bf16[64,...) custom-call(f32[1,128]{1,0:T(1,128)} %bitcast.13, f32[1,128]{1,0:T(1,128)} %bitcast.14, s32[1,128]{1,0:T(1,128)} %bitcast.15, ...), custom_call_target="tpu_custom_call" | custom-call | tf_op jit(solution)/shard_map/pallas_call | solution.py:337
  2.7 14.1 %all_to_all.40.table_ref = f32[8,4,128]{2,1,0:T(4,128)S(1)} all-to-all(f32[8,4,128]{2,1,0:T(4,128)S(1)} %get-tuple-element.21), channel_id=1, replica_groups=mesh['z'=4,'x'=8,'core'=2,'wrow'=8] {'wrow'}, dimensions={0} | all-to-all | bytes 32768 | tf_op jit(solution)/shard_map/all_to_all | solution.py:389
  16.8 8.6 %shard_map.114 = (bf16[64,8,128]{2,1,0:T(8,128)(2,1)S(1)}, f32[6,512,128]{2,1,0:T(8,128)S(1)}, bf16[512,64]{1,0:T(8,128)(2,1)S(1)}) custom-call(f32[8,4,128]{2,1,0:T(4,128)S(1)} %all_to_all.40.table_ref, f32[1,3072]{1,0:T(1,128)S(1)} %get-tuple-element.22.mass_ref, bf16[64,3072]{1,0:T(8,128)(2,1)S(1)} %get-tuple-element.23.basis_ref, s32[2]{0:T(128)S(1)} %pad_add_fusion.place_ref), custom_call_target="tpu_custom_call" | custom-call | tf_op jit(solution)/shard_map/pallas_call | solution.py:337
  25.4 26.3 %all_to_all.41.pieces_ref = bf16[64,8,128]{2,1,0:T(8,128)(2,1)S(1)} all-to-all(bf16[64,8,128]{2,1,0:T(8,128)(2,1)S(1)} %get-tuple-element.29), channel_id=1, replica_groups=mesh['z'=4,'x'=8,'core'=2,'wrow'=8] {'z','x','core'}, dimensions={0} | all-to-all | bytes 262144 | tf_op jit(solution)/shard_map/all_to_all | solution.py:405
  51.7 9.0 %shard_map.115 = (f32[32,2,128]{2,1,0:T(2,128)S(1)}, f32[8,128]{1,0:T(8,128)S(1)}, bf16[1024,4096]{1,0:T(8,128)(2,1)S(1)}, f32[8,128]{1,0:T(8,128)S(1)}) custom-call(f32[8,4,128]{2,1,0:T(4,128)S(1)} %all_to_all.40.table_ref, f32[6,512,128]{2,1,0:T(8,128)S(1)} %get-tuple-element.24.wide_ref, bf16[512,64]{1,0:T(8,128)(2,1)S(1)} %get-tuple-element.25.chooser_ref, ...), custom_call_target="tpu_custom_call" | custom-call | tf_op jit(solution)/shard_map/pallas_call | solution.py:337
  60.7 11.7 %all_to_all.42.received_ref = f32[32,2,128]{2,1,0:T(2,128)S(1)} all-to-all(f32[32,2,128]{2,1,0:T(2,128)S(1)} %get-tuple-element.30), channel_id=1, replica_groups=mesh['z'=4,'x'=8,'core'=2,'wrow'=8] {'z','x'}, dimensions={0} | all-to-all | bytes 65536 | tf_op jit(solution)/shard_map/all_to_all | solution.py:417
  72.4 11.2 %all_to_all.43.received_ref = f32[16,2,128]{2,1,0:T(2,128)S(1)} all-to-all(f32[16,2,128]{2,1,0:T(2,128)S(1)} %shard_map.116), channel_id=1, replica_groups=mesh['z'=4,'x'=8,'core'=2,'wrow'=8] {'core','wrow'}, dimensions={0} | all-to-all | bytes 32768 | tf_op jit(solution)/shard_map/all_to_all | solution.py:418
  83.6 3.6 %shard_map.117 = (f32[32,2,128]{2,1,0:T(2,128)S(1)}, f32[8,128]{1,0:T(8,128)S(1)}) custom-call(f32[16,2,128]{2,1,0:T(2,128)S(1)} %all_to_all.43.received_ref, f32[8,128]{1,0:T(8,128)S(1)} %get-tuple-element.31.old_ref, bf16[1024,4096]{1,0:T(8,128)(2,1)S(1)} %get-tuple-element.32.amp_ref, f32[1,4096]{1,0:T(1,128)S(1)} %get-tuple-element.28.weight_ref, ...), custom_call_target="tpu_custom_call" | custom-call | tf_op jit(solution)/shard_map/pallas_call | solution.py:337
  87.1 11.6 %all_to_all.44.received_ref = f32[32,2,128]{2,1,0:T(2,128)S(1)} all-to-all(f32[32,2,128]{2,1,0:T(2,128)S(1)} %get-tuple-element.34), channel_id=1, replica_groups=mesh['z'=4,'x'=8,'core'=2,'wrow'=8] {'z','x'}, dimensions={0} | all-to-all | bytes 65536 | tf_op jit(solution)/shard_map/all_to_all | solution.py:417
  98.8 11.3 %all_to_all.45.received_ref = f32[16,2,128]{2,1,0:T(2,128)S(1)} all-to-all(f32[16,2,128]{2,1,0:T(2,128)S(1)} %shard_map.118), channel_id=1, replica_groups=mesh['z'=4,'x'=8,'core'=2,'wrow'=8] {'core','wrow'}, dimensions={0} | all-to-all | bytes 32768 | tf_op jit(solution)/shard_map/all_to_all | solution.py:418
  110.0 3.6 %shard_map.119 = (f32[32,2,128]{2,1,0:T(2,128)S(1)}, f32[8,128]{1,0:T(8,128)S(1)}) custom-call(f32[16,2,128]{2,1,0:T(2,128)S(1)} %all_to_all.45.received_ref, f32[8,128]{1,0:T(8,128)S(1)} %get-tuple-element.35.old_ref, bf16[1024,4096]{1,0:T(8,128)(2,1)S(1)} %get-tuple-element.32.amp_ref, f32[1,4096]{1,0:T(1,128)S(1)} %get-tuple-element.28.weight_ref, ...), custom_call_target="tpu_custom_call" | custom-call | tf_op jit(solution)/shard_map/pallas_call | solution.py:337
  113.6 11.6 %all_to_all.46.received_ref = f32[32,2,128]{2,1,0:T(2,128)S(1)} all-to-all(f32[32,2,128]{2,1,0:T(2,128)S(1)} %get-tuple-element.36), channel_id=1, replica_groups=mesh['z'=4,'x'=8,'core'=2,'wrow'=8] {'z','x'}, dimensions={0} | all-to-all | bytes 65536 | tf_op jit(solution)/shard_map/all_to_all | solution.py:417
  125.2 11.3 %all_to_all.47.received_ref = f32[16,2,128]{2,1,0:T(2,128)S(1)} all-to-all(f32[16,2,128]{2,1,0:T(2,128)S(1)} %shard_map.120), channel_id=1, replica_groups=mesh['z'=4,'x'=8,'core'=2,'wrow'=8] {'core','wrow'}, dimensions={0} | all-to-all | bytes 32768 | tf_op jit(solution)/shard_map/all_to_all | solution.py:418
  136.5 3.4 %shard_map.121 = (f32[2,64]{1,0:T(2,128)}, f32[1,4096]{1,0:T(1,128)}) custom-call(f32[16,2,128]{2,1,0:T(2,128)S(1)} %all_to_all.47.received_ref, f32[8,128]{1,0:T(8,128)S(1)} %get-tuple-element.37.old_ref, bf16[1024,4096]{1,0:T(8,128)(2,1)S(1)} %get-tuple-element.32.amp_ref, s32[2]{0:T(128)S(1)} %pad_add_fusion.place_ref), custom_call_target="tpu_custom_call" | custom-call | tf_op jit(solution)/shard_map/pallas_call | solution.py:337
  (3 shorter events, 0.1 us)

commit v4 on v3

--- a/solution.py
+++ b/solution.py
@@ -17,7 +17,9 @@
 TILE = 512
 CHUNK = 16
 ROWS = 8
-PARAMS = 6
+PARAMS = 4
+NEXT_ROWS = 256
+LAST_ROWS = 256
 VMEM_LIMIT = 24 << 20
 
 
@@ -63,11 +65,11 @@
     second = owner & (index != first_at)
     mass = mass_ref[...]
     square = mass * mass
-    product = mass * width_ref[...]
+    inverse = 1.0 / (mass * width_ref[...])
     columns = [
         jnp.sum(jnp.where(mask, value, 0.0), axis=1, keepdims=True)
         for mask in (first, second)
-        for value in (square, product)
+        for value in (square, inverse)
     ]
     lane = lax.broadcasted_iota(jnp.int32, (OWN, LANES), 1)
     table = jnp.zeros((OWN, LANES), jnp.float32)
@@ -94,11 +96,10 @@
         rows = slice(block * OWN, (block + 1) * OWN)
         for pair in range(2):
             first = 4 * block + 2 * pair
-            square = jnp.broadcast_to(turned[0:OWN, first : first + 1], (OWN, LANES))
-            product = jnp.broadcast_to(turned[0:OWN, first + 1 : first + 2], (OWN, LANES))
-            wide_ref[3 * pair, rows, :] = square
-            wide_ref[3 * pair + 1, rows, :] = product * product
-            wide_ref[3 * pair + 2, rows, :] = product
+            square = turned[0:OWN, first : first + 1]
+            inverse = turned[0:OWN, first + 1 : first + 2]
+            wide_ref[2 * pair, rows, :] = jnp.broadcast_to(square, (OWN, LANES))
+            wide_ref[2 * pair + 1, rows, :] = jnp.broadcast_to(inverse, (OWN, LANES))
         level = turned[OWN : 2 * OWN, 4 * block : 4 * block + 1]
         chooser_ref[rows, :] = (level == column).astype(jnp.bfloat16)
 
@@ -106,11 +107,10 @@
 def lineshapes(mass, wide_ref, rows):
     real = imag = None
     for pair in range(2):
-        product = wide_ref[3 * pair + 2, rows, :]
-        gap = wide_ref[3 * pair, rows, :] - mass
-        quotient = product / (gap * gap + wide_ref[3 * pair + 1, rows, :])
-        real = quotient * gap if real is None else real + quotient * gap
-        imag = quotient * product if imag is None else imag + quotient * product
+        gap = (wide_ref[2 * pair, rows, :] - mass) * wide_ref[2 * pair + 1, rows, :]
+        share = 1.0 / (gap * gap + 1.0)
+        real = gap * share if real is None else real + gap * share
+        imag = share if imag is None else imag + share
     return real, imag
 
 
@@ -178,11 +178,43 @@
     return signed, swapped
 
 
-def field_of(parts, amp_tile):
-    sums = jnp.dot(parts, amp_tile, preferred_element_type=jnp.float32)
+def load_columns(signed, swapped, vector_rows, column_ref):
+    blocks = vector_rows // LANES
+    first = signed.shape[0] - blocks
+    rows = [signed[first:], swapped[first:], jnp.zeros((LANES - 2 * blocks, LANES), jnp.float32)]
+    turned = jnp.concatenate(rows, axis=0).T
+    for place in range(2):
+        for block in range(blocks):
+            column = turned[:, place * blocks + block : place * blocks + block + 1]
+            column_ref[place, block * LANES : (block + 1) * LANES, :] = jnp.broadcast_to(column, (LANES, LANES))
+
+
+def field_of(parts, amp_ref, columns, column_ref=None):
+    waves = amp_ref.shape[0]
+    vector_rows = 0 if column_ref is None else column_ref.shape[1]
+    matrix_rows = waves - vector_rows
+    sums = jnp.dot(parts[:, :matrix_rows], amp_ref[:matrix_rows, columns], preferred_element_type=jnp.float32)
     real = (sums[4:5] + sums[2:3]) + sums[0:1]
     imag = (sums[5:6] + sums[3:4]) + sums[1:2]
+    if vector_rows:
+        lanes = TILE // LANES
+        reals = [jnp.zeros((ROWS, LANES), jnp.float32) for _ in range(lanes)]
+        imags = [jnp.zeros((ROWS, LANES), jnp.float32) for _ in range(lanes)]
+        for start in range(0, vector_rows, ROWS):
+            rows = slice(start, start + ROWS)
+            values = amp_ref[matrix_rows + start : matrix_rows + start + ROWS, columns].astype(jnp.float32)
+            by_real, by_imag = column_ref[0, rows, :], column_ref[1, rows, :]
+            for place in range(lanes):
+                value = values[:, place * LANES : (place + 1) * LANES]
+                reals[place] = reals[place] + value * by_real
+                imags[place] = imags[place] + value * by_imag
+        real = real + jnp.sum(jnp.concatenate(reals, axis=1), axis=0, keepdims=True)
+        imag = imag + jnp.sum(jnp.concatenate(imags, axis=1), axis=0, keepdims=True)
     return real, imag
+
+
+def tile_at(step):
+    return pl.ds(pl.multiple_of(step * TILE, TILE), TILE)
 
 
 def project_tile(real, imag, weight, own_tile, by_real_ref, by_imag_ref, curve_ref):
@@ -273,7 +305,7 @@
             amp_ref[row + OWN : row + OWN + ROWS, columns] = imag
 
         fill_tile(mass_ref[:, columns], basis_ref[:, columns], wide_ref, chooser_ref, store)
-        real, imag = field_of(parts, amp_ref[:, columns])
+        real, imag = field_of(parts, amp_ref, columns)
         own = amp_ref[own_rows(place_ref), columns]
         project_tile(real, imag, weight_ref[:, columns], own, by_real_ref, by_imag_ref, curve_ref)
 
@@ -293,39 +325,47 @@
 
 def next_kernel(
     scale, received_ref, old_ref, amp_ref, weight_ref, place_ref, gram_ref, out_ref, coupling_ref,
-    parts_ref, by_real_ref, by_imag_ref, curve_ref
+    parts_ref, by_real_ref, by_imag_ref, curve_ref, column_ref
 ):
     coupling = new_coupling(received_ref, old_ref)
     coupling_ref[...] = coupling
     signed, swapped = load_coupling(coupling, parts_ref)
+    load_columns(signed, swapped, column_ref.shape[1], column_ref)
     parts = parts_ref[...].astype(jnp.bfloat16)
     clear(by_real_ref, by_imag_ref, curve_ref)
-
-    @pl.loop(0, amp_ref.shape[1] // (TILE))
-    def _(step):
-        columns = pl.ds(pl.multiple_of(step * TILE, TILE), TILE)
-        real, imag = field_of(parts, amp_ref[:, columns])
-        own = amp_ref[own_rows(place_ref), columns]
-        project_tile(real, imag, weight_ref[:, columns], own, by_real_ref, by_imag_ref, curve_ref)
-
+    tiles = amp_ref.shape[1] // TILE
+
+    def project(step, field):
+        own = amp_ref[own_rows(place_ref), tile_at(step)]
+        project_tile(*field, weight_ref[:, tile_at(step)], own, by_real_ref, by_imag_ref, curve_ref)
+
+    def ahead(step, field):
+        later = field_of(parts, amp_ref, tile_at(step + 1), column_ref)
+        project(step, field)
+        return later
+
+    field = lax.fori_loop(0, tiles - 1, ahead, field_of(parts, amp_ref, tile_at(0), column_ref))
+    project(tiles - 1, field)
     terms = gradient_rows(scale, by_real_ref, by_imag_ref, curve_ref)
     send_terms(terms + gram_rows(gram_ref[...], signed, swapped, place_ref), out_ref)
 
 
-def last_kernel(received_ref, old_ref, amp_ref, place_ref, coupling_out_ref, intensity_ref, parts_ref, coupling_ref):
+def last_kernel(
+    received_ref, old_ref, amp_ref, place_ref, coupling_out_ref, intensity_ref, parts_ref, coupling_ref, column_ref
+):
     coupling = new_coupling(received_ref, old_ref)
     coupling_ref[...] = coupling
-    load_coupling(coupling, parts_ref)
+    signed, swapped = load_coupling(coupling, parts_ref)
+    load_columns(signed, swapped, column_ref.shape[1], column_ref)
     parts = parts_ref[...].astype(jnp.bfloat16)
     mine = coupling_ref[pl.ds(place_ref[0], 1), :]
     coupling_out_ref[0:1, :] = mine[:, 0:OWN]
     coupling_out_ref[1:2, :] = pltpu.roll(mine, OWN, 1)[:, 0:OWN]
 
-    @pl.loop(0, amp_ref.shape[1] // (TILE))
+    @pl.loop(0, amp_ref.shape[1] // TILE)
     def _(step):
-        columns = pl.ds(pl.multiple_of(step * TILE, TILE), TILE)
-        real, imag = field_of(parts, amp_ref[:, columns])
-        intensity_ref[:, columns] = real * real + imag * imag + BACKGROUND
+        real, imag = field_of(parts, amp_ref, tile_at(step), column_ref)
+        intensity_ref[:, tile_at(step)] = real * real + imag * imag + BACKGROUND
 
 
 def call(kernel, outs, scratch, *args, smem, hbm=()):
@@ -422,7 +462,7 @@
         terms, coupling = call(
             functools.partial(next_kernel, inverse_count),
             (shape(zx, 2, LANES), shape(rows, LANES)),
-            pass_scratch(waves),
+            pass_scratch(waves) + [pltpu.VMEM((2, NEXT_ROWS, LANES), jnp.float32)],
             received, coupling, amp, weight, places, gram_row,
             smem=(4,),
         )
@@ -430,7 +470,11 @@
     coupling_out, intensity = call(
         last_kernel,
         (shape(2, OWN), shape(1, data_count)),
-        [pltpu.VMEM((8, 2 * waves), jnp.float32), pltpu.VMEM((rows, LANES), jnp.float32)],
+        [
+            pltpu.VMEM((8, 2 * waves), jnp.float32),
+            pltpu.VMEM((rows, LANES), jnp.float32),
+            pltpu.VMEM((2, LAST_ROWS, LANES), jnp.float32),
+        ],
         received, coupling, amp, places,
         smem=(3,),
     )

time: 140 us -> 139 us (level)
  Pallas kernels: 30.2 us -> 28.5 us
    pallas_call x9, Pallas kernels: 30.2 us -> 28.5 us  [call(): pl.pallas_call(kernel, out_shape=outs, in_specs=[pl.BlockSpec(memory_spac...]
where the time goes in v4:
time: 139 us; the launch traced here: 138 us
  blocking collectives  109 us (78%)
  Pallas kernels  28.5 us (21%)
    all_to_all x3, blocking collectives, exchange(): lax.all_to_all(values, ZX, 0, 0)  34.8 us
    all_to_all x3, blocking collectives, exchange(): return lax.all_to_all(merged, PEERS, 0, 0)  33.8 us
    pallas_call x9, Pallas kernels, call(): pl.pallas_call(kernel, out_shape=outs, in_specs=[pl.BlockSpec(memory_spac...  28.5 us
    all_to_all x1, blocking collectives, shards(): pieces = lax.all_to_all(tile, EVENT, 0, 0)  26.3 us
    all_to_all x1, blocking collectives, shards(): table = lax.all_to_all(own_table, 'wrow', 0, 0)  14.1 us

profile of v4, /device:TPU:1, one launch (start us, length us, event | category | flops | bytes accessed | tf_op | source)
XLA Modules:
  0.0 138.3 jit_solution(4477978467387728315)
XLA Ops:
  0.6 0.1 pad_add_fusion.place_ref
  0.7 2.0 %shard_map.113 = (f32[8,4,128]{2,1,0:T(4,128)S(1)}, f32[1,3072]{1,0:T(1,128)S(1)}, bf16[64,3072]{1,0:T(8,128)(2,1)S(1)}, f32[1,4096]{1,0:T(1,128)S(1)}, bf16[64,...) custom-call(f32[1,128]{1,0:T(1,128)} %bitcast.13, f32[1,128]{1,0:T(1,128)} %bitcast.14, s32[1,128]{1,0:T(1,128)} %bitcast.15, ...), custom_call_target="tpu_custom_call" | custom-call | tf_op jit(solution)/shard_map/pallas_call | solution.py:377
  2.7 14.1 %all_to_all.40.table_ref = f32[8,4,128]{2,1,0:T(4,128)S(1)} all-to-all(f32[8,4,128]{2,1,0:T(4,128)S(1)} %get-tuple-element.21), channel_id=1, replica_groups=mesh['z'=4,'x'=8,'core'=2,'wrow'=8] {'wrow'}, dimensions={0} | all-to-all | bytes 32768 | tf_op jit(solution)/shard_map/all_to_all | solution.py:429
  16.8 8.2 %shard_map.114 = (bf16[64,8,128]{2,1,0:T(8,128)(2,1)S(1)}, f32[4,512,128]{2,1,0:T(8,128)S(1)}, bf16[512,64]{1,0:T(8,128)(2,1)S(1)}) custom-call(f32[8,4,128]{2,1,0:T(4,128)S(1)} %all_to_all.40.table_ref, f32[1,3072]{1,0:T(1,128)S(1)} %get-tuple-element.22.mass_ref, bf16[64,3072]{1,0:T(8,128)(2,1)S(1)} %get-tuple-element.23.basis_ref, s32[2]{0:T(128)S(1)} %pad_add_fusion.place_ref), custom_call_target="tpu_custom_call" | custom-call | tf_op jit(solution)/shard_map/pallas_call | solution.py:377
  25.0 26.3 %all_to_all.41.pieces_ref = bf16[64,8,128]{2,1,0:T(8,128)(2,1)S(1)} all-to-all(bf16[64,8,128]{2,1,0:T(8,128)(2,1)S(1)} %get-tuple-element.29), channel_id=1, replica_groups=mesh['z'=4,'x'=8,'core'=2,'wrow'=8] {'z','x','core'}, dimensions={0} | all-to-all | bytes 262144 | tf_op jit(solution)/shard_map/all_to_all | solution.py:445
  51.3 8.2 %shard_map.115 = (f32[32,2,128]{2,1,0:T(2,128)S(1)}, f32[8,128]{1,0:T(8,128)S(1)}, bf16[1024,4096]{1,0:T(8,128)(2,1)S(1)}, f32[8,128]{1,0:T(8,128)S(1)}) custom-call(f32[8,4,128]{2,1,0:T(4,128)S(1)} %all_to_all.40.table_ref, f32[4,512,128]{2,1,0:T(8,128)S(1)} %get-tuple-element.24.wide_ref, bf16[512,64]{1,0:T(8,128)(2,1)S(1)} %get-tuple-element.25.chooser_ref, ...), custom_call_target="tpu_custom_call" | custom-call | tf_op jit(solution)/shard_map/pallas_call | solution.py:377
  59.5 11.6 %all_to_all.42.received_ref = f32[32,2,128]{2,1,0:T(2,128)S(1)} all-to-all(f32[32,2,128]{2,1,0:T(2,128)S(1)} %get-tuple-element.30), channel_id=1, replica_groups=mesh['z'=4,'x'=8,'core'=2,'wrow'=8] {'z','x'}, dimensions={0} | all-to-all | bytes 65536 | tf_op jit(solution)/shard_map/all_to_all | solution.py:457
  71.2 11.3 %all_to_all.43.received_ref = f32[16,2,128]{2,1,0:T(2,128)S(1)} all-to-all(f32[16,2,128]{2,1,0:T(2,128)S(1)} %shard_map.116), channel_id=1, replica_groups=mesh['z'=4,'x'=8,'core'=2,'wrow'=8] {'core','wrow'}, dimensions={0} | all-to-all | bytes 32768 | tf_op jit(solution)/shard_map/all_to_all | solution.py:458
  82.5 3.3 %shard_map.117 = (f32[32,2,128]{2,1,0:T(2,128)S(1)}, f32[8,128]{1,0:T(8,128)S(1)}) custom-call(f32[16,2,128]{2,1,0:T(2,128)S(1)} %all_to_all.43.received_ref, f32[8,128]{1,0:T(8,128)S(1)} %get-tuple-element.31.old_ref, bf16[1024,4096]{1,0:T(8,128)(2,1)S(1)} %get-tuple-element.32.amp_ref, f32[1,4096]{1,0:T(1,128)S(1)} %get-tuple-element.28.weight_ref, ...), custom_call_target="tpu_custom_call" | custom-call | tf_op jit(solution)/shard_map/pallas_call | solution.py:377
  85.8 11.6 %all_to_all.44.received_ref = f32[32,2,128]{2,1,0:T(2,128)S(1)} all-to-all(f32[32,2,128]{2,1,0:T(2,128)S(1)} %get-tuple-element.34), channel_id=1, replica_groups=mesh['z'=4,'x'=8,'core'=2,'wrow'=8] {'z','x'}, dimensions={0} | all-to-all | bytes 65536 | tf_op jit(solution)/shard_map/all_to_all | solution.py:457
  97.4 11.3 %all_to_all.45.received_ref = f32[16,2,128]{2,1,0:T(2,128)S(1)} all-to-all(f32[16,2,128]{2,1,0:T(2,128)S(1)} %shard_map.118), channel_id=1, replica_groups=mesh['z'=4,'x'=8,'core'=2,'wrow'=8] {'core','wrow'}, dimensions={0} | all-to-all | bytes 32768 | tf_op jit(solution)/shard_map/all_to_all | solution.py:458
  108.7 3.3 %shard_map.119 = (f32[32,2,128]{2,1,0:T(2,128)S(1)}, f32[8,128]{1,0:T(8,128)S(1)}) custom-call(f32[16,2,128]{2,1,0:T(2,128)S(1)} %all_to_all.45.received_ref, f32[8,128]{1,0:T(8,128)S(1)} %get-tuple-element.35.old_ref, bf16[1024,4096]{1,0:T(8,128)(2,1)S(1)} %get-tuple-element.32.amp_ref, f32[1,4096]{1,0:T(1,128)S(1)} %get-tuple-element.28.weight_ref, ...), custom_call_target="tpu_custom_call" | custom-call | tf_op jit(solution)/shard_map/pallas_call | solution.py:377
  112.0 11.6 %all_to_all.46.received_ref = f32[32,2,128]{2,1,0:T(2,128)S(1)} all-to-all(f32[32,2,128]{2,1,0:T(2,128)S(1)} %get-tuple-element.36), channel_id=1, replica_groups=mesh['z'=4,'x'=8,'core'=2,'wrow'=8] {'z','x'}, dimensions={0} | all-to-all | bytes 65536 | tf_op jit(solution)/shard_map/all_to_all | solution.py:457
  123.6 11.3 %all_to_all.47.received_ref = f32[16,2,128]{2,1,0:T(2,128)S(1)} all-to-all(f32[16,2,128]{2,1,0:T(2,128)S(1)} %shard_map.120), channel_id=1, replica_groups=mesh['z'=4,'x'=8,'core'=2,'wrow'=8] {'core','wrow'}, dimensions={0} | all-to-all | bytes 32768 | tf_op jit(solution)/shard_map/all_to_all | solution.py:458
  134.9 3.4 %shard_map.121 = (f32[2,64]{1,0:T(2,128)}, f32[1,4096]{1,0:T(1,128)}) custom-call(f32[16,2,128]{2,1,0:T(2,128)S(1)} %all_to_all.47.received_ref, f32[8,128]{1,0:T(8,128)S(1)} %get-tuple-element.37.old_ref, bf16[1024,4096]{1,0:T(8,128)(2,1)S(1)} %get-tuple-element.32.amp_ref, s32[2]{0:T(128)S(1)} %pad_add_fusion.place_ref), custom_call_target="tpu_custom_call" | custom-call | tf_op jit(solution)/shard_map/pallas_call | solution.py:377
  (3 shorter events, 0.1 us)

commit v5 on v4

--- a/solution.py
+++ b/solution.py
@@ -23,38 +23,25 @@
 VMEM_LIMIT = 24 << 20
 
 
+def copies(pairs, sems):
+    started = [pltpu.make_async_copy(source, target, sems.at[place]) for place, (source, target) in enumerate(pairs)]
+    for copy in started:
+        copy.start()
+    return started
+
+
 def prepare_kernel(
-    mass_in, width_in, wave_in, level_in, coupling_in, mc_mass_in, mc_basis_in, data_mass_in, data_basis_in,
-    weight_in, place_ref, out_ref, mc_mass_out, mc_basis_out, data_mass_out, data_basis_out, weight_out,
-    mass_ref, width_ref, wave_ref, level_ref, coupling_ref, small_sems, large_sems
+    mass_in, width_in, wave_in, level_in, coupling_in, place_ref, out_ref,
+    mass_ref, width_ref, wave_ref, level_ref, coupling_ref, sems
 ):
-    small = [
-        pltpu.make_async_copy(source, target, small_sems.at[place])
-        for place, (source, target) in enumerate(
-            (
-                (mass_in, mass_ref),
-                (width_in, width_ref),
-                (wave_in, wave_ref),
-                (level_in, level_ref),
-                (coupling_in, coupling_ref),
-            )
-        )
-    ]
-    large = [
-        pltpu.make_async_copy(source, target, large_sems.at[place])
-        for place, (source, target) in enumerate(
-            (
-                (mc_mass_in, mc_mass_out),
-                (mc_basis_in, mc_basis_out),
-                (data_mass_in, data_mass_out),
-                (data_basis_in, data_basis_out),
-                (weight_in, weight_out),
-            )
-        )
-    ]
-    for copy in small + large:
-        copy.start()
-    for copy in small:
+    pairs = (
+        (mass_in, mass_ref),
+        (width_in, width_ref),
+        (wave_in, wave_ref),
+        (level_in, level_ref),
+        (coupling_in, coupling_ref),
+    )
+    for copy in copies(pairs, sems):
         copy.wait()
     count = mass_ref.shape[1]
     local = wave_ref[...] - place_ref[0] * OWN
@@ -81,8 +68,6 @@
     )
     rows = jnp.concatenate([turned[0:4, 0:OWN], rest], axis=1)
     send_terms(rows, out_ref)
-    for copy in large:
-        copy.wait()
 
 
 def load_table(table_ref, wide_ref, chooser_ref):
@@ -134,7 +119,15 @@
             store(2 * start + inner, real, imag)
 
 
-def gram_kernel(scale, table_ref, mass_ref, basis_ref, place_ref, out_ref, wide_ref, chooser_ref, amp_ref, sum_ref, turn_ref):
+def gram_kernel(
+    scale, table_ref, mass_in, basis_in, data_mass_in, data_basis_in, weight_in, place_ref,
+    out_ref, wide_ref, chooser_ref, data_mass_ref, data_basis_ref, weight_ref,
+    mass_ref, basis_ref, amp_ref, sum_ref, turn_ref, sems, data_sems
+):
+    now = copies(((mass_in, mass_ref), (basis_in, basis_ref)), sems)
+    later = copies(
+        ((data_mass_in, data_mass_ref), (data_basis_in, data_basis_ref), (weight_in, weight_ref)), data_sems
+    )
     load_table(table_ref, wide_ref, chooser_ref)
     sum_ref[...] = jnp.zeros_like(sum_ref)
     blocks = table_ref.shape[0]
@@ -142,6 +135,9 @@
     def store(row, real, imag):
         amp_ref[row : row + ROWS, :] = real
         amp_ref[row + OWN : row + OWN + ROWS, :] = imag
+
+    for copy in now:
+        copy.wait()
 
     @pl.loop(0, mass_ref.shape[1] // TILE)
     def _(step):
@@ -160,6 +156,8 @@
         turned = (jnp.concatenate([gram_real, gram_imag], axis=0) * scale).T
         turn_ref[:, block, :] = turned[0:OWN, :]
     out_ref[...] = turn_ref[...].astype(jnp.bfloat16)
+    for copy in later:
+        copy.wait()
 
 
 def load_coupling(coupling, parts_ref):
@@ -214,6 +212,8 @@
 
 
 def tile_at(step):
+    if isinstance(step, int):
+        return pl.ds(step * TILE, TILE)
     return pl.ds(pl.multiple_of(step * TILE, TILE), TILE)
 
 
@@ -286,13 +286,13 @@
 
 
 def first_kernel(
-    scale, table_ref, wide_ref, chooser_ref, mass_ref, basis_ref, weight_ref, place_ref, pieces_ref,
-    out_ref, coupling_ref, amp_ref, gram_ref, parts_ref, by_real_ref, by_imag_ref, curve_ref
+    scale, table_ref, wide_ref, chooser_ref, mass_ref, basis_ref, weight_ref, place_ref,
+    out_ref, coupling_ref, amp_out, amp_ref, parts_ref, by_real_ref, by_imag_ref, curve_ref, sems
 ):
     for block in range(table_ref.shape[0]):
         half = table_ref[block]
         coupling_ref[block : block + 1, :] = jnp.concatenate([half[1:2, OWN:LANES], half[2:3, OWN:LANES]], axis=1)
-    signed, swapped = load_coupling(coupling_ref[...], parts_ref)
+    load_coupling(coupling_ref[...], parts_ref)
     parts = parts_ref[...].astype(jnp.bfloat16)
     clear(by_real_ref, by_imag_ref, curve_ref)
 
@@ -308,11 +308,18 @@
         real, imag = field_of(parts, amp_ref, columns)
         own = amp_ref[own_rows(place_ref), columns]
         project_tile(real, imag, weight_ref[:, columns], own, by_real_ref, by_imag_ref, curve_ref)
-
+        pltpu.make_async_copy(amp_ref.at[:, columns], amp_out.at[:, columns], sems.at[step]).start()
+
+    out_ref[...] = gradient_rows(scale, by_real_ref, by_imag_ref, curve_ref)
+    for step in range(amp_ref.shape[1] // TILE):
+        columns = pl.ds(step * TILE, TILE)
+        pltpu.make_async_copy(amp_ref.at[:, columns], amp_out.at[:, columns], sems.at[step]).wait()
+
+
+def add_kernel(pieces_ref, base_ref, coupling_ref, place_ref, out_ref, gram_ref):
     gram = jnp.sum(pieces_ref[...].astype(jnp.float32), axis=0)
     gram_ref[...] = gram
-    terms = gradient_rows(scale, by_real_ref, by_imag_ref, curve_ref)
-    send_terms(terms + gram_rows(gram, signed, swapped, place_ref), out_ref)
+    send_terms(base_ref[...] + gram_rows(gram, *signs(coupling_ref[...]), place_ref), out_ref)
 
 
 def new_coupling(received_ref, coupling_ref):
@@ -323,8 +330,8 @@
     return coupling_ref[...] - grad / (curve + pltpu.roll(curve, OWN, 1))
 
 
-def next_kernel(
-    scale, received_ref, old_ref, amp_ref, weight_ref, place_ref, gram_ref, out_ref, coupling_ref,
+def next_pass(
+    scale, received_ref, old_ref, amp_ref, arrive, weight_ref, place_ref, gram_ref, out_ref, coupling_ref,
     parts_ref, by_real_ref, by_imag_ref, curve_ref, column_ref
 ):
     coupling = new_coupling(received_ref, old_ref)
@@ -340,14 +347,36 @@
         project_tile(*field, weight_ref[:, tile_at(step)], own, by_real_ref, by_imag_ref, curve_ref)
 
     def ahead(step, field):
+        arrive(step + 1)
         later = field_of(parts, amp_ref, tile_at(step + 1), column_ref)
         project(step, field)
         return later
 
+    arrive(0)
     field = lax.fori_loop(0, tiles - 1, ahead, field_of(parts, amp_ref, tile_at(0), column_ref))
     project(tiles - 1, field)
     terms = gradient_rows(scale, by_real_ref, by_imag_ref, curve_ref)
     send_terms(terms + gram_rows(gram_ref[...], signed, swapped, place_ref), out_ref)
+
+
+def second_kernel(scale, received_ref, old_ref, amp_in, weight_ref, place_ref, gram_ref, out_ref, coupling_ref, amp_ref, *scratch):
+    sems = scratch[-1]
+
+    def copy(step):
+        return pltpu.make_async_copy(amp_in.at[:, tile_at(step)], amp_ref.at[:, tile_at(step)], sems.at[step])
+
+    for step in range(amp_ref.shape[1] // TILE):
+        copy(step).start()
+    next_pass(
+        scale, received_ref, old_ref, amp_ref, lambda step: copy(step).wait(), weight_ref, place_ref, gram_ref,
+        out_ref, coupling_ref, *scratch[:-1]
+    )
+
+
+def next_kernel(scale, received_ref, old_ref, amp_ref, weight_ref, place_ref, gram_ref, *rest):
+    next_pass(
+        scale, received_ref, old_ref, amp_ref, lambda step: None, weight_ref, place_ref, gram_ref, *rest
+    )
 
 
 def last_kernel(
@@ -368,7 +397,7 @@
         intensity_ref[:, tile_at(step)] = real * real + imag * imag + BACKGROUND
 
 
-def call(kernel, outs, scratch, *args, smem, hbm=()):
+def call(kernel, outs, scratch, *args, smem, hbm=(), hbm_out=(), cost=None):
     def space(place):
         return pltpu.SMEM if place in smem else pltpu.HBM if place in hbm else pltpu.VMEM
 
@@ -378,7 +407,10 @@
         kernel,
         out_shape=outs,
         in_specs=[pl.BlockSpec(memory_space=space(place)) for place in range(len(args))],
-        out_specs=whole if single else tuple(whole for _ in outs),
+        out_specs=whole
+        if single
+        else tuple(pl.BlockSpec(memory_space=pltpu.HBM) if place in hbm_out else whole for place in range(len(outs))),
+        cost_estimate=cost,
         scratch_shapes=scratch,
         compiler_params=pltpu.CompilerParams(vmem_limit_bytes=VMEM_LIMIT),
     )(*(pltpu.with_memory_space_constraint(arg, pltpu.HBM) if place in hbm else arg for place, arg in enumerate(args)))
@@ -402,16 +434,9 @@
     levels = mc_basis.shape[0]
     mc_count, data_count = mc_mass.shape[0], data_mass.shape[0]
     places = jnp.stack([lax.axis_index("wrow"), lax.axis_index(EVENT)]).astype(jnp.int32)
-    own_table, mc_mass, mc_basis, data_mass, data_basis, weight = call(
+    own_table = call(
         prepare_kernel,
-        (
-            shape(rows, 4, LANES),
-            shape(1, mc_count),
-            shape(levels, mc_count, dtype=jnp.bfloat16),
-            shape(1, data_count),
-            shape(levels, data_count, dtype=jnp.bfloat16),
-            shape(1, data_count),
-        ),
+        shape(rows, 4, LANES),
         [
             pltpu.VMEM((1, res_mass.shape[0]), jnp.float32),
             pltpu.VMEM((1, res_width.shape[0]), jnp.float32),
@@ -419,53 +444,78 @@
             pltpu.VMEM((1, OWN), jnp.int32),
             pltpu.VMEM((2, OWN), jnp.float32),
             pltpu.SemaphoreType.DMA((5,)),
-            pltpu.SemaphoreType.DMA((5,)),
         ],
-        res_mass[None], res_width[None], res_wave[None], wave_q[None], couplings,
-        mc_mass[None], mc_basis, data_mass[None], data_basis, data_weight[None], places,
-        smem=(10,),
-        hbm=range(10),
+        res_mass[None], res_width[None], res_wave[None], wave_q[None], couplings, places,
+        smem=(5,),
+        hbm=range(5),
     )
     table = lax.all_to_all(own_table, "wrow", 0, 0)
-    tile, wide, chooser = call(
+    tile, wide, chooser, data_mass, data_basis, weight = call(
         functools.partial(gram_kernel, 1.0 / (mc_count * events)),
         (
             shape(OWN, rows, LANES, dtype=jnp.bfloat16),
             shape(PARAMS, waves, LANES),
             shape(waves, levels, dtype=jnp.bfloat16),
+            shape(1, data_count),
+            shape(levels, data_count, dtype=jnp.bfloat16),
+            shape(1, data_count),
         ),
         [
+            pltpu.VMEM((1, mc_count), jnp.float32),
+            pltpu.VMEM((levels, mc_count), jnp.bfloat16),
             pltpu.VMEM((2 * waves, TILE), jnp.bfloat16),
             pltpu.VMEM((2 * waves, LANES), jnp.float32),
             pltpu.VMEM((OWN, rows, LANES), jnp.float32),
+            pltpu.SemaphoreType.DMA((2,)),
+            pltpu.SemaphoreType.DMA((3,)),
         ],
-        table, mc_mass, mc_basis, places,
-        smem=(3,),
+        table, mc_mass[None], mc_basis, data_mass[None], data_basis, data_weight[None], places,
+        smem=(6,),
+        hbm=range(1, 6),
     )
     pieces = lax.all_to_all(tile, EVENT, 0, 0)
     inverse_count = 1.0 / (data_count * events)
-    amp_shape = pltpu.VMEM((2 * waves, data_count), jnp.bfloat16)
-    terms, coupling, amp, gram_row = call(
+    tile_sems = pltpu.SemaphoreType.DMA((data_count // TILE,))
+    amp_shape = (2 * waves, data_count)
+    base, coupling, amp = call(
         functools.partial(first_kernel, inverse_count),
-        (shape(zx, 2, LANES), shape(rows, LANES), amp_shape, shape(rows, LANES)),
-        pass_scratch(waves),
-        table, wide, chooser, data_mass, data_basis, weight, places, pieces,
+        (shape(2, LANES), shape(rows, LANES), pltpu.HBM(amp_shape, jnp.bfloat16)),
+        [pltpu.VMEM(amp_shape, jnp.bfloat16)] + pass_scratch(waves) + [tile_sems],
+        table, wide, chooser, data_mass, data_basis, weight, places,
         smem=(6,),
+        hbm_out=(2,),
+        cost=pl.CostEstimate(
+            flops=40 * waves * data_count, bytes_accessed=8 * waves * data_count, transcendentals=waves * data_count
+        ),
+    )
+    terms, gram_row = call(
+        add_kernel, (shape(zx, 2, LANES), shape(rows, LANES)), [], pieces, base, coupling, places, smem=(3,)
     )
 
     def exchange(values):
         merged = call(merge_kernel, shape(2 * rows, 2, LANES), [], lax.all_to_all(values, ZX, 0, 0), smem=())
         return lax.all_to_all(merged, PEERS, 0, 0)
 
-    for _ in range(1, ITERS):
+    column_scratch = [pltpu.VMEM((2, NEXT_ROWS, LANES), jnp.float32)]
+    for step in range(1, ITERS):
         received = exchange(terms)
-        terms, coupling = call(
-            functools.partial(next_kernel, inverse_count),
-            (shape(zx, 2, LANES), shape(rows, LANES)),
-            pass_scratch(waves) + [pltpu.VMEM((2, NEXT_ROWS, LANES), jnp.float32)],
-            received, coupling, amp, weight, places, gram_row,
-            smem=(4,),
-        )
+        if step == 1:
+            terms, coupling, amp = call(
+                functools.partial(second_kernel, inverse_count),
+                (shape(zx, 2, LANES), shape(rows, LANES), shape(*amp_shape, dtype=jnp.bfloat16)),
+                pass_scratch(waves) + column_scratch + [tile_sems],
+                received, coupling, amp, weight, places, gram_row,
+                smem=(4,),
+                hbm=(2,),
+            )
+        else:
+            terms, coupling = call(
+                functools.partial(next_kernel, inverse_count),
+                (shape(zx, 2, LANES), shape(rows, LANES)),
+                pass_scratch(waves) + column_scratch,
+                received, coupling, amp, weight, places, gram_row,
+                smem=(4,),
+            )
     received = exchange(terms)
     coupling_out, intensity = call(
         last_kernel,

time: 139 us -> 138 us (level)
  blocking collectives: 109 us -> 86.7 us
  starting transfers between devices: 0 us -> 15.5 us
  Pallas kernels: 28.5 us -> 32 us
  waiting for transfers between devices: 0 us -> 2.23 us
    all_to_all x1 -> x0, blocking collectives: 26.3 us -> none  [shards(): pieces = lax.all_to_all(tile, EVENT, 0, 0)]
    all_to_all x0 -> x1, starting transfers between devices: none -> 15.5 us  [shards(): pieces = lax.all_to_all(tile, EVENT, 0, 0)]
    all_to_all x3, blocking collectives: 34.8 us -> 39 us  [exchange(): lax.all_to_all(values, ZX, 0, 0)]
    pallas_call x9 -> x10, Pallas kernels: 28.5 us -> 32 us  [call(): pl.pallas_call(kernel, out_shape=outs, in_specs=[pl.BlockSpec(memory_spac...]
    all_to_all x0 -> x1, waiting for transfers between devices: none -> 2.23 us  [shards(): pieces = lax.all_to_all(tile, EVENT, 0, 0)]
  transfers between devices with their start and end apart: 0 -> 1, of which waited for: 0 -> 1; matrix products, arithmetic and copies ran while one was open for 0% -> 0% of each run, Pallas kernels for 0% -> 6%
where the time goes in v5:
time: 138 us; the launch traced here: 137 us
  blocking collectives  86.7 us (63%)
  Pallas kernels  32 us (23%)
  starting transfers between devices  15.5 us (11%)
  waiting for transfers between devices  2.23 us (2%)
    all_to_all x3, blocking collectives, exchange(): lax.all_to_all(values, ZX, 0, 0)  39 us
    all_to_all x3, blocking collectives, exchange(): return lax.all_to_all(merged, PEERS, 0, 0)  33.7 us
    pallas_call x10, Pallas kernels, call(): pl.pallas_call(kernel, out_shape=outs, in_specs=[pl.BlockSpec(memory_spac...  32 us
    all_to_all x1, starting transfers between devices, shards(): pieces = lax.all_to_all(tile, EVENT, 0, 0)  15.5 us
    all_to_all x1, blocking collectives, shards(): table = lax.all_to_all(own_table, 'wrow', 0, 0)  14.1 us
  transfers between devices with their start and end apart: 1, of which 1 were waited for; matrix products, arithmetic and copies ran while one was open for 0% of the time, Pallas kernels for 6%

profile of v5, /device:TPU:1, one launch (start us, length us, event | category | flops | bytes accessed | tf_op | source)
XLA Modules:
  0.0 137.2 jit_solution(14338128311794230051)
XLA Ops:
  0.6 0.1 pad_add_fusion.place_ref
  0.7 1.7 %shard_map.113 = f32[8,4,128]{2,1,0:T(4,128)S(1)} custom-call(f32[1,128]{1,0:T(1,128)} %bitcast.13, f32[1,128]{1,0:T(1,128)} %bitcast.14, s32[1,128]{1,0:T(1,128)} %bitcast.15, s32[1,64]{1,0:T(1,128)} %bitcast.16, f32[2,64]{1,0:T(2,128)} %coupling_in.1, s32[2]{0:T(128)S(1)} %pad_add_fusion.place_ref), custom_call_target="tpu_custom_call" | custom-call | tf_op jit(solution)/shard_map/pallas_call | solution.py:406
  2.4 14.1 %all_to_all.40.table_ref = f32[8,4,128]{2,1,0:T(4,128)S(1)} all-to-all(f32[8,4,128]{2,1,0:T(4,128)S(1)} %shard_map.113), channel_id=1, replica_groups=mesh['z'=4,'x'=8,'core'=2,'wrow'=8] {'wrow'}, dimensions={0} | all-to-all | bytes 32768 | tf_op jit(solution)/shard_map/all_to_all | solution.py:452
  16.4 9.3 %shard_map.114 = (bf16[64,8,128]{2,1,0:T(8,128)(2,1)}, f32[4,512,128]{2,1,0:T(8,128)S(1)}, bf16[512,64]{1,0:T(8,128)(2,1)S(1)}, f32[1,4096]{1,0:T(1,128)S(1)}, b...) custom-call(f32[8,4,128]{2,1,0:T(4,128)S(1)} %all_to_all.40.table_ref, f32[1,3072]{1,0:T(1,128)} %bitcast.12, ...), custom_call_target="tpu_custom_call" | custom-call | tf_op jit(solution)/shard_map/pallas_call | solution.py:406
  25.8 15.5 %all-to-all-start.1 = ((bf16[64,8,128]{2,1,0:T(8,128)(2,1)}), bf16[64,8,128]{2,1,0:T(8,128)(2,1)S(1)}, u32[]{:S(2)}, u32[]{:S(2)}) async-start(bf16[64,8,128]{2,1,0:T(8,128)(2,1)} %get-tuple-element.20), calls=%async_computation.1 | async-start | bytes 262144 | tf_op jit(solution)/shard_map/all_to_all | solution.py:476
  41.3 8.9 %shard_map.115 = (f32[2,128]{1,0:T(2,128)S(1)}, f32[8,128]{1,0:T(8,128)S(1)}, bf16[1024,4096]{1,0:T(8,128)(2,1)}) custom-call(f32[8,4,128]{2,1,0:T(4,128)S(1)} %all_to_all.40.table_ref, f32[4,512,128]{2,1,0:T(8,128)S(1)} %get-tuple-element.21.wide_ref, bf16[512,64]{1,0:T(8,128)(2,1)S(1)} %get-tuple-element.22.chooser_ref, ...), custom_call_target="tpu_custom_call" | custom-call | flops 83886080 | bytes 16777216 | tf_op jit(solution)/shard_map/pallas_call | solution.py:406
  50.2 2.2 %all-to-all-done.1.pieces_ref = bf16[64,8,128]{2,1,0:T(8,128)(2,1)S(1)} async-done(((bf16[64,8,128]{2,1,0:T(8,128)(2,1)}), bf16[64,8,128]{2,1,0:T(8,128)(2,1)S(1)}, u32[]{:S(2)}, u32[]{:S(2)}) %all-to-all-start.1) | async-done | bytes 131104 | tf_op jit(solution)/shard_map/all_to_all | solution.py:476
  52.4 0.7 shard_map.116
  53.2 15.8 %all_to_all.41.received_ref = f32[32,2,128]{2,1,0:T(2,128)S(1)} all-to-all(f32[32,2,128]{2,1,0:T(2,128)S(1)} %get-tuple-element.28), channel_id=1, replica_groups=mesh['z'=4,'x'=8,'core'=2,'wrow'=8] {'z','x'}, dimensions={0} | all-to-all | bytes 65536 | tf_op jit(solution)/shard_map/all_to_all | solution.py:496
  69.0 11.2 %all_to_all.42.received_ref = f32[16,2,128]{2,1,0:T(2,128)S(1)} all-to-all(f32[16,2,128]{2,1,0:T(2,128)S(1)} %shard_map.117), channel_id=1, replica_groups=mesh['z'=4,'x'=8,'core'=2,'wrow'=8] {'core','wrow'}, dimensions={0} | all-to-all | bytes 32768 | tf_op jit(solution)/shard_map/all_to_all | solution.py:497
  80.1 4.6 %shard_map.118 = (f32[32,2,128]{2,1,0:T(2,128)S(1)}, f32[8,128]{1,0:T(8,128)S(1)}, bf16[1024,4096]{1,0:T(8,128)(2,1)S(1)}) custom-call(f32[16,2,128]{2,1,0:T(2,128)S(1)} %all_to_all.42.received_ref, f32[8,128]{1,0:T(8,128)S(1)} %get-tuple-element.27.coupling_ref.old_ref, bf16[1024,4096]{1,0:T(8,128)(2,1)} %get-tuple-element.29.amp_in, ...), custom_call_target="tpu_custom_call" | custom-call | tf_op jit(solution)/shard_map/pallas_call | solution.py:406
  84.7 11.6 %all_to_all.43.received_ref = f32[32,2,128]{2,1,0:T(2,128)S(1)} all-to-all(f32[32,2,128]{2,1,0:T(2,128)S(1)} %get-tuple-element.31), channel_id=1, replica_groups=mesh['z'=4,'x'=8,'core'=2,'wrow'=8] {'z','x'}, dimensions={0} | all-to-all | bytes 65536 | tf_op jit(solution)/shard_map/all_to_all | solution.py:496
  96.4 11.3 %all_to_all.44.received_ref = f32[16,2,128]{2,1,0:T(2,128)S(1)} all-to-all(f32[16,2,128]{2,1,0:T(2,128)S(1)} %shard_map.119), channel_id=1, replica_groups=mesh['z'=4,'x'=8,'core'=2,'wrow'=8] {'core','wrow'}, dimensions={0} | all-to-all | bytes 32768 | tf_op jit(solution)/shard_map/all_to_all | solution.py:497
  107.6 3.3 %shard_map.120 = (f32[32,2,128]{2,1,0:T(2,128)S(1)}, f32[8,128]{1,0:T(8,128)S(1)}) custom-call(f32[16,2,128]{2,1,0:T(2,128)S(1)} %all_to_all.44.received_ref, f32[8,128]{1,0:T(8,128)S(1)} %get-tuple-element.32.old_ref, bf16[1024,4096]{1,0:T(8,128)(2,1)S(1)} %get-tuple-element.33.amp_ref, f32[1,4096]{1,0:T(1,128)S(1)} %get-tuple-element.25.weight_ref, ...), custom_call_target="tpu_custom_call" | custom-call | tf_op jit(solution)/shard_map/pallas_call | solution.py:406
  110.9 11.6 %all_to_all.45.received_ref = f32[32,2,128]{2,1,0:T(2,128)S(1)} all-to-all(f32[32,2,128]{2,1,0:T(2,128)S(1)} %get-tuple-element.34), channel_id=1, replica_groups=mesh['z'=4,'x'=8,'core'=2,'wrow'=8] {'z','x'}, dimensions={0} | all-to-all | bytes 65536 | tf_op jit(solution)/shard_map/all_to_all | solution.py:496
  122.6 11.3 %all_to_all.46.received_ref = f32[16,2,128]{2,1,0:T(2,128)S(1)} all-to-all(f32[16,2,128]{2,1,0:T(2,128)S(1)} %shard_map.121), channel_id=1, replica_groups=mesh['z'=4,'x'=8,'core'=2,'wrow'=8] {'core','wrow'}, dimensions={0} | all-to-all | bytes 32768 | tf_op jit(solution)/shard_map/all_to_all | solution.py:497
  133.8 3.4 %shard_map.122 = (f32[2,64]{1,0:T(2,128)}, f32[1,4096]{1,0:T(1,128)}) custom-call(f32[16,2,128]{2,1,0:T(2,128)S(1)} %all_to_all.46.received_ref, f32[8,128]{1,0:T(8,128)S(1)} %get-tuple-element.35.old_ref, bf16[1024,4096]{1,0:T(8,128)(2,1)S(1)} %get-tuple-element.33.amp_ref, s32[2]{0:T(128)S(1)} %pad_add_fusion.place_ref), custom_call_target="tpu_custom_call" | custom-call | tf_op jit(solution)/shard_map/pallas_call | solution.py:406
  (3 shorter events, 0.1 us)
Async XLA Ops:
  25.8 26.6 %all-to-all-start.1 = ((bf16[64,8,128]{2,1,0:T(8,128)(2,1)}), bf16[64,8,128]{2,1,0:T(8,128)(2,1)S(1)}, u32[]{:S(2)}, u32[]{:S(2)}) async-start(bf16[64,8,128]{2,1,0:T(8,128)(2,1)} %get-tuple-element.20), calls=%async_computation.1 | async-start | bytes 262144 | tf_op jit(solution)/shard_map/all_to_all | solution.py:476

commit v6 on v5

--- a/solution.py
+++ b/solution.py
@@ -20,6 +20,7 @@
 PARAMS = 4
 NEXT_ROWS = 256
 LAST_ROWS = 256
+HEAD = 1
 VMEM_LIMIT = 24 << 20
 
 
@@ -31,8 +32,8 @@
 
 
 def prepare_kernel(
-    mass_in, width_in, wave_in, level_in, coupling_in, place_ref, out_ref,
-    mass_ref, width_ref, wave_ref, level_ref, coupling_ref, sems
+    mass_in, width_in, wave_in, level_in, coupling_in, mc_mass_in, mc_basis_in, place_ref,
+    out_ref, mc_mass_ref, mc_basis_ref, mass_ref, width_ref, wave_ref, level_ref, coupling_ref, sems, mc_sems
 ):
     pairs = (
         (mass_in, mass_ref),
@@ -41,7 +42,9 @@
         (level_in, level_ref),
         (coupling_in, coupling_ref),
     )
-    for copy in copies(pairs, sems):
+    small = copies(pairs, sems)
+    large = copies(((mc_mass_in, mc_mass_ref), (mc_basis_in, mc_basis_ref)), mc_sems)
+    for copy in small:
         copy.wait()
     count = mass_ref.shape[1]
     local = wave_ref[...] - place_ref[0] * OWN
@@ -68,6 +71,8 @@
     )
     rows = jnp.concatenate([turned[0:4, 0:OWN], rest], axis=1)
     send_terms(rows, out_ref)
+    for copy in large:
+        copy.wait()
 
 
 def load_table(table_ref, wide_ref, chooser_ref):
@@ -120,11 +125,10 @@
 
 
 def gram_kernel(
-    scale, table_ref, mass_in, basis_in, data_mass_in, data_basis_in, weight_in, place_ref,
+    scale, table_ref, mass_ref, basis_ref, data_mass_in, data_basis_in, weight_in, place_ref,
     out_ref, wide_ref, chooser_ref, data_mass_ref, data_basis_ref, weight_ref,
-    mass_ref, basis_ref, amp_ref, sum_ref, turn_ref, sems, data_sems
-):
-    now = copies(((mass_in, mass_ref), (basis_in, basis_ref)), sems)
+    amp_ref, sum_ref, turn_ref, data_sems
+):
     later = copies(
         ((data_mass_in, data_mass_ref), (data_basis_in, data_basis_ref), (weight_in, weight_ref)), data_sems
     )
@@ -135,9 +139,6 @@
     def store(row, real, imag):
         amp_ref[row : row + ROWS, :] = real
         amp_ref[row + OWN : row + OWN + ROWS, :] = imag
-
-    for copy in now:
-        copy.wait()
 
     @pl.loop(0, mass_ref.shape[1] // TILE)
     def _(step):
@@ -287,7 +288,7 @@
 
 def first_kernel(
     scale, table_ref, wide_ref, chooser_ref, mass_ref, basis_ref, weight_ref, place_ref,
-    out_ref, coupling_ref, amp_out, amp_ref, parts_ref, by_real_ref, by_imag_ref, curve_ref, sems
+    out_ref, coupling_ref, head_ref, amp_out, amp_ref, parts_ref, by_real_ref, by_imag_ref, curve_ref, sems
 ):
     for block in range(table_ref.shape[0]):
         half = table_ref[block]
@@ -295,25 +296,32 @@
     load_coupling(coupling_ref[...], parts_ref)
     parts = parts_ref[...].astype(jnp.bfloat16)
     clear(by_real_ref, by_imag_ref, curve_ref)
-
-    @pl.loop(0, mass_ref.shape[1] // TILE)
+    tail = amp_ref.shape[1] // TILE
+
+    def compute(event_tile, target_ref, target_tile):
+        events, columns = tile_at(event_tile), tile_at(target_tile)
+
+        def store(row, real, imag):
+            target_ref[row : row + ROWS, columns] = real
+            target_ref[row + OWN : row + OWN + ROWS, columns] = imag
+
+        fill_tile(mass_ref[:, events], basis_ref[:, events], wide_ref, chooser_ref, store)
+        real, imag = field_of(parts, target_ref, columns)
+        own = target_ref[own_rows(place_ref), columns]
+        project_tile(real, imag, weight_ref[:, events], own, by_real_ref, by_imag_ref, curve_ref)
+
+    def copy(step):
+        return pltpu.make_async_copy(amp_ref.at[:, tile_at(step)], amp_out.at[:, tile_at(step)], sems.at[step])
+
+    @pl.loop(0, tail)
     def _(step):
-        columns = pl.ds(pl.multiple_of(step * TILE, TILE), TILE)
-
-        def store(row, real, imag):
-            amp_ref[row : row + ROWS, columns] = real
-            amp_ref[row + OWN : row + OWN + ROWS, columns] = imag
-
-        fill_tile(mass_ref[:, columns], basis_ref[:, columns], wide_ref, chooser_ref, store)
-        real, imag = field_of(parts, amp_ref, columns)
-        own = amp_ref[own_rows(place_ref), columns]
-        project_tile(real, imag, weight_ref[:, columns], own, by_real_ref, by_imag_ref, curve_ref)
-        pltpu.make_async_copy(amp_ref.at[:, columns], amp_out.at[:, columns], sems.at[step]).start()
-
+        compute(step + HEAD, amp_ref, step)
+        copy(step).start()
+
+    compute(0, head_ref, 0)
     out_ref[...] = gradient_rows(scale, by_real_ref, by_imag_ref, curve_ref)
-    for step in range(amp_ref.shape[1] // TILE):
-        columns = pl.ds(step * TILE, TILE)
-        pltpu.make_async_copy(amp_ref.at[:, columns], amp_out.at[:, columns], sems.at[step]).wait()
+    for step in range(tail):
+        copy(step).wait()
 
 
 def add_kernel(pieces_ref, base_ref, coupling_ref, place_ref, out_ref, gram_ref):
@@ -331,7 +339,7 @@
 
 
 def next_pass(
-    scale, received_ref, old_ref, amp_ref, arrive, weight_ref, place_ref, gram_ref, out_ref, coupling_ref,
+    scale, received_ref, old_ref, head_ref, tail_ref, arrive, weight_ref, place_ref, gram_ref, out_ref, coupling_ref,
     parts_ref, by_real_ref, by_imag_ref, curve_ref, column_ref
 ):
     coupling = new_coupling(received_ref, old_ref)
@@ -340,47 +348,53 @@
     load_columns(signed, swapped, column_ref.shape[1], column_ref)
     parts = parts_ref[...].astype(jnp.bfloat16)
     clear(by_real_ref, by_imag_ref, curve_ref)
-    tiles = amp_ref.shape[1] // TILE
-
-    def project(step, field):
-        own = amp_ref[own_rows(place_ref), tile_at(step)]
-        project_tile(*field, weight_ref[:, tile_at(step)], own, by_real_ref, by_imag_ref, curve_ref)
+    tiles = tail_ref.shape[1] // TILE
+
+    def field_at(source_ref, step):
+        return field_of(parts, source_ref, tile_at(step), column_ref)
+
+    def project(source_ref, step, event_tile, field):
+        own = source_ref[own_rows(place_ref), tile_at(step)]
+        project_tile(*field, weight_ref[:, tile_at(event_tile)], own, by_real_ref, by_imag_ref, curve_ref)
 
     def ahead(step, field):
         arrive(step + 1)
-        later = field_of(parts, amp_ref, tile_at(step + 1), column_ref)
-        project(step, field)
+        later = field_at(tail_ref, step + 1)
+        project(tail_ref, step, step + HEAD, field)
         return later
 
+    field = field_at(head_ref, 0)
     arrive(0)
-    field = lax.fori_loop(0, tiles - 1, ahead, field_of(parts, amp_ref, tile_at(0), column_ref))
-    project(tiles - 1, field)
+    later = field_at(tail_ref, 0)
+    project(head_ref, 0, 0, field)
+    field = lax.fori_loop(0, tiles - 1, ahead, later)
+    project(tail_ref, tiles - 1, tiles - 1 + HEAD, field)
     terms = gradient_rows(scale, by_real_ref, by_imag_ref, curve_ref)
     send_terms(terms + gram_rows(gram_ref[...], signed, swapped, place_ref), out_ref)
 
 
-def second_kernel(scale, received_ref, old_ref, amp_in, weight_ref, place_ref, gram_ref, out_ref, coupling_ref, amp_ref, *scratch):
+def second_kernel(
+    scale, received_ref, old_ref, head_ref, tail_in, weight_ref, place_ref, gram_ref, out_ref, coupling_ref, tail_ref, *scratch
+):
     sems = scratch[-1]
 
     def copy(step):
-        return pltpu.make_async_copy(amp_in.at[:, tile_at(step)], amp_ref.at[:, tile_at(step)], sems.at[step])
-
-    for step in range(amp_ref.shape[1] // TILE):
+        return pltpu.make_async_copy(tail_in.at[:, tile_at(step)], tail_ref.at[:, tile_at(step)], sems.at[step])
+
+    for step in range(tail_ref.shape[1] // TILE):
         copy(step).start()
     next_pass(
-        scale, received_ref, old_ref, amp_ref, lambda step: copy(step).wait(), weight_ref, place_ref, gram_ref,
+        scale, received_ref, old_ref, head_ref, tail_ref, lambda step: copy(step).wait(), weight_ref, place_ref, gram_ref,
         out_ref, coupling_ref, *scratch[:-1]
     )
 
 
-def next_kernel(scale, received_ref, old_ref, amp_ref, weight_ref, place_ref, gram_ref, *rest):
-    next_pass(
-        scale, received_ref, old_ref, amp_ref, lambda step: None, weight_ref, place_ref, gram_ref, *rest
-    )
+def next_kernel(scale, received_ref, old_ref, head_ref, tail_ref, *rest):
+    next_pass(scale, received_ref, old_ref, head_ref, tail_ref, lambda step: None, *rest)
 
 
 def last_kernel(
-    received_ref, old_ref, amp_ref, place_ref, coupling_out_ref, intensity_ref, parts_ref, coupling_ref, column_ref
+    received_ref, old_ref, head_ref, tail_ref, place_ref, coupling_out_ref, intensity_ref, parts_ref, coupling_ref, column_ref
 ):
     coupling = new_coupling(received_ref, old_ref)
     coupling_ref[...] = coupling
@@ -391,10 +405,15 @@
     coupling_out_ref[0:1, :] = mine[:, 0:OWN]
     coupling_out_ref[1:2, :] = pltpu.roll(mine, OWN, 1)[:, 0:OWN]
 
-    @pl.loop(0, amp_ref.shape[1] // TILE)
+    def finish(source_ref, step, event_tile):
+        real, imag = field_of(parts, source_ref, tile_at(step), column_ref)
+        intensity_ref[:, tile_at(event_tile)] = real * real + imag * imag + BACKGROUND
+
+    finish(head_ref, 0, 0)
+
+    @pl.loop(0, tail_ref.shape[1] // TILE)
     def _(step):
-        real, imag = field_of(parts, amp_ref, tile_at(step), column_ref)
-        intensity_ref[:, tile_at(step)] = real * real + imag * imag + BACKGROUND
+        finish(tail_ref, step, step + HEAD)
 
 
 def call(kernel, outs, scratch, *args, smem, hbm=(), hbm_out=(), cost=None):
@@ -434,9 +453,9 @@
     levels = mc_basis.shape[0]
     mc_count, data_count = mc_mass.shape[0], data_mass.shape[0]
     places = jnp.stack([lax.axis_index("wrow"), lax.axis_index(EVENT)]).astype(jnp.int32)
-    own_table = call(
+    own_table, mc_mass, mc_basis = call(
         prepare_kernel,
-        shape(rows, 4, LANES),
+        (shape(rows, 4, LANES), shape(1, mc_count), shape(levels, mc_count, dtype=jnp.bfloat16)),
         [
             pltpu.VMEM((1, res_mass.shape[0]), jnp.float32),
             pltpu.VMEM((1, res_width.shape[0]), jnp.float32),
@@ -444,10 +463,11 @@
             pltpu.VMEM((1, OWN), jnp.int32),
             pltpu.VMEM((2, OWN), jnp.float32),
             pltpu.SemaphoreType.DMA((5,)),
+            pltpu.SemaphoreType.DMA((2,)),
         ],
-        res_mass[None], res_width[None], res_wave[None], wave_q[None], couplings, places,
-        smem=(5,),
-        hbm=range(5),
+        res_mass[None], res_width[None], res_wave[None], wave_q[None], couplings, mc_mass[None], mc_basis, places,
+        smem=(7,),
+        hbm=range(7),
     )
     table = lax.all_to_all(own_table, "wrow", 0, 0)
     tile, wide, chooser, data_mass, data_basis, weight = call(
@@ -461,29 +481,31 @@
             shape(1, data_count),
         ),
         [
-            pltpu.VMEM((1, mc_count), jnp.float32),
-            pltpu.VMEM((levels, mc_count), jnp.bfloat16),
             pltpu.VMEM((2 * waves, TILE), jnp.bfloat16),
             pltpu.VMEM((2 * waves, LANES), jnp.float32),
             pltpu.VMEM((OWN, rows, LANES), jnp.float32),
-            pltpu.SemaphoreType.DMA((2,)),
             pltpu.SemaphoreType.DMA((3,)),
         ],
-        table, mc_mass[None], mc_basis, data_mass[None], data_basis, data_weight[None], places,
+        table, mc_mass, mc_basis, data_mass[None], data_basis, data_weight[None], places,
         smem=(6,),
-        hbm=range(1, 6),
+        hbm=range(3, 6),
     )
     pieces = lax.all_to_all(tile, EVENT, 0, 0)
     inverse_count = 1.0 / (data_count * events)
     tile_sems = pltpu.SemaphoreType.DMA((data_count // TILE,))
-    amp_shape = (2 * waves, data_count)
-    base, coupling, amp = call(
+    tail_shape = (2 * waves, data_count - HEAD * TILE)
+    base, coupling, head, tail = call(
         functools.partial(first_kernel, inverse_count),
-        (shape(2, LANES), shape(rows, LANES), pltpu.HBM(amp_shape, jnp.bfloat16)),
-        [pltpu.VMEM(amp_shape, jnp.bfloat16)] + pass_scratch(waves) + [tile_sems],
+        (
+            shape(2, LANES),
+            shape(rows, LANES),
+            shape(2 * waves, HEAD * TILE, dtype=jnp.bfloat16),
+            pltpu.HBM(tail_shape, jnp.bfloat16),
+        ),
+        [pltpu.VMEM(tail_shape, jnp.bfloat16)] + pass_scratch(waves) + [tile_sems],
         table, wide, chooser, data_mass, data_basis, weight, places,
         smem=(6,),
-        hbm_out=(2,),
+        hbm_out=(3,),
         cost=pl.CostEstimate(
             flops=40 * waves * data_count, bytes_accessed=8 * waves * data_count, transcendentals=waves * data_count
         ),
@@ -500,21 +522,21 @@
     for step in range(1, ITERS):
         received = exchange(terms)
         if step == 1:
-            terms, coupling, amp = call(
+            terms, coupling, tail = call(
                 functools.partial(second_kernel, inverse_count),
-                (shape(zx, 2, LANES), shape(rows, LANES), shape(*amp_shape, dtype=jnp.bfloat16)),
+                (shape(zx, 2, LANES), shape(rows, LANES), shape(*tail_shape, dtype=jnp.bfloat16)),
                 pass_scratch(waves) + column_scratch + [tile_sems],
-                received, coupling, amp, weight, places, gram_row,
-                smem=(4,),
-                hbm=(2,),
+                received, coupling, head, tail, weight, places, gram_row,
+                smem=(5,),
+                hbm=(3,),
             )
         else:
             terms, coupling = call(
                 functools.partial(next_kernel, inverse_count),
                 (shape(zx, 2, LANES), shape(rows, LANES)),
                 pass_scratch(waves) + column_scratch,
-                received, coupling, amp, weight, places, gram_row,
-                smem=(4,),
+                received, coupling, head, tail, weight, places, gram_row,
+                smem=(5,),
             )
     received = exchange(terms)
     coupling_out, intensity = call(
@@ -525,8 +547,8 @@
             pltpu.VMEM((rows, LANES), jnp.float32),
             pltpu.VMEM((2, LAST_ROWS, LANES), jnp.float32),
         ],
-        received, coupling, amp, places,
-        smem=(3,),
+        received, coupling, head, tail, places,
+        smem=(4,),
     )
     return coupling_out, intensity.reshape(data_count)
 

time: 138 us -> 135 us (0.978)
  Pallas kernels: 32 us -> 29.8 us
    pallas_call x10, Pallas kernels: 32 us -> 29.8 us  [call(): pl.pallas_call(kernel, out_shape=outs, in_specs=[pl.BlockSpec(memory_spac...]
where the time goes in v6:
time: 135 us
  blocking collectives  86 us (64%)
  Pallas kernels  29.8 us (22%)
  starting transfers between devices  15.5 us (11%)
  waiting for transfers between devices  2.98 us (2%)
    all_to_all x3, blocking collectives, exchange(): lax.all_to_all(values, ZX, 0, 0)  38.2 us
    all_to_all x3, blocking collectives, exchange(): return lax.all_to_all(merged, PEERS, 0, 0)  33.7 us
    pallas_call x10, Pallas kernels, call(): pl.pallas_call(kernel, out_shape=outs, in_specs=[pl.BlockSpec(memory_spac...  29.8 us
    all_to_all x1, starting transfers between devices, shards(): pieces = lax.all_to_all(tile, EVENT, 0, 0)  15.5 us
    all_to_all x1, blocking collectives, shards(): table = lax.all_to_all(own_table, 'wrow', 0, 0)  14.1 us
    all_to_all x1, waiting for transfers between devices, shards(): pieces = lax.all_to_all(tile, EVENT, 0, 0)  2.98 us
  transfers between devices with their start and end apart: 1, of which 1 were waited for; matrix products, arithmetic and copies ran while one was open for 0% of the time, Pallas kernels for 6%

profile of v6, /device:TPU:1, one launch (start us, length us, event | category | flops | bytes accessed | tf_op | source)
XLA Modules:
  0.0 135.0 jit_solution(10266034775651813772)
XLA Ops:
  0.6 0.1 pad_add_fusion.place_ref.rest_1_
  0.7 1.7 %shard_map.113 = (f32[8,4,128]{2,1,0:T(4,128)S(1)}, f32[1,3072]{1,0:T(1,128)S(1)}, bf16[64,3072]{1,0:T(8,128)(2,1)S(1)}) custom-call(f32[1,128]{1,0:T(1,128)} %bitcast.13, f32[1,128]{1,0:T(1,128)} %bitcast.14, s32[1,128]{1,0:T(1,128)} %bitcast.15, s32[1,64]{1,0:T(1,128)} %bitcast.16, f32[2,64]{1,0:T(2,128)} %coupling_in.1, f32[1,3072]{1,0:T(1,128)} %bitcast.12, ...), custom_call_target="tpu_custom_call" | custom-call | tf_op jit(solution)/shard_map/pallas_call | solution.py:425
  2.4 14.1 %all_to_all.40.table_ref = f32[8,4,128]{2,1,0:T(4,128)S(1)} all-to-all(f32[8,4,128]{2,1,0:T(4,128)S(1)} %get-tuple-element.24), channel_id=1, replica_groups=mesh['z'=4,'x'=8,'core'=2,'wrow'=8] {'wrow'}, dimensions={0} | all-to-all | bytes 32768 | tf_op jit(solution)/shard_map/all_to_all | solution.py:472
  16.5 8.8 %shard_map.114 = (bf16[64,8,128]{2,1,0:T(8,128)(2,1)}, f32[4,512,128]{2,1,0:T(8,128)S(1)}, bf16[512,64]{1,0:T(8,128)(2,1)S(1)}, f32[1,4096]{1,0:T(1,128)S(1)}, b...) custom-call(f32[8,4,128]{2,1,0:T(4,128)S(1)} %all_to_all.40.table_ref, f32[1,3072]{1,0:T(1,128)S(1)} %get-tuple-element.25.mass_ref, ...), custom_call_target="tpu_custom_call" | custom-call | tf_op jit(solution)/shard_map/pallas_call | solution.py:425
  25.3 15.5 %all-to-all-start.1 = ((bf16[64,8,128]{2,1,0:T(8,128)(2,1)}), bf16[64,8,128]{2,1,0:T(8,128)(2,1)S(1)}, u32[]{:S(2)}, u32[]{:S(2)}) async-start(bf16[64,8,128]{2,1,0:T(8,128)(2,1)} %get-tuple-element.27), calls=%async_computation.1 | async-start | bytes 262144 | tf_op jit(solution)/shard_map/all_to_all | solution.py:493
  40.8 8.1 %shard_map.115 = (f32[2,128]{1,0:T(2,128)S(1)}, f32[8,128]{1,0:T(8,128)S(1)}, bf16[1024,512]{1,0:T(8,128)(2,1)S(1)}, bf16[1024,3584]{1,0:T(8,128)(2,1)}) custom-call(f32[8,4,128]{2,1,0:T(4,128)S(1)} %all_to_all.40.table_ref, f32[4,512,128]{2,1,0:T(8,128)S(1)} %get-tuple-element.28.wide_ref, bf16[512,64]{1,0:T(8,128)(2,1)S(1)} %get-tuple-element.29.chooser_ref, ...), custom_call_target="tpu_custom_call" | custom-call | flops 83886080 | bytes 16777216 | tf_op jit(solution)/shard_map/pallas_call | solution.py:425
  48.9 3.0 %all-to-all-done.1.pieces_ref = bf16[64,8,128]{2,1,0:T(8,128)(2,1)S(1)} async-done(((bf16[64,8,128]{2,1,0:T(8,128)(2,1)}), bf16[64,8,128]{2,1,0:T(8,128)(2,1)S(1)}, u32[]{:S(2)}, u32[]{:S(2)}) %all-to-all-start.1) | async-done | bytes 131104 | tf_op jit(solution)/shard_map/all_to_all | solution.py:493
  51.9 0.7 shard_map.116
  52.6 15.0 %all_to_all.41.received_ref = f32[32,2,128]{2,1,0:T(2,128)S(1)} all-to-all(f32[32,2,128]{2,1,0:T(2,128)S(1)} %get-tuple-element.35), channel_id=1, replica_groups=mesh['z'=4,'x'=8,'core'=2,'wrow'=8] {'z','x'}, dimensions={0} | all-to-all | bytes 65536 | tf_op jit(solution)/shard_map/all_to_all | solution.py:518
  67.7 11.2 %all_to_all.42.received_ref = f32[16,2,128]{2,1,0:T(2,128)S(1)} all-to-all(f32[16,2,128]{2,1,0:T(2,128)S(1)} %shard_map.117), channel_id=1, replica_groups=mesh['z'=4,'x'=8,'core'=2,'wrow'=8] {'core','wrow'}, dimensions={0} | all-to-all | bytes 32768 | tf_op jit(solution)/shard_map/all_to_all | solution.py:519
  78.8 4.3 %shard_map.118 = (f32[32,2,128]{2,1,0:T(2,128)S(1)}, f32[8,128]{1,0:T(8,128)S(1)}, bf16[1024,3584]{1,0:T(8,128)(2,1)S(1)}) custom-call(f32[16,2,128]{2,1,0:T(2,128)S(1)} %all_to_all.42.received_ref, f32[8,128]{1,0:T(8,128)S(1)} %get-tuple-element.34.coupling_ref.old_ref, bf16[1024,512]{1,0:T(8,128)(2,1)S(1)} %get-tuple-element.36.head_ref, ...), custom_call_target="tpu_custom_call" | custom-call | tf_op jit(solution)/shard_map/pallas_call | solution.py:425
  83.1 11.6 %all_to_all.43.received_ref = f32[32,2,128]{2,1,0:T(2,128)S(1)} all-to-all(f32[32,2,128]{2,1,0:T(2,128)S(1)} %get-tuple-element.39), channel_id=1, replica_groups=mesh['z'=4,'x'=8,'core'=2,'wrow'=8] {'z','x'}, dimensions={0} | all-to-all | bytes 65536 | tf_op jit(solution)/shard_map/all_to_all | solution.py:518
  94.8 11.3 %all_to_all.44.received_ref = f32[16,2,128]{2,1,0:T(2,128)S(1)} all-to-all(f32[16,2,128]{2,1,0:T(2,128)S(1)} %shard_map.119), channel_id=1, replica_groups=mesh['z'=4,'x'=8,'core'=2,'wrow'=8] {'core','wrow'}, dimensions={0} | all-to-all | bytes 32768 | tf_op jit(solution)/shard_map/all_to_all | solution.py:519
  106.0 2.8 %shard_map.120 = (f32[32,2,128]{2,1,0:T(2,128)S(1)}, f32[8,128]{1,0:T(8,128)S(1)}) custom-call(f32[16,2,128]{2,1,0:T(2,128)S(1)} %all_to_all.44.received_ref, f32[8,128]{1,0:T(8,128)S(1)} %get-tuple-element.40.old_ref, bf16[1024,512]{1,0:T(8,128)(2,1)S(1)} %get-tuple-element.36.head_ref, bf16[1024,3584]{1,0:T(8,128)(2,1)S(1)} %get-tuple-element.41.tail_ref, ...), custom_call_target="tpu_custom_call" | custom-call | tf_op jit(solution)/shard_map/pallas_call | solution.py:425
  108.8 11.6 %all_to_all.45.received_ref = f32[32,2,128]{2,1,0:T(2,128)S(1)} all-to-all(f32[32,2,128]{2,1,0:T(2,128)S(1)} %get-tuple-element.42), channel_id=1, replica_groups=mesh['z'=4,'x'=8,'core'=2,'wrow'=8] {'z','x'}, dimensions={0} | all-to-all | bytes 65536 | tf_op jit(solution)/shard_map/all_to_all | solution.py:518
  120.5 11.3 %all_to_all.46.received_ref = f32[16,2,128]{2,1,0:T(2,128)S(1)} all-to-all(f32[16,2,128]{2,1,0:T(2,128)S(1)} %shard_map.121), channel_id=1, replica_groups=mesh['z'=4,'x'=8,'core'=2,'wrow'=8] {'core','wrow'}, dimensions={0} | all-to-all | bytes 32768 | tf_op jit(solution)/shard_map/all_to_all | solution.py:519
  131.7 3.2 %shard_map.122 = (f32[2,64]{1,0:T(2,128)}, f32[1,4096]{1,0:T(1,128)}) custom-call(f32[16,2,128]{2,1,0:T(2,128)S(1)} %all_to_all.46.received_ref, f32[8,128]{1,0:T(8,128)S(1)} %get-tuple-element.43.old_ref, bf16[1024,512]{1,0:T(8,128)(2,1)S(1)} %get-tuple-element.36.head_ref, bf16[1024,3584]{1,0:T(8,128)(2,1)S(1)} %get-tuple-element.41.tail_ref, ...), custom_call_target="tpu_custom_call" | custom-call | tf_op jit(solution)/shard_map/pallas_call | solution.py:425
  (3 shorter events, 0.1 us)
Async XLA Ops:
  25.3 26.6 %all-to-all-start.1 = ((bf16[64,8,128]{2,1,0:T(8,128)(2,1)}), bf16[64,8,128]{2,1,0:T(8,128)(2,1)S(1)}, u32[]{:S(2)}, u32[]{:S(2)}) async-start(bf16[64,8,128]{2,1,0:T(8,128)(2,1)} %get-tuple-element.27), calls=%async_computation.1 | async-start | bytes 262144 | tf_op jit(solution)/shard_map/all_to_all | solution.py:493

commit v7 on v6

--- a/solution.py
+++ b/solution.py
@@ -21,6 +21,7 @@
 NEXT_ROWS = 256
 LAST_ROWS = 256
 HEAD = 1
+AHEAD = 3
 VMEM_LIMIT = 24 << 20
 
 
@@ -32,9 +33,10 @@
 
 
 def prepare_kernel(
-    mass_in, width_in, wave_in, level_in, coupling_in, mc_mass_in, mc_basis_in, place_ref,
+    mass_in, width_in, wave_in, level_in, coupling_in, mc_mass_in, mc_basis_in,
     out_ref, mc_mass_ref, mc_basis_ref, mass_ref, width_ref, wave_ref, level_ref, coupling_ref, sems, mc_sems
 ):
+    place_ref = here()
     pairs = (
         (mass_in, mass_ref),
         (width_in, width_ref),
@@ -125,10 +127,11 @@
 
 
 def gram_kernel(
-    scale, table_ref, mass_ref, basis_ref, data_mass_in, data_basis_in, weight_in, place_ref,
+    scale, table_ref, mass_ref, basis_ref, data_mass_in, data_basis_in, weight_in,
     out_ref, wide_ref, chooser_ref, data_mass_ref, data_basis_ref, weight_ref,
     amp_ref, sum_ref, turn_ref, data_sems
 ):
+    place_ref = here()
     later = copies(
         ((data_mass_in, data_mass_ref), (data_basis_in, data_basis_ref), (weight_in, weight_ref)), data_sems
     )
@@ -257,9 +260,9 @@
     mixed_imag = jnp.sum(gram * swapped, keepdims=True)
     row_weight = jnp.sum(jnp.abs(gram), keepdims=True)
     lane = lax.broadcasted_iota(jnp.int32, (1, LANES), 1)
-    here = place_ref[1]
-    grad_row = jnp.where(lane == here, mixed_real, 0.0) + jnp.where(lane == here + OWN, mixed_imag, 0.0)
-    curve_row = jnp.where(lane == here + OWN, row_weight, 0.0)
+    event = place_ref[1]
+    grad_row = jnp.where(lane == event, mixed_real, 0.0) + jnp.where(lane == event + OWN, mixed_imag, 0.0)
+    curve_row = jnp.where(lane == event + OWN, row_weight, 0.0)
     return jnp.concatenate([grad_row, curve_row], axis=0)
 
 
@@ -268,6 +271,11 @@
     return jnp.where(lane < OWN, coupling, -coupling), pltpu.roll(coupling, OWN, 1)
 
 
+def here():
+    chip = lax.axis_index("z") * lax.axis_size("x") + lax.axis_index("x")
+    return lax.axis_index("wrow"), chip * lax.axis_size("core") + lax.axis_index("core")
+
+
 def send_terms(terms, out_ref):
     for peer in range(out_ref.shape[0]):
         out_ref[peer] = terms
@@ -287,9 +295,10 @@
 
 
 def first_kernel(
-    scale, table_ref, wide_ref, chooser_ref, mass_ref, basis_ref, weight_ref, place_ref,
+    scale, table_ref, wide_ref, chooser_ref, mass_ref, basis_ref, weight_ref,
     out_ref, coupling_ref, head_ref, amp_out, amp_ref, parts_ref, by_real_ref, by_imag_ref, curve_ref, sems
 ):
+    place_ref = here()
     for block in range(table_ref.shape[0]):
         half = table_ref[block]
         coupling_ref[block : block + 1, :] = jnp.concatenate([half[1:2, OWN:LANES], half[2:3, OWN:LANES]], axis=1)
@@ -324,7 +333,8 @@
         copy(step).wait()
 
 
-def add_kernel(pieces_ref, base_ref, coupling_ref, place_ref, out_ref, gram_ref):
+def add_kernel(pieces_ref, base_ref, coupling_ref, out_ref, gram_ref):
+    place_ref = here()
     gram = jnp.sum(pieces_ref[...].astype(jnp.float32), axis=0)
     gram_ref[...] = gram
     send_terms(base_ref[...] + gram_rows(gram, *signs(coupling_ref[...]), place_ref), out_ref)
@@ -339,9 +349,10 @@
 
 
 def next_pass(
-    scale, received_ref, old_ref, head_ref, tail_ref, arrive, weight_ref, place_ref, gram_ref, out_ref, coupling_ref,
+    scale, received_ref, old_ref, head_ref, tail_ref, arrive, weight_ref, gram_ref, out_ref, coupling_ref,
     parts_ref, by_real_ref, by_imag_ref, curve_ref, column_ref
 ):
+    place_ref = here()
     coupling = new_coupling(received_ref, old_ref)
     coupling_ref[...] = coupling
     signed, swapped = load_coupling(coupling, parts_ref)
@@ -374,17 +385,26 @@
 
 
 def second_kernel(
-    scale, received_ref, old_ref, head_ref, tail_in, weight_ref, place_ref, gram_ref, out_ref, coupling_ref, tail_ref, *scratch
+    scale, received_ref, old_ref, head_ref, tail_in, weight_ref, gram_ref, out_ref, coupling_ref, tail_ref, *scratch
 ):
     sems = scratch[-1]
 
     def copy(step):
         return pltpu.make_async_copy(tail_in.at[:, tile_at(step)], tail_ref.at[:, tile_at(step)], sems.at[step])
 
-    for step in range(tail_ref.shape[1] // TILE):
+    tiles = tail_ref.shape[1] // TILE
+
+    def arrive(step):
+        copy(step).wait()
+
+        @pl.when(step + AHEAD < tiles)
+        def _():
+            copy(step + AHEAD).start()
+
+    for step in range(AHEAD):
         copy(step).start()
     next_pass(
-        scale, received_ref, old_ref, head_ref, tail_ref, lambda step: copy(step).wait(), weight_ref, place_ref, gram_ref,
+        scale, received_ref, old_ref, head_ref, tail_ref, arrive, weight_ref, gram_ref,
         out_ref, coupling_ref, *scratch[:-1]
     )
 
@@ -394,8 +414,9 @@
 
 
 def last_kernel(
-    received_ref, old_ref, head_ref, tail_ref, place_ref, coupling_out_ref, intensity_ref, parts_ref, coupling_ref, column_ref
-):
+    received_ref, old_ref, head_ref, tail_ref, coupling_out_ref, intensity_ref, parts_ref, coupling_ref, column_ref
+):
+    place_ref = here()
     coupling = new_coupling(received_ref, old_ref)
     coupling_ref[...] = coupling
     signed, swapped = load_coupling(coupling, parts_ref)
@@ -416,9 +437,9 @@
         finish(tail_ref, step, step + HEAD)
 
 
-def call(kernel, outs, scratch, *args, smem, hbm=(), hbm_out=(), cost=None):
+def call(kernel, outs, scratch, *args, hbm=(), hbm_out=(), cost=None):
     def space(place):
-        return pltpu.SMEM if place in smem else pltpu.HBM if place in hbm else pltpu.VMEM
+        return pltpu.HBM if place in hbm else pltpu.VMEM
 
     single = not isinstance(outs, tuple)
     whole = pl.BlockSpec(memory_space=pltpu.VMEM)
@@ -452,7 +473,6 @@
     events = zx * lax.axis_size("core")
     levels = mc_basis.shape[0]
     mc_count, data_count = mc_mass.shape[0], data_mass.shape[0]
-    places = jnp.stack([lax.axis_index("wrow"), lax.axis_index(EVENT)]).astype(jnp.int32)
     own_table, mc_mass, mc_basis = call(
         prepare_kernel,
         (shape(rows, 4, LANES), shape(1, mc_count), shape(levels, mc_count, dtype=jnp.bfloat16)),
@@ -465,8 +485,7 @@
             pltpu.SemaphoreType.DMA((5,)),
             pltpu.SemaphoreType.DMA((2,)),
         ],
-        res_mass[None], res_width[None], res_wave[None], wave_q[None], couplings, mc_mass[None], mc_basis, places,
-        smem=(7,),
+        res_mass[None], res_width[None], res_wave[None], wave_q[None], couplings, mc_mass[None], mc_basis,
         hbm=range(7),
     )
     table = lax.all_to_all(own_table, "wrow", 0, 0)
@@ -486,8 +505,7 @@
             pltpu.VMEM((OWN, rows, LANES), jnp.float32),
             pltpu.SemaphoreType.DMA((3,)),
         ],
-        table, mc_mass, mc_basis, data_mass[None], data_basis, data_weight[None], places,
-        smem=(6,),
+        table, mc_mass, mc_basis, data_mass[None], data_basis, data_weight[None],
         hbm=range(3, 6),
     )
     pieces = lax.all_to_all(tile, EVENT, 0, 0)
@@ -503,19 +521,18 @@
             pltpu.HBM(tail_shape, jnp.bfloat16),
         ),
         [pltpu.VMEM(tail_shape, jnp.bfloat16)] + pass_scratch(waves) + [tile_sems],
-        table, wide, chooser, data_mass, data_basis, weight, places,
-        smem=(6,),
+        table, wide, chooser, data_mass, data_basis, weight,
         hbm_out=(3,),
         cost=pl.CostEstimate(
             flops=40 * waves * data_count, bytes_accessed=8 * waves * data_count, transcendentals=waves * data_count
         ),
     )
     terms, gram_row = call(
-        add_kernel, (shape(zx, 2, LANES), shape(rows, LANES)), [], pieces, base, coupling, places, smem=(3,)
+        add_kernel, (shape(zx, 2, LANES), shape(rows, LANES)), [], pieces, base, coupling
     )
 
     def exchange(values):
-        merged = call(merge_kernel, shape(2 * rows, 2, LANES), [], lax.all_to_all(values, ZX, 0, 0), smem=())
+        merged = call(merge_kernel, shape(2 * rows, 2, LANES), [], lax.all_to_all(values, ZX, 0, 0))
         return lax.all_to_all(merged, PEERS, 0, 0)
 
     column_scratch = [pltpu.VMEM((2, NEXT_ROWS, LANES), jnp.float32)]
@@ -526,18 +543,16 @@
                 functools.partial(second_kernel, inverse_count),
                 (shape(zx, 2, LANES), shape(rows, LANES), shape(*tail_shape, dtype=jnp.bfloat16)),
                 pass_scratch(waves) + column_scratch + [tile_sems],
-                received, coupling, head, tail, weight, places, gram_row,
-                smem=(5,),
-                hbm=(3,),
+                received, coupling, head, tail, weight,  gram_row,
+                        hbm=(3,),
             )
         else:
             terms, coupling = call(
                 functools.partial(next_kernel, inverse_count),
                 (shape(zx, 2, LANES), shape(rows, LANES)),
                 pass_scratch(waves) + column_scratch,
-                received, coupling, head, tail, weight, places, gram_row,
-                smem=(5,),
-            )
+                received, coupling, head, tail, weight,  gram_row,
+                    )
     received = exchange(terms)
     coupling_out, intensity = call(
         last_kernel,
@@ -547,8 +562,7 @@
             pltpu.VMEM((rows, LANES), jnp.float32),
             pltpu.VMEM((2, LAST_ROWS, LANES), jnp.float32),
         ],
-        received, coupling, head, tail, places,
-        smem=(4,),
+        received, coupling, head, tail,
     )
     return coupling_out, intensity.reshape(data_count)
 

time: 135 us -> 132 us (0.978)
  Pallas kernels: 29.8 us -> 26.9 us
    pallas_call x10, Pallas kernels: 29.8 us -> 26.9 us  [call(): pl.pallas_call(kernel, out_shape=outs, in_specs=[pl.BlockSpec(memory_spac...]
where the time goes in v7:
time: 132 us
  blocking collectives  85.3 us (65%)
  Pallas kernels  26.9 us (20%)
  starting transfers between devices  15.4 us (12%)
  waiting for transfers between devices  3.58 us (3%)
    all_to_all x3, blocking collectives, exchange(): lax.all_to_all(values, ZX, 0, 0)  37.6 us
    all_to_all x3, blocking collectives, exchange(): return lax.all_to_all(merged, PEERS, 0, 0)  33.7 us
    pallas_call x10, Pallas kernels, call(): pl.pallas_call(kernel, out_shape=outs, in_specs=[pl.BlockSpec(memory_spac...  26.9 us
    all_to_all x1, starting transfers between devices, shards(): pieces = lax.all_to_all(tile, EVENT, 0, 0)  15.4 us
    all_to_all x1, blocking collectives, shards(): table = lax.all_to_all(own_table, 'wrow', 0, 0)  14.1 us
    all_to_all x1, waiting for transfers between devices, shards(): pieces = lax.all_to_all(tile, EVENT, 0, 0)  3.58 us
  transfers between devices with their start and end apart: 1, of which 1 were waited for; matrix products, arithmetic and copies ran while one was open for 0% of the time, Pallas kernels for 6%

profile of v7, /device:TPU:1, one launch (start us, length us, event | category | flops | bytes accessed | tf_op | source)
XLA Modules:
  0.0 131.9 jit_solution(18197402265291307497)
XLA Ops:
  0.6 1.2 shard_map.113
  1.8 14.1 %all_to_all.40.table_ref = f32[8,4,128]{2,1,0:T(4,128)S(1)} all-to-all(f32[8,4,128]{2,1,0:T(4,128)S(1)} %get-tuple-element.24), channel_id=1, replica_groups=mesh['z'=4,'x'=8,'core'=2,'wrow'=8] {'wrow'}, dimensions={0} | all-to-all | bytes 32768 | tf_op jit(solution)/shard_map/all_to_all | solution.py:491
  15.9 8.3 %shard_map.114 = (bf16[64,8,128]{2,1,0:T(8,128)(2,1)}, f32[4,512,128]{2,1,0:T(8,128)S(1)}, bf16[512,64]{1,0:T(8,128)(2,1)S(1)}, f32[1,4096]{1,0:T(1,128)S(1)}, b...) custom-call(f32[8,4,128]{2,1,0:T(4,128)S(1)} %all_to_all.40.table_ref, f32[1,3072]{1,0:T(1,128)S(1)} %get-tuple-element.25.mass_ref, ...), custom_call_target="tpu_custom_call" | custom-call | tf_op jit(solution)/shard_map/pallas_call | solution.py:446
  24.2 15.4 %all-to-all-start.1 = ((bf16[64,8,128]{2,1,0:T(8,128)(2,1)}), bf16[64,8,128]{2,1,0:T(8,128)(2,1)S(1)}, u32[]{:S(2)}, u32[]{:S(2)}) async-start(bf16[64,8,128]{2,1,0:T(8,128)(2,1)} %get-tuple-element.27), calls=%async_computation.1 | async-start | bytes 262144 | tf_op jit(solution)/shard_map/all_to_all | solution.py:511
  39.6 7.5 %shard_map.115 = (f32[2,128]{1,0:T(2,128)S(1)}, f32[8,128]{1,0:T(8,128)S(1)}, bf16[1024,512]{1,0:T(8,128)(2,1)S(1)}, bf16[1024,3584]{1,0:T(8,128)(2,1)}) custom-call(f32[8,4,128]{2,1,0:T(4,128)S(1)} %all_to_all.40.table_ref, f32[4,512,128]{2,1,0:T(8,128)S(1)} %get-tuple-element.28.wide_ref, bf16[512,64]{1,0:T(8,128)(2,1)S(1)} %get-tuple-element.29.chooser_ref, ...), custom_call_target="tpu_custom_call" | custom-call | flops 83886080 | bytes 16777216 | tf_op jit(solution)/shard_map/pallas_call | solution.py:446
  47.1 3.6 %all-to-all-done.1.pieces_ref = bf16[64,8,128]{2,1,0:T(8,128)(2,1)S(1)} async-done(((bf16[64,8,128]{2,1,0:T(8,128)(2,1)}), bf16[64,8,128]{2,1,0:T(8,128)(2,1)S(1)}, u32[]{:S(2)}, u32[]{:S(2)}) %all-to-all-start.1) | async-done | bytes 131104 | tf_op jit(solution)/shard_map/all_to_all | solution.py:511
  50.7 0.2 shard_map.116
  50.9 14.4 %all_to_all.41.received_ref = f32[32,2,128]{2,1,0:T(2,128)S(1)} all-to-all(f32[32,2,128]{2,1,0:T(2,128)S(1)} %get-tuple-element.35), channel_id=1, replica_groups=mesh['z'=4,'x'=8,'core'=2,'wrow'=8] {'z','x'}, dimensions={0} | all-to-all | bytes 65536 | tf_op jit(solution)/shard_map/all_to_all | solution.py:535
  65.3 11.2 %all_to_all.42.received_ref = f32[16,2,128]{2,1,0:T(2,128)S(1)} all-to-all(f32[16,2,128]{2,1,0:T(2,128)S(1)} %shard_map.117), channel_id=1, replica_groups=mesh['z'=4,'x'=8,'core'=2,'wrow'=8] {'core','wrow'}, dimensions={0} | all-to-all | bytes 32768 | tf_op jit(solution)/shard_map/all_to_all | solution.py:536
  76.5 4.5 %shard_map.118 = (f32[32,2,128]{2,1,0:T(2,128)S(1)}, f32[8,128]{1,0:T(8,128)S(1)}, bf16[1024,3584]{1,0:T(8,128)(2,1)S(1)}) custom-call(f32[16,2,128]{2,1,0:T(2,128)S(1)} %all_to_all.42.received_ref, f32[8,128]{1,0:T(8,128)S(1)} %get-tuple-element.34.coupling_ref.old_ref, bf16[1024,512]{1,0:T(8,128)(2,1)S(1)} %get-tuple-element.36.head_ref, ...), custom_call_target="tpu_custom_call" | custom-call | tf_op jit(solution)/shard_map/pallas_call | solution.py:446
  81.0 11.6 %all_to_all.43.received_ref = f32[32,2,128]{2,1,0:T(2,128)S(1)} all-to-all(f32[32,2,128]{2,1,0:T(2,128)S(1)} %get-tuple-element.39), channel_id=1, replica_groups=mesh['z'=4,'x'=8,'core'=2,'wrow'=8] {'z','x'}, dimensions={0} | all-to-all | bytes 65536 | tf_op jit(solution)/shard_map/all_to_all | solution.py:535
  92.6 11.3 %all_to_all.44.received_ref = f32[16,2,128]{2,1,0:T(2,128)S(1)} all-to-all(f32[16,2,128]{2,1,0:T(2,128)S(1)} %shard_map.119), channel_id=1, replica_groups=mesh['z'=4,'x'=8,'core'=2,'wrow'=8] {'core','wrow'}, dimensions={0} | all-to-all | bytes 32768 | tf_op jit(solution)/shard_map/all_to_all | solution.py:536
  103.9 2.4 %shard_map.120 = (f32[32,2,128]{2,1,0:T(2,128)S(1)}, f32[8,128]{1,0:T(8,128)S(1)}) custom-call(f32[16,2,128]{2,1,0:T(2,128)S(1)} %all_to_all.44.received_ref, f32[8,128]{1,0:T(8,128)S(1)} %get-tuple-element.40.old_ref, bf16[1024,512]{1,0:T(8,128)(2,1)S(1)} %get-tuple-element.36.head_ref, bf16[1024,3584]{1,0:T(8,128)(2,1)S(1)} %get-tuple-element.41.tail_ref, ...), custom_call_target="tpu_custom_call" | custom-call | tf_op jit(solution)/shard_map/pallas_call | solution.py:446
  106.3 11.6 %all_to_all.45.received_ref = f32[32,2,128]{2,1,0:T(2,128)S(1)} all-to-all(f32[32,2,128]{2,1,0:T(2,128)S(1)} %get-tuple-element.42), channel_id=1, replica_groups=mesh['z'=4,'x'=8,'core'=2,'wrow'=8] {'z','x'}, dimensions={0} | all-to-all | bytes 65536 | tf_op jit(solution)/shard_map/all_to_all | solution.py:535
  117.9 11.3 %all_to_all.46.received_ref = f32[16,2,128]{2,1,0:T(2,128)S(1)} all-to-all(f32[16,2,128]{2,1,0:T(2,128)S(1)} %shard_map.121), channel_id=1, replica_groups=mesh['z'=4,'x'=8,'core'=2,'wrow'=8] {'core','wrow'}, dimensions={0} | all-to-all | bytes 32768 | tf_op jit(solution)/shard_map/all_to_all | solution.py:536
  129.2 2.7 %shard_map.122 = (f32[2,64]{1,0:T(2,128)}, f32[1,4096]{1,0:T(1,128)}) custom-call(f32[16,2,128]{2,1,0:T(2,128)S(1)} %all_to_all.46.received_ref, f32[8,128]{1,0:T(8,128)S(1)} %get-tuple-element.43.old_ref, bf16[1024,512]{1,0:T(8,128)(2,1)S(1)} %get-tuple-element.36.head_ref, bf16[1024,3584]{1,0:T(8,128)(2,1)S(1)} %get-tuple-element.41.tail_ref), custom_call_target="tpu_custom_call" | custom-call | tf_op jit(solution)/shard_map/pallas_call | solution.py:446
  (3 shorter events, 0.1 us)
Async XLA Ops:
  24.2 26.5 %all-to-all-start.1 = ((bf16[64,8,128]{2,1,0:T(8,128)(2,1)}), bf16[64,8,128]{2,1,0:T(8,128)(2,1)S(1)}, u32[]{:S(2)}, u32[]{:S(2)}) async-start(bf16[64,8,128]{2,1,0:T(8,128)(2,1)} %get-tuple-element.27), calls=%async_computation.1 | async-start | bytes 262144 | tf_op jit(solution)/shard_map/all_to_all | solution.py:511

commit v8 on v7

--- a/solution.py
+++ b/solution.py
@@ -21,7 +21,6 @@
 NEXT_ROWS = 256
 LAST_ROWS = 256
 HEAD = 1
-AHEAD = 3
 VMEM_LIMIT = 24 << 20
 
 
@@ -191,11 +190,11 @@
             column_ref[place, block * LANES : (block + 1) * LANES, :] = jnp.broadcast_to(column, (LANES, LANES))
 
 
-def field_of(parts, amp_ref, columns, column_ref=None):
+def field_of(parts, amp_ref, column_ref=None):
     waves = amp_ref.shape[0]
     vector_rows = 0 if column_ref is None else column_ref.shape[1]
     matrix_rows = waves - vector_rows
-    sums = jnp.dot(parts[:, :matrix_rows], amp_ref[:matrix_rows, columns], preferred_element_type=jnp.float32)
+    sums = jnp.dot(parts[:, :matrix_rows], amp_ref[:matrix_rows, :], preferred_element_type=jnp.float32)
     real = (sums[4:5] + sums[2:3]) + sums[0:1]
     imag = (sums[5:6] + sums[3:4]) + sums[1:2]
     if vector_rows:
@@ -204,7 +203,7 @@
         imags = [jnp.zeros((ROWS, LANES), jnp.float32) for _ in range(lanes)]
         for start in range(0, vector_rows, ROWS):
             rows = slice(start, start + ROWS)
-            values = amp_ref[matrix_rows + start : matrix_rows + start + ROWS, columns].astype(jnp.float32)
+            values = amp_ref[matrix_rows + start : matrix_rows + start + ROWS, :].astype(jnp.float32)
             by_real, by_imag = column_ref[0, rows, :], column_ref[1, rows, :]
             for place in range(lanes):
                 value = values[:, place * LANES : (place + 1) * LANES]
@@ -305,29 +304,29 @@
     load_coupling(coupling_ref[...], parts_ref)
     parts = parts_ref[...].astype(jnp.bfloat16)
     clear(by_real_ref, by_imag_ref, curve_ref)
-    tail = amp_ref.shape[1] // TILE
-
-    def compute(event_tile, target_ref, target_tile):
-        events, columns = tile_at(event_tile), tile_at(target_tile)
+    tail = amp_ref.shape[0]
+
+    def compute(event_tile, target_ref):
+        events = tile_at(event_tile)
 
         def store(row, real, imag):
-            target_ref[row : row + ROWS, columns] = real
-            target_ref[row + OWN : row + OWN + ROWS, columns] = imag
+            target_ref[row : row + ROWS, :] = real
+            target_ref[row + OWN : row + OWN + ROWS, :] = imag
 
         fill_tile(mass_ref[:, events], basis_ref[:, events], wide_ref, chooser_ref, store)
-        real, imag = field_of(parts, target_ref, columns)
-        own = target_ref[own_rows(place_ref), columns]
+        real, imag = field_of(parts, target_ref)
+        own = target_ref[own_rows(place_ref), :]
         project_tile(real, imag, weight_ref[:, events], own, by_real_ref, by_imag_ref, curve_ref)
 
     def copy(step):
-        return pltpu.make_async_copy(amp_ref.at[:, tile_at(step)], amp_out.at[:, tile_at(step)], sems.at[step])
+        return pltpu.make_async_copy(amp_ref.at[step], amp_out.at[step], sems.at[step])
 
     @pl.loop(0, tail)
     def _(step):
-        compute(step + HEAD, amp_ref, step)
+        compute(step + HEAD, amp_ref.at[step])
         copy(step).start()
 
-    compute(0, head_ref, 0)
+    compute(0, head_ref)
     out_ref[...] = gradient_rows(scale, by_real_ref, by_imag_ref, curve_ref)
     for step in range(tail):
         copy(step).wait()
@@ -359,27 +358,27 @@
     load_columns(signed, swapped, column_ref.shape[1], column_ref)
     parts = parts_ref[...].astype(jnp.bfloat16)
     clear(by_real_ref, by_imag_ref, curve_ref)
-    tiles = tail_ref.shape[1] // TILE
-
-    def field_at(source_ref, step):
-        return field_of(parts, source_ref, tile_at(step), column_ref)
-
-    def project(source_ref, step, event_tile, field):
-        own = source_ref[own_rows(place_ref), tile_at(step)]
+    tiles = tail_ref.shape[0]
+
+    def field_at(source_ref):
+        return field_of(parts, source_ref, column_ref)
+
+    def project(source_ref, event_tile, field):
+        own = source_ref[own_rows(place_ref), :]
         project_tile(*field, weight_ref[:, tile_at(event_tile)], own, by_real_ref, by_imag_ref, curve_ref)
 
     def ahead(step, field):
         arrive(step + 1)
-        later = field_at(tail_ref, step + 1)
-        project(tail_ref, step, step + HEAD, field)
+        later = field_at(tail_ref.at[step + 1])
+        project(tail_ref.at[step], step + HEAD, field)
         return later
 
-    field = field_at(head_ref, 0)
+    field = field_at(head_ref)
     arrive(0)
-    later = field_at(tail_ref, 0)
-    project(head_ref, 0, 0, field)
+    later = field_at(tail_ref.at[0])
+    project(head_ref, 0, field)
     field = lax.fori_loop(0, tiles - 1, ahead, later)
-    project(tail_ref, tiles - 1, tiles - 1 + HEAD, field)
+    project(tail_ref.at[tiles - 1], tiles - 1 + HEAD, field)
     terms = gradient_rows(scale, by_real_ref, by_imag_ref, curve_ref)
     send_terms(terms + gram_rows(gram_ref[...], signed, swapped, place_ref), out_ref)
 
@@ -390,21 +389,12 @@
     sems = scratch[-1]
 
     def copy(step):
-        return pltpu.make_async_copy(tail_in.at[:, tile_at(step)], tail_ref.at[:, tile_at(step)], sems.at[step])
-
-    tiles = tail_ref.shape[1] // TILE
-
-    def arrive(step):
-        copy(step).wait()
-
-        @pl.when(step + AHEAD < tiles)
-        def _():
-            copy(step + AHEAD).start()
-
-    for step in range(AHEAD):
+        return pltpu.make_async_copy(tail_in.at[step], tail_ref.at[step], sems.at[step])
+
+    for step in range(tail_ref.shape[0]):
         copy(step).start()
     next_pass(
-        scale, received_ref, old_ref, head_ref, tail_ref, arrive, weight_ref, gram_ref,
+        scale, received_ref, old_ref, head_ref, tail_ref, lambda step: copy(step).wait(), weight_ref, gram_ref,
         out_ref, coupling_ref, *scratch[:-1]
     )
 
@@ -426,15 +416,15 @@
     coupling_out_ref[0:1, :] = mine[:, 0:OWN]
     coupling_out_ref[1:2, :] = pltpu.roll(mine, OWN, 1)[:, 0:OWN]
 
-    def finish(source_ref, step, event_tile):
-        real, imag = field_of(parts, source_ref, tile_at(step), column_ref)
+    def finish(source_ref, event_tile):
+        real, imag = field_of(parts, source_ref, column_ref)
         intensity_ref[:, tile_at(event_tile)] = real * real + imag * imag + BACKGROUND
 
-    finish(head_ref, 0, 0)
-
-    @pl.loop(0, tail_ref.shape[1] // TILE)
+    finish(head_ref, 0)
+
+    @pl.loop(0, tail_ref.shape[0])
     def _(step):
-        finish(tail_ref, step, step + HEAD)
+        finish(tail_ref.at[step], step + HEAD)
 
 
 def call(kernel, outs, scratch, *args, hbm=(), hbm_out=(), cost=None):
@@ -511,7 +501,7 @@
     pieces = lax.all_to_all(tile, EVENT, 0, 0)
     inverse_count = 1.0 / (data_count * events)
     tile_sems = pltpu.SemaphoreType.DMA((data_count // TILE,))
-    tail_shape = (2 * waves, data_count - HEAD * TILE)
+    tail_shape = (data_count // TILE - HEAD, 2 * waves, TILE)
     base, coupling, head, tail = call(
         functools.partial(first_kernel, inverse_count),
         (

time: 132 us -> 132 us (level)
  no operation moved by 1% of the time
where the time goes in v8:
time: 132 us; the launch traced here: 131 us
  blocking collectives  85.4 us (65%)
  Pallas kernels  26 us (20%)
  starting transfers between devices  15.4 us (12%)
  waiting for transfers between devices  3.59 us (3%)
    all_to_all x3, blocking collectives, exchange(): lax.all_to_all(values, ZX, 0, 0)  37.6 us
    all_to_all x3, blocking collectives, exchange(): return lax.all_to_all(merged, PEERS, 0, 0)  33.7 us
    pallas_call x10, Pallas kernels, call(): pl.pallas_call(kernel, out_shape=outs, in_specs=[pl.BlockSpec(memory_spac...  26 us
    all_to_all x1, starting transfers between devices, shards(): pieces = lax.all_to_all(tile, EVENT, 0, 0)  15.4 us
    all_to_all x1, blocking collectives, shards(): table = lax.all_to_all(own_table, 'wrow', 0, 0)  14.1 us
    all_to_all x1, waiting for transfers between devices, shards(): pieces = lax.all_to_all(tile, EVENT, 0, 0)  3.59 us
  transfers between devices with their start and end apart: 1, of which 1 were waited for; matrix products, arithmetic and copies ran while one was open for 0% of the time, Pallas kernels for 6%

profile of v8, /device:TPU:1, one launch (start us, length us, event | category | flops | bytes accessed | tf_op | source)
XLA Modules:
  0.0 131.1 jit_solution(7354384622868159206)
XLA Ops:
  0.6 1.2 shard_map.113
  1.8 14.1 %all_to_all.40.table_ref = f32[8,4,128]{2,1,0:T(4,128)S(1)} all-to-all(f32[8,4,128]{2,1,0:T(4,128)S(1)} %get-tuple-element.24), channel_id=1, replica_groups=mesh['z'=4,'x'=8,'core'=2,'wrow'=8] {'wrow'}, dimensions={0} | all-to-all | bytes 32768 | tf_op jit(solution)/shard_map/all_to_all | solution.py:481
  15.9 8.3 %shard_map.114 = (bf16[64,8,128]{2,1,0:T(8,128)(2,1)}, f32[4,512,128]{2,1,0:T(8,128)S(1)}, bf16[512,64]{1,0:T(8,128)(2,1)S(1)}, f32[1,4096]{1,0:T(1,128)S(1)}, b...) custom-call(f32[8,4,128]{2,1,0:T(4,128)S(1)} %all_to_all.40.table_ref, f32[1,3072]{1,0:T(1,128)S(1)} %get-tuple-element.25.mass_ref, ...), custom_call_target="tpu_custom_call" | custom-call | tf_op jit(solution)/shard_map/pallas_call | solution.py:436
  24.2 15.4 %all-to-all-start.1 = ((bf16[64,8,128]{2,1,0:T(8,128)(2,1)}), bf16[64,8,128]{2,1,0:T(8,128)(2,1)S(1)}, u32[]{:S(2)}, u32[]{:S(2)}) async-start(bf16[64,8,128]{2,1,0:T(8,128)(2,1)} %get-tuple-element.27), calls=%async_computation.1 | async-start | bytes 262144 | tf_op jit(solution)/shard_map/all_to_all | solution.py:501
  39.6 7.5 %shard_map.115 = (f32[2,128]{1,0:T(2,128)S(1)}, f32[8,128]{1,0:T(8,128)S(1)}, bf16[1024,512]{1,0:T(8,128)(2,1)S(1)}, bf16[7,1024,512]{2,1,0:T(8,128)(2,1)}) custom-call(f32[8,4,128]{2,1,0:T(4,128)S(1)} %all_to_all.40.table_ref, f32[4,512,128]{2,1,0:T(8,128)S(1)} %get-tuple-element.28.wide_ref, bf16[512,64]{1,0:T(8,128)(2,1)S(1)} %get-tuple-element.29.chooser_ref, ...), custom_call_target="tpu_custom_call" | custom-call | flops 83886080 | bytes 16777216 | tf_op jit(solution)/shard_map/pallas_call | solution.py:436
  47.1 3.6 %all-to-all-done.1.pieces_ref = bf16[64,8,128]{2,1,0:T(8,128)(2,1)S(1)} async-done(((bf16[64,8,128]{2,1,0:T(8,128)(2,1)}), bf16[64,8,128]{2,1,0:T(8,128)(2,1)S(1)}, u32[]{:S(2)}, u32[]{:S(2)}) %all-to-all-start.1) | async-done | bytes 131104 | tf_op jit(solution)/shard_map/all_to_all | solution.py:501
  50.7 0.2 shard_map.116
  50.9 14.4 %all_to_all.41.received_ref = f32[32,2,128]{2,1,0:T(2,128)S(1)} all-to-all(f32[32,2,128]{2,1,0:T(2,128)S(1)} %get-tuple-element.35), channel_id=1, replica_groups=mesh['z'=4,'x'=8,'core'=2,'wrow'=8] {'z','x'}, dimensions={0} | all-to-all | bytes 65536 | tf_op jit(solution)/shard_map/all_to_all | solution.py:525
  65.3 11.2 %all_to_all.42.received_ref = f32[16,2,128]{2,1,0:T(2,128)S(1)} all-to-all(f32[16,2,128]{2,1,0:T(2,128)S(1)} %shard_map.117), channel_id=1, replica_groups=mesh['z'=4,'x'=8,'core'=2,'wrow'=8] {'core','wrow'}, dimensions={0} | all-to-all | bytes 32768 | tf_op jit(solution)/shard_map/all_to_all | solution.py:526
  76.5 3.7 %shard_map.118 = (f32[32,2,128]{2,1,0:T(2,128)S(1)}, f32[8,128]{1,0:T(8,128)S(1)}, bf16[7,1024,512]{2,1,0:T(8,128)(2,1)S(1)}) custom-call(f32[16,2,128]{2,1,0:T(2,128)S(1)} %all_to_all.42.received_ref, f32[8,128]{1,0:T(8,128)S(1)} %get-tuple-element.34.coupling_ref.old_ref, bf16[1024,512]{1,0:T(8,128)(2,1)S(1)} %get-tuple-element.36.head_ref, ...), custom_call_target="tpu_custom_call" | custom-call | tf_op jit(solution)/shard_map/pallas_call | solution.py:436
  80.2 11.6 %all_to_all.43.received_ref = f32[32,2,128]{2,1,0:T(2,128)S(1)} all-to-all(f32[32,2,128]{2,1,0:T(2,128)S(1)} %get-tuple-element.39), channel_id=1, replica_groups=mesh['z'=4,'x'=8,'core'=2,'wrow'=8] {'z','x'}, dimensions={0} | all-to-all | bytes 65536 | tf_op jit(solution)/shard_map/all_to_all | solution.py:525
  91.8 11.3 %all_to_all.44.received_ref = f32[16,2,128]{2,1,0:T(2,128)S(1)} all-to-all(f32[16,2,128]{2,1,0:T(2,128)S(1)} %shard_map.119), channel_id=1, replica_groups=mesh['z'=4,'x'=8,'core'=2,'wrow'=8] {'core','wrow'}, dimensions={0} | all-to-all | bytes 32768 | tf_op jit(solution)/shard_map/all_to_all | solution.py:526
  103.1 2.4 %shard_map.120 = (f32[32,2,128]{2,1,0:T(2,128)S(1)}, f32[8,128]{1,0:T(8,128)S(1)}) custom-call(f32[16,2,128]{2,1,0:T(2,128)S(1)} %all_to_all.44.received_ref, f32[8,128]{1,0:T(8,128)S(1)} %get-tuple-element.40.old_ref, bf16[1024,512]{1,0:T(8,128)(2,1)S(1)} %get-tuple-element.36.head_ref, bf16[7,1024,512]{2,1,0:T(8,128)(2,1)S(1)} %get-tuple-element.41.tail_ref, ...), custom_call_target="tpu_custom_call" | custom-call | tf_op jit(solution)/shard_map/pallas_call | solution.py:436
  105.5 11.6 %all_to_all.45.received_ref = f32[32,2,128]{2,1,0:T(2,128)S(1)} all-to-all(f32[32,2,128]{2,1,0:T(2,128)S(1)} %get-tuple-element.42), channel_id=1, replica_groups=mesh['z'=4,'x'=8,'core'=2,'wrow'=8] {'z','x'}, dimensions={0} | all-to-all | bytes 65536 | tf_op jit(solution)/shard_map/all_to_all | solution.py:525
  117.1 11.3 %all_to_all.46.received_ref = f32[16,2,128]{2,1,0:T(2,128)S(1)} all-to-all(f32[16,2,128]{2,1,0:T(2,128)S(1)} %shard_map.121), channel_id=1, replica_groups=mesh['z'=4,'x'=8,'core'=2,'wrow'=8] {'core','wrow'}, dimensions={0} | all-to-all | bytes 32768 | tf_op jit(solution)/shard_map/all_to_all | solution.py:526
  128.4 2.7 %shard_map.122 = (f32[2,64]{1,0:T(2,128)}, f32[1,4096]{1,0:T(1,128)}) custom-call(f32[16,2,128]{2,1,0:T(2,128)S(1)} %all_to_all.46.received_ref, f32[8,128]{1,0:T(8,128)S(1)} %get-tuple-element.43.old_ref, bf16[1024,512]{1,0:T(8,128)(2,1)S(1)} %get-tuple-element.36.head_ref, bf16[7,1024,512]{2,1,0:T(8,128)(2,1)S(1)} %get-tuple-element.41.tail_ref), custom_call_target="tpu_custom_call" | custom-call | tf_op jit(solution)/shard_map/pallas_call | solution.py:436
  (3 shorter events, 0.1 us)
Async XLA Ops:
  24.2 26.5 %all-to-all-start.1 = ((bf16[64,8,128]{2,1,0:T(8,128)(2,1)}), bf16[64,8,128]{2,1,0:T(8,128)(2,1)S(1)}, u32[]{:S(2)}, u32[]{:S(2)}) async-start(bf16[64,8,128]{2,1,0:T(8,128)(2,1)} %get-tuple-element.27), calls=%async_computation.1 | async-start | bytes 262144 | tf_op jit(solution)/shard_map/all_to_all | solution.py:501
